TPU v7x, 32 devices: a whole 2x2x4 slice. The times are simulated.
32 devices in a mesh: groups: 2 (over y), vocab: 4 (over z), rows: 2 (over x), teach: 2 (over core).
Axes of the slice: x: 2, y: 2, z: 4, core: 2. Of those that a mesh axis runs over, the one named last changes fastest.
Arguments:
- hidden_rows: bfloat16 [32, 3584], P(('groups', 'vocab')), parts along dimension 0, may hold values from -512 to 512
- mentor_unnormalized: float32 [32, 4864], P(('groups', 'teach'), ('vocab', 'rows')), parts along dimension 0, may hold values from -1000 to 1000
- head_weight: bfloat16 [4864, 3584], P(('vocab', 'rows', 'teach')), may hold values from -2 to 2
- row_mask: int32 [32], P('groups'), parts along dimension 0, may hold values 0 or 1
Outputs:
- divergence: float32 [32], P('groups'), parts along dimension 0
- hidden_grad: bfloat16 [32, 3584], P(('groups', 'vocab', 'rows', 'teach')), parts along dimension 0
- weight_grad: bfloat16 [9728, 3584], P(('groups', 'vocab', 'rows', 'teach')), parts along dimension 0
There are 2 independent parts, one for each index of `groups`. A program takes and returns all parts, laid end to end along the dimension named above; an argument that names none is the same for every part. Nothing has to cross between parts.
All inputs are finite; a program needn't handle non-finite values.
Results may differ from a plain program's by a relative error of at most 0.0051.
Values may be sent and summed in bfloat16 or wider, within the bound.
No kernel may reach another device: no remote copies, remote signals or barrier semaphores. Data moves between devices by JAX's collectives and lax.ppermute only.
A program may use at most 64 MiB of HBM per device.

v0:
```python
import jax
import jax.numpy as jnp
from jax import lax
from jax.sharding import PartitionSpec as P

smoothing_divisor = 2.0
objective_scale = 256.0


def body(hidden_rows, mentor_unnormalized, head_weight, row_mask):
    mentor_divided = lax.all_to_all(
        mentor_unnormalized, "teach", split_axis=1, concat_axis=0, tiled=True
    )
    gathered = lax.all_gather(hidden_rows, "vocab", axis=0, tiled=True)
    head_product_matrix = lax.dot_general(
        gathered, head_weight, (((1,), (1,)), ((), ())), preferred_element_type=jnp.float32
    )
    learner_unnormalized = head_product_matrix / smoothing_divisor
    divided_learner_values = mentor_divided / smoothing_divisor
    max_student, max_teacher = lax.pmax(
        (jnp.max(learner_unnormalized, axis=1), jnp.max(divided_learner_values, axis=1)),
        ("vocab", "rows", "teach"),
    )
    weights_t = jnp.exp(divided_learner_values - max_teacher[:, None])
    sum_student, sum_teacher, cross_term = lax.psum(
        (
            jnp.sum(jnp.exp(learner_unnormalized - max_student[:, None]), axis=1),
            jnp.sum(weights_t, axis=1),
            jnp.sum(weights_t * (divided_learner_values - learner_unnormalized), axis=1),
        ),
        ("vocab", "rows", "teach"),
    )
    lse_student = max_student + jnp.log(sum_student)
    lse_teacher = max_teacher + jnp.log(sum_teacher)
    valid_token_count = row_mask.astype(jnp.float32)
    divergence = valid_token_count * (cross_term / sum_teacher - lse_teacher + lse_student)
    mentor_softmax = jnp.exp(divided_learner_values - lse_teacher[:, None])
    learner_softmax = jnp.exp(learner_unnormalized - lse_student[:, None])
    raw_score_derivative = (
        valid_token_count[:, None]
        * (objective_scale * smoothing_divisor)
        * (learner_softmax - mentor_softmax)
    ).astype(jnp.bfloat16)
    weight_grad = lax.dot_general(
        raw_score_derivative, gathered, (((0,), (0,)), ((), ())), preferred_element_type=jnp.float32
    )
    hidden_grad = lax.psum_scatter(
        jnp.dot(raw_score_derivative, head_weight, preferred_element_type=jnp.float32),
        ("vocab", "rows", "teach"),
        scatter_dimension=0,
        tiled=True,
    )
    return (divergence, hidden_grad.astype(jnp.bfloat16), weight_grad.astype(jnp.bfloat16))


def solution(mesh):
    return jax.shard_map(
        body,
        mesh=mesh,
        in_specs=(
            P(("groups", "vocab"), None),
            P(("groups", "teach"), ("vocab", "rows")),
            P(("vocab", "rows", "teach"), None),
            P("groups"),
        ),
        out_specs=(
            P("groups"),
            P(("groups", "vocab", "rows", "teach"), None),
            P(("groups", "vocab", "rows", "teach"), None),
        ),
        check_vma=False,
    )
```

profile of v0, /device:TPU:0, one launch (start us, length us, event | category | flops | bytes accessed | tf_op | source)
XLA Modules:
  0.0 148.9 jit_solution(4370438108467878461)
XLA Ops:
  0.6 0.0 copy-start
  0.6 1.0 all_to_all.10
  1.6 0.6 copy.8
  2.2 3.2 %all-to-all-start = ((f32[8,2,304]{2,0,1:T(8,128)}), f32[8,2,304]{2,0,1:T(8,128)S(1)}, u32[]{:S(2)}, u32[]{:S(2)}) async-start(f32[8,2,304]{2,0,1:T(8,128)} %copy.8), calls=%async_computation | async-start | bytes 49152 | tf_op jit(solution)/shard_map/all_to_all | solution.py:11
  5.5 0.7 convert_multiply_fusion
  6.1 0.7 all-to-all-done
  6.8 0.1 bitcast_reduce_fusion
  6.9 0.1 reduce_max.21
  7.0 15.3 %all-gather = bf16[4,4,3584]{2,1,0:T(4,128)(2,1)S(1)} all-gather(bf16[1,4,3584]{2,1,0:T(4,128)(2,1)} %bitcast.36), channel_id=1, replica_groups=mesh['groups'=2,'vocab'=4,'rows'=2,'teach'=2] {'vocab'}, dimensions={0}, use_global_device_ids=true | all-gather | bytes 143360 | tf_op jit(solution)/shard_map/all_gather | solution.py:14
  22.3 0.0 copy-done
  22.3 0.8 fusion.9
  23.1 30.6 %all-reduce.3 = (f32[16]{0:T(128)S(1)}, f32[16]{0:T(128)S(1)}) all-reduce(f32[16]{0:T(128)S(1)} %get-tuple-element.11, f32[16]{0:T(128)S(1)} %reduce_max.21), channel_id=1, replica_groups=mesh['groups'=2,'vocab'=4,'rows'=2,'teach'=2] {'vocab','rows','teach'}, use_global_device_ids=true, to_apply=%region_7.0 | all-reduce | flops 32 | bytes 256 | tf_op jit(solution)/shard_map/pmax | solution.py:20
  53.8 0.1 sub.51
  53.8 0.2 fusion.8
  54.0 0.1 reduce_sum.31
  54.1 0.2 fusion.2
  54.3 29.5 %all-reduce.2 = (f32[16]{0:T(128)S(1)}, f32[16]{0:T(128)S(1)}) all-reduce(f32[16]{0:T(128)S(1)} %get-tuple-element.4, f32[16]{0:T(128)S(1)} %reduce_sum.31), channel_id=1, replica_groups=mesh['groups'=2,'vocab'=4,'rows'=2,'teach'=2] {'vocab','rows','teach'}, use_global_device_ids=true, to_apply=%region_9.0 | all-reduce | flops 32 | bytes 256 | tf_op jit(solution)/shard_map/psum | solution.py:25
  83.8 0.1 fusion.6
  83.9 0.0 copy-start.1
  83.9 0.0 copy-start.2
  83.9 0.4 fusion.10
  84.4 2.1 %convolution_convert_fusion = bf16[304,3584]{1,0:T(8,128)(2,1)} fusion(bf16[16,304]{1,0:T(8,128)(2,1)S(1)} %fusion.6, bf16[16,3584]{1,0:T(8,128)(2,1)S(1)} %reshape.24), kind=kOutput, calls=%fused_computation | convolution fusion | flops 35954688 | bytes 2303488 | tf_op jit(solution)/shard_map/dot_general | solution.py:44
  86.5 59.9 %all-reduce.5 = (f32[16]{0:T(128)S(1)}, bf16[16,3584]{1,0:T(8,128)(2,1)S(1)}) all-reduce(f32[16]{0:T(128)S(1)} %get-tuple-element.3, f32[16,3584]{1,0:T(8,128)S(1)} %fusion.10), channel_id=1, replica_groups=mesh['groups'=2,'vocab'=4,'rows'=2,'teach'=2] {'vocab','rows','teach'}, use_global_device_ids=true, to_apply=%region_3.0 | all-reduce | flops 57360 | bytes 344192 | tf_op jit(solution)/shard_map/psum | solution.py:25
  146.4 0.0 copy-done.1
  146.4 0.5 add_multiply_fusion
  146.9 0.0 copy-done.2
  146.9 0.7 dynamic-slice
  147.6 1.3 dynamic-slice_convert_fusion
  (2 shorter events, 0.0 us)
Async XLA Ops:
  0.6 21.7 %copy-start = (bf16[304,3584]{1,0:T(8,128)(2,1)S(1)}, bf16[304,3584]{1,0:T(8,128)(2,1)}, u32[]{:S(2)}) copy-start(bf16[304,3584]{1,0:T(8,128)(2,1)} %param.6) | copy-start | bytes 6537220
  2.2 4.6 %all-to-all-start = ((f32[8,2,304]{2,0,1:T(8,128)}), f32[8,2,304]{2,0,1:T(8,128)S(1)}, u32[]{:S(2)}, u32[]{:S(2)}) async-start(f32[8,2,304]{2,0,1:T(8,128)} %copy.8), calls=%async_computation | async-start | bytes 49152 | tf_op jit(solution)/shard_map/all_to_all | solution.py:11
  83.9 62.5 %copy-start.1 = (s32[16]{0:T(128)S(1)}, s32[16]{0:T(128)}, u32[]{:S(2)}) copy-start(s32[16]{0:T(128)} %param.7) | copy-start | bytes 196
  83.9 63.0 %copy-start.2 = (u32[32]{0:T(128)S(1)}, u32[32]{0:T(128)}, u32[]{:S(2)}) copy-start(u32[32]{0:T(128)} %constant.13) | copy-start | bytes 388
where the time goes:
time: 149 us
  blocking collectives  135 us (91%)
  local copies, waits for them, and re-layouts  3.85 us (3%)
  matrix products  3.34 us (2%)
  starting transfers between devices  3.25 us (2%)
  other arithmetic  1.73 us (1%)
    psum x2, blocking collectives, body(): lax.psum((jnp.sum(jnp.exp(learner_unnormalized - max_student[:, None]), a...  89.4 us
    pmax x1, blocking collectives, body(): lax.pmax((jnp.max(learner_unnormalized, axis=1), jnp.max(divided_learner_...  30.6 us
    all_gather x1, blocking collectives, body(): gathered = lax.all_gather(hidden_rows, 'vocab', axis=0, tiled=True)  15.3 us
    all_to_all x1, starting transfers between devices, body(): lax.all_to_all(mentor_unnormalized, 'teach', split_axis=1, concat_axis=0,...  3.25 us
  transfers between devices with their start and end apart: 1, of which 1 were waited for; matrix products, arithmetic and copies ran while one was open for 0% of the time, Pallas kernels for 0%

commit v1 on v0

v1 whole, which is shorter than its diff:
```python
import jax
import jax.numpy as jnp
from jax import lax
from jax.sharding import PartitionSpec as P

smoothing_divisor = 2.0
objective_scale = 256.0


def flip(n, d):
    return [(i, i ^ d) for i in range(n)]


def bits(n):
    out = []
    d = 1
    while d < n:
        out.append(d)
        d *= 2
    return out


def swap(a, d):
    n = a.shape[0]
    b = a.reshape((n // (2 * d), 2, d) + a.shape[1:])
    return jnp.concatenate([b[:, 1:], b[:, :1]], axis=1).reshape(a.shape)


def relative(a, position, n, stride):
    for d in bits(n):
        a = jnp.where((position & d) != 0, swap(a, d * stride), a)
    return a


def make_body(nz, nx, nc):
    def body(hidden_rows, mentor, head_weight, row_mask):
        z, x, c = lax.axis_index("vocab"), lax.axis_index("rows"), lax.axis_index("teach")
        total = row_mask.shape[0]
        q = total // (nz * nx * nc)
        own = relative(relative(hidden_rows, c, nc, q), x, nx, q * nc)
        gathered = own
        if nz == 4:
            gathered = jnp.concatenate(
                [own] + [lax.ppermute(own, "vocab", flip(nz, k)) for k in (1, 2, 3)], 0
            )
        else:
            for d in bits(nz):
                gathered = jnp.concatenate([gathered, lax.ppermute(gathered, "vocab", flip(nz, d))], 0)
        width = mentor.shape[1] // 2
        left, right = mentor[:, :width], mentor[:, width:]
        kept = jnp.where(c == 0, left, right)
        got = lax.ppermute(jnp.where(c == 0, right, left), "teach", flip(nc, 1))
        scaled = jnp.concatenate([jnp.where(c == 0, kept, got), jnp.where(c == 0, got, kept)], 0)

        def rel(a):
            a = relative(a, c, nc, q)
            a = relative(a, x, nx, q * nc)
            return relative(a, z, nz, q * nc * nx)

        scaled = rel(scaled) / smoothing_divisor
        mask = rel(row_mask).astype(jnp.float32)
        student = (
            lax.dot_general(
                gathered, head_weight, (((1,), (1,)), ((), ())), preferred_element_type=jnp.float32
            )
            / smoothing_divisor
        )
        ms = jnp.max(student, axis=1)
        mt = jnp.max(scaled, axis=1)
        es = jnp.exp(student - ms[:, None])
        et = jnp.exp(scaled - mt[:, None])
        stats = jnp.stack(
            [ms, mt, jnp.sum(es, axis=1), jnp.sum(et, axis=1), jnp.sum(et * (scaled - student), axis=1)], 0
        )
        both = jnp.concatenate([es, et], 0)
        high = both.astype(jnp.bfloat16)
        low = (both - high.astype(jnp.float32)).astype(jnp.bfloat16)
        part = jnp.dot(
            jnp.concatenate([high, low], 0), head_weight, preferred_element_type=jnp.float32
        )
        part = part[: 2 * total] + part[2 * total :]
        part = part.reshape(2, nz, nx, nc, q, -1)

        def merge(keep, stats, others):
            top = stats[:2]
            for _, s in others:
                top = jnp.maximum(top, s[:2])
            factor = [jnp.exp(s[:2] - top) for s in [stats] + [s for _, s in others]]
            sums = sum(
                jnp.concatenate([f * s[2:4], (f[1] * s[4])[None]], 0)
                for f, s in zip(factor, [stats] + [s for _, s in others])
            )
            return top, factor, jnp.concatenate([top, sums], 0)

        def level(part, stats, axis, n, dim, stride):
            if n == 4:
                steps = [(1, 2, 3)]
            else:
                steps = [(d,) for d in reversed(bits(n))]
            size = n
            for ds in steps:
                span = size // (len(ds) + 1)
                keep = lax.slice_in_dim(part, 0, span, axis=dim)
                others = []
                for d in ds:
                    a = lax.ppermute(lax.slice_in_dim(part, d, d + span, axis=dim), axis, flip(n, d))
                    s = lax.ppermute(stats, axis, flip(n, d))
                    s = s.T
                    for b in bits(n):
                        if d & b:
                            s = swap(s, b * stride)
                    others.append((a, s.T))
                _, factor, stats = merge(keep, stats, others)
                rows = [f.reshape(2, nz, nx, nc, q, 1) for f in factor]

                def cut(f):
                    shape = keep.shape
                    for ax in range(1, 4):
                        f = lax.slice_in_dim(f, 0, shape[ax], axis=ax)
                    return f

                part = keep * cut(rows[0])
                for (a, _), f in zip(others, rows[1:]):
                    part = part + a * cut(f)
                size = span
            return part, stats

        part, stats = level(part, stats, "teach", nc, 3, q)
        part, stats = level(part, stats, "rows", nx, 2, q * nc)
        part, stats = level(part, stats, "vocab", nz, 1, q * nc * nx)
        part = part.reshape(2, q, -1)
        ms, mt, ls, lt, cross = stats
        lse_s = ms + jnp.log(ls)
        lse_t = mt + jnp.log(lt)
        divergence = rel(mask * (cross / lt - lse_t + lse_s))
        gain = mask * (objective_scale * smoothing_divisor)
        grad = (
            gain[:, None] * (jnp.exp(student - lse_s[:, None]) - jnp.exp(scaled - lse_t[:, None]))
        ).astype(jnp.bfloat16)
        weight_grad = lax.dot_general(
            grad, gathered, (((0,), (0,)), ((), ())), preferred_element_type=jnp.float32
        )
        hidden_grad = gain[:q, None] * (part[0] / ls[:q, None] - part[1] / lt[:q, None])
        return divergence, hidden_grad.astype(jnp.bfloat16), weight_grad.astype(jnp.bfloat16)

    return body


def solution(mesh):
    body = make_body(mesh.shape["vocab"], mesh.shape["rows"], mesh.shape["teach"])
    return jax.shard_map(
        body,
        mesh=mesh,
        in_specs=(
            P(("groups", "vocab"), None),
            P(("groups", "teach"), ("vocab", "rows")),
            P(("vocab", "rows", "teach"), None),
            P("groups"),
        ),
        out_specs=(
            P("groups"),
            P(("groups", "vocab", "rows", "teach"), None),
            P(("groups", "vocab", "rows", "teach"), None),
        ),
        check_vma=False,
    )
```

time: 149 us -> 50.3 us (0.34)
  blocking collectives: 135 us -> 0 us
  starting transfers between devices: 3.25 us -> 17.6 us
  waiting for transfers between devices: 0.7 us -> 12.4 us
  other arithmetic: 1.73 us -> 7.5 us
  local copies, waits for them, and re-layouts: 3.85 us -> 7.54 us
    psum x2 -> x0, blocking collectives: 89.4 us -> none  [body(): lax.psum((jnp.sum(jnp.exp(learner_unnormalized - max_student[:, None]), a...]
    pmax x1 -> x0, blocking collectives: 30.6 us -> none  [body(): lax.pmax((jnp.max(learner_unnormalized, axis=1), jnp.max(divided_learner_...]
    ppermute x0 -> x14, starting transfers between devices: none -> 17.6 us  [the longest x5 6.16 us: level(): s = lax.ppermute(stats, axis, flip(n, d))]
    all_gather x1 -> x0, blocking collectives: 15.3 us -> none  [body(): gathered = lax.all_gather(hidden_rows, 'vocab', axis=0, tiled=True)]
    ppermute x0 -> x14, waiting for transfers between devices: none -> 12.4 us  [the longest x5 7.31 us: level(): lax.ppermute(lax.slice_in_dim(part, d, d + span, axis=dim), axis, flip(n,...]
    reshape x0 -> x46, local copies, waits for them, and re-layouts: none -> 4.7 us  [the longest x14 2.51 us: swap(): b = a.reshape((n // (2 * d), 2, d) + a.shape[1:])]
    select_n x0 -> x14, other arithmetic: none -> 3.77 us  [the longest x12 2.05 us: relative(): a = jnp.where(position & d != 0, swap(a, d * stride), a)]
    all_to_all x1 -> x0, starting transfers between devices: 3.25 us -> none  [body(): lax.all_to_all(mentor_unnormalized, 'teach', split_axis=1, concat_axis=0,...]
  transfers between devices with their start and end apart: 1 -> 14, of which waited for: 1 -> 7; matrix products, arithmetic and copies ran while one was open for 0% -> 26% of each run, Pallas kernels for 0% -> 0%
where the time goes in v1:
time: 50.3 us; the launch traced here: 49.8 us
  starting transfers between devices  17.6 us (35%)
  waiting for transfers between devices  12.4 us (25%)
  local copies, waits for them, and re-layouts  7.54 us (15%)
  other arithmetic  7.5 us (15%)
  matrix products  3.54 us (7%)
  between operations  1.24 us (2%)
    ppermute x5, waiting for transfers between devices, level(): lax.ppermute(lax.slice_in_dim(part, d, d + span, axis=dim), axis, flip(n,...  7.31 us
    ppermute x5, starting transfers between devices, level(): s = lax.ppermute(stats, axis, flip(n, d))  6.16 us
    ppermute x3, starting transfers between devices, body(): lax.ppermute(own, 'vocab', flip(nz, k))  5.76 us
    ppermute x5, starting transfers between devices, level(): lax.ppermute(lax.slice_in_dim(part, d, d + span, axis=dim), axis, flip(n,...  5.66 us
    ppermute x5, waiting for transfers between devices, level(): s = lax.ppermute(stats, axis, flip(n, d))  5.09 us
    reshape x14, local copies, waits for them, and re-layouts, swap(): b = a.reshape((n // (2 * d), 2, d) + a.shape[1:])  2.51 us
    dot_general x1, matrix products, body(): lax.dot_general(grad, gathered, (((0,), (0,)), ((), ())), preferred_eleme...  2.18 us
    select_n x12, other arithmetic, relative(): a = jnp.where(position & d != 0, swap(a, d * stride), a)  2.05 us
  transfers between devices with their start and end apart: 14, of which 7 were waited for; matrix products, arithmetic and copies ran while one was open for 26% of the time, Pallas kernels for 0%

profile of v1, /device:TPU:0, one launch (start us, length us, event | category | flops | bytes accessed | tf_op | source)
XLA Modules:
  0.0 49.8 jit_solution(847230139734454736)
XLA Ops:
  0.7 0.9 %reshape.397 = bf16[2,2,1,3584]{3,1,0,2:T(2,128)(2,1)S(1)} reshape(bf16[4,3584]{1,0:T(4,128)(2,1)} %param.4) | data formatting | bytes 57344 | tf_op jit(solution)/shard_map/reshape | solution.py:25
  1.7 0.8 %broadcast_select_fusion = bf16[4,3584]{1,0:T(4,128)(2,1)S(1)} fusion(bf16[4,3584]{1,0:T(4,128)(2,1)S(1)} %reshape.398, bf16[4,3584]{1,0:T(4,128)(2,1)} %param.4, pred[]{:T(512)S(6)} %ne.11), kind=kLoop, calls=%fused_computation.21 | loop fusion | flops 14336 | bytes 86017 | tf_op jit(solution)/shard_map/jit(_where)/select_n | solution.py:31
  2.7 5.1 %collective-permute-start.2 = (bf16[4,3584]{1,0:T(4,128)(2,1)S(1)}, bf16[4,3584]{1,0:T(4,128)(2,1)S(1)}, u32[]{:S(2)}, u32[]{:S(2)}) collective-permute-start(bf16[4,3584]{1,0:T(4,128)(2,1)S(1)} %broadcast_select_fusion.1), channel_id=1, source_target_pairs={{0,12},{4,8},{8,4},{12,0},{1,13},{5,9},{9,5},{13,1},{2,14},{6,10},... | collective-permute-start | bytes 86024 | tf_op jit(solution)/shard_map/ppermute | solution.py:44
  7.8 0.6 %collective-permute-start = (bf16[4,3584]{1,0:T(4,128)(2,1)S(1)}, bf16[4,3584]{1,0:T(4,128)(2,1)S(1)}, u32[]{:S(2)}, u32[]{:S(2)}) collective-permute-start(bf16[4,3584]{1,0:T(4,128)(2,1)S(1)} %broadcast_select_fusion.1), channel_id=1, source_target_pairs={{0,4},{4,0},{8,12},{12,8},{1,5},{5,1},{9,13},{13,9},{2,6},{6,2},{1... | collective-permute-start | bytes 86024 | tf_op jit(solution)/shard_map/ppermute | solution.py:44
  8.4 0.9 %slice_select_fusion = f32[8,304]{1,0:T(8,128)S(1)} fusion(f32[8,608]{1,0:T(8,128)} %param.5, pred[]{:T(512)S(6)} %eq.2), kind=kLoop, calls=%fused_computation.47 | loop fusion | flops 2432 | bytes 29185 | tf_op jit(solution)/shard_map/jit(_where)/select_n | solution.py:52
  9.3 0.7 %reshape.389 = s32[8,2,1]{1,0,2:T(8,128)S(1)} reshape(s32[16]{0:T(128)} %param.7) | data formatting | bytes 128 | tf_op jit(solution)/shard_map/reshape | solution.py:25
  10.2 0.7 %broadcast_select_fusion.6 = s32[16]{0:T(128)S(1)} fusion(s32[16]{0:T(128)S(1)} %reshape.390, s32[16]{0:T(128)} %param.7, pred[]{:T(512)S(6)} %ne.11), kind=kLoop, calls=%fused_computation.97 | loop fusion | flops 16 | bytes 193 | tf_op jit(solution)/shard_map/jit(_where)/select_n | solution.py:31
  11.5 0.9 %broadcast_select_fusion.4 = (f32[8,304]{1,0:T(8,128)S(1)}, f32[8,304]{1,0:T(8,128)S(1)}) fusion(f32[8,304]{1,0:T(8,128)S(1)} %collective-permute-done.3, pred[]{:T(512)S(6)} %eq.2, f32[8,608]{1,0:T(8,128)} %param.5), kind=kLoop, calls=%fused_computation.54 | loop fusion | flops 7296 | bytes 48641 | tf_op jit(solution)/shard_map/jit(_where)/select_n | solution.py:53
  13.5 0.8 %multiply_reduce_fusion = (f32[16]{0:T(128)S(1)}, f32[16]{0:T(128)S(1)}, f32[16,304]{1,0:T(8,128)S(1)}) fusion(f32[16,304]{1,0:T(8,128)S(1)} %get-tuple-element.6, f32[16]{0:T(128)S(1)} %sub.96, bf16[304,3584]{1,0:T(8,128)(2,1)S(1)} %copy-done, bf16[4,3584]{1,0:T(4,128)(2,1)S(1)} %collective-permute-done.2, bf16[4,3584]{1,0:T(4,128)(2,1)S(1)} %collective-permute-done.1, ...), kind=kOutput, calls=%fused_computation.36 | convolution fusion | flops 35353056 | bytes 2332864 | tf_op jit(solution)/shard_map/dot_general | solution.py:63
  14.3 0.2 fusion.26
  14.6 0.6 %fusion.2 = f32[64,3584]{1,0:T(8,128)S(1)} fusion(bf16[304,3584]{1,0:T(8,128)(2,1)S(1)} %copy-done, bf16[32,304]{1,0:T(8,128)(2,1)S(1)} %subtract_convert_fusion, bf16[32,304]{1,0:T(8,128)(2,1)S(1)} %fusion.6), kind=kOutput, calls=%fused_computation.9 | convolution fusion | flops 139538432 | bytes 3135488 | tf_op jit(solution)/shard_map/dot_general | solution.py:78
  15.3 0.3 reshape.430
  15.5 0.2 slice.440
  15.8 0.6 %collective-permute-start.9 = (f32[2,4,2,1,1,3584]{5,3,2,1,0,4:T(1,128)S(1)}, f32[2,4,2,1,1,3584]{5,3,2,1,0,4:T(1,128)S(1)}, u32[]{:S(2)}, u32[]{:S(2)}) collective-permute-start(f32[2,4,2,1,1,3584]{5,3,2,1,0,4:T(1,128)S(1)} %slice.440), channel_id=1, source_target_pairs={{0,1},{1,0},{2,3},{3,2},{4,5},{5,4},{6,7},{7,6},{8,9},{9,8},{10,11... | collective-permute-start | bytes 688136 | tf_op jit(solution)/shard_map/ppermute | solution.py:106
  16.9 1.6 %collective-permute-start.5 = (f32[5,16]{1,0:T(8,128)S(1)}, f32[5,16]{1,0:T(8,128)S(1)}, u32[]{:S(2)}, u32[]{:S(2)}) collective-permute-start(f32[5,16]{1,0:T(8,128)S(1)} %pad_maximum_fusion.16), channel_id=1, source_target_pairs={{0,2},{2,0},{1,3},{3,1},{4,6},{6,4},{5,7},{7,5},{8,10},{10,8},{9,1... | collective-permute-start | bytes 968 | tf_op jit(solution)/shard_map/ppermute | solution.py:107
  18.9 1.7 %collective-permute-done.5 = f32[5,16]{1,0:T(8,128)S(1)} collective-permute-done((f32[5,16]{1,0:T(8,128)S(1)}, f32[5,16]{1,0:T(8,128)S(1)}, u32[]{:S(2)}, u32[]{:S(2)}) %collective-permute-start.5) | collective-permute-done | bytes 352 | tf_op jit(solution)/shard_map/ppermute | solution.py:107
  21.0 3.8 %collective-permute-start.8 = (f32[5,16]{1,0:T(8,128)S(1)}, f32[5,16]{1,0:T(8,128)S(1)}, u32[]{:S(2)}, u32[]{:S(2)}) collective-permute-start(f32[5,16]{1,0:T(8,128)S(1)} %pad_maximum_fusion.17), channel_id=1, source_target_pairs={{0,12},{4,8},{8,4},{12,0},{1,13},{5,9},{9,5},{13,1},{2,14},{6,10},... | collective-permute-start | bytes 968 | tf_op jit(solution)/shard_map/ppermute | solution.py:107
  24.8 0.6 %collective-permute-start.6 = (f32[5,16]{1,0:T(8,128)S(1)}, f32[5,16]{1,0:T(8,128)S(1)}, u32[]{:S(2)}, u32[]{:S(2)}) collective-permute-start(f32[5,16]{1,0:T(8,128)S(1)} %pad_maximum_fusion.17), channel_id=1, source_target_pairs={{0,4},{4,0},{8,12},{12,8},{1,5},{5,1},{9,13},{13,9},{2,6},{6,2},{1... | collective-permute-start | bytes 968 | tf_op jit(solution)/shard_map/ppermute | solution.py:107
  25.7 0.8 %collective-permute-done.8 = f32[5,16]{1,0:T(8,128)S(1)} collective-permute-done((f32[5,16]{1,0:T(8,128)S(1)}, f32[5,16]{1,0:T(8,128)S(1)}, u32[]{:S(2)}, u32[]{:S(2)}) %collective-permute-start.8) | collective-permute-done | bytes 352 | tf_op jit(solution)/shard_map/ppermute | solution.py:107
  26.6 2.6 %collective-permute-done.7 = f32[5,16]{1,0:T(8,128)S(1)} collective-permute-done((f32[5,16]{1,0:T(8,128)S(1)}, f32[5,16]{1,0:T(8,128)S(1)}, u32[]{:S(2)}, u32[]{:S(2)}) %collective-permute-start.7) | collective-permute-done | bytes 352 | tf_op jit(solution)/shard_map/ppermute | solution.py:107
  30.0 0.6 %fusion.46 = (f32[1,1]{1,0:T(1,128)}, f32[1,1]{1,0:T(1,128)}) fusion(f32[3,16]{1,0:T(4,128)S(1)} %fusion.18), kind=kLoop, calls=%fused_computation.144 | loop fusion | bytes 16 | tf_op jit(solution)/shard_map/slice | solution.py:143
  31.5 2.2 %convolution_convert_fusion = bf16[304,3584]{1,0:T(8,128)(2,1)} fusion(bf16[4,3584]{1,0:T(4,128)(2,1)S(1)} %collective-permute-done.2, bf16[4,3584]{1,0:T(4,128)(2,1)S(1)} %collective-permute-done.1, bf16[4,3584]{1,0:T(4,128)(2,1)S(1)} %collective-permute-done, bf16[4,3584]{1,0:T(4,128)(2,1)S(1)} %broadcast_select_fusion.1, ...), kind=kOutput, calls=%fused_computation | convolution fusion | flops 36437760 | bytes 2332864 | tf_op jit(solution)/shard_map/dot_general | solution.py:140
  33.9 0.5 %broadcast_select_fusion.11 = f32[16]{0:T(128)} fusion(f32[16]{0:T(128)S(1)} %reshape.429, f32[16]{0:T(128)S(1)} %broadcast_select_fusion.9, pred[]{:T(512)S(6)} %ne.8), kind=kLoop, calls=%fused_computation.102 | loop fusion | flops 16 | bytes 193 | tf_op jit(solution)/shard_map/jit(_where)/select_n | solution.py:31
  34.4 0.3 fusion
  34.7 1.6 %collective-permute-start.10 = (f32[2,4,1,1,1,3584]{5,3,2,1,0,4:T(1,128)S(1)}, f32[2,4,1,1,1,3584]{5,3,2,1,0,4:T(1,128)S(1)}, u32[]{:S(2)}, u32[]{:S(2)}) collective-permute-start(f32[2,4,1,1,1,3584]{5,3,2,1,0,4:T(1,128)S(1)} %slice.444), channel_id=1, source_target_pairs={{0,2},{2,0},{1,3},{3,1},{4,6},{6,4},{5,7},{7,5},{8,10},{10,8},{9,1... | collective-permute-start | bytes 344072 | tf_op jit(solution)/shard_map/ppermute | solution.py:106
  36.6 2.9 %collective-permute-done.10 = f32[2,4,1,1,1,3584]{5,3,2,1,0,4:T(1,128)S(1)} collective-permute-done((f32[2,4,1,1,1,3584]{5,3,2,1,0,4:T(1,128)S(1)}, f32[2,4,1,1,1,3584]{5,3,2,1,0,4:T(1,128)S(1)}, u32[]{:S(2)}, u32[]{:S(2)}) %collective-permute-start.10) | collective-permute-done | bytes 114720 | tf_op jit(solution)/shard_map/ppermute | solution.py:106
  39.8 3.2 %collective-permute-start.13 = (f32[2,1,1,1,1,3584]{5,3,2,1,0,4:T(1,128)S(1)}, f32[2,1,1,1,1,3584]{5,3,2,1,0,4:T(1,128)S(1)}, u32[]{:S(2)}, u32[]{:S(2)}) collective-permute-start(f32[2,1,1,1,1,3584]{5,3,2,1,0,4:T(1,128)S(1)} %get-tuple-element.34), channel_id=1, source_target_pairs={{0,12},{4,8},{8,4},{12,0},{1,13},{5,9},{9,5},{13,1},{2,14},{6,10},... | collective-permute-start | bytes 86024 | tf_op jit(solution)/shard_map/ppermute | solution.py:106
  43.0 0.3 collective-permute-start.12
  43.4 0.3 collective-permute-done.11
  43.7 1.9 %collective-permute-done.13 = f32[2,1,1,1,1,3584]{5,3,2,1,0,4:T(1,128)S(1)} collective-permute-done((f32[2,1,1,1,1,3584]{5,3,2,1,0,4:T(1,128)S(1)}, f32[2,1,1,1,1,3584]{5,3,2,1,0,4:T(1,128)S(1)}, u32[]{:S(2)}, u32[]{:S(2)}) %collective-permute-start.13) | collective-permute-done | bytes 28704 | tf_op jit(solution)/shard_map/ppermute | solution.py:106
  45.6 2.2 %collective-permute-done.12 = f32[2,1,1,1,1,3584]{5,3,2,1,0,4:T(1,128)S(1)} collective-permute-done((f32[2,1,1,1,1,3584]{5,3,2,1,0,4:T(1,128)S(1)}, f32[2,1,1,1,1,3584]{5,3,2,1,0,4:T(1,128)S(1)}, u32[]{:S(2)}, u32[]{:S(2)}) %collective-permute-start.12) | collective-permute-done | bytes 28704 | tf_op jit(solution)/shard_map/ppermute | solution.py:106
  47.9 1.9 %convert_bitcast_fusion = bf16[1,3584]{1,0:T(2,128)(2,1)} fusion(f32[2,1,1,1,1,3584]{5,3,2,1,0,4:T(1,128)S(1)} %multiply_add_fusion, f32[]{:T(128)} %bitcast.27, f32[]{:T(128)} %bitcast.26, f32[]{:T(128)S(1)} %bitcast.119), kind=kLoop, calls=%fused_computation.43 | loop fusion | flops 17920 | bytes 35852 | tf_op jit(solution)/shard_map/convert_element_type | solution.py:144
  (156 shorter events, 6.4 us)
Async XLA Ops:
  0.6 12.9 %copy-start = (bf16[304,3584]{1,0:T(8,128)(2,1)S(1)}, bf16[304,3584]{1,0:T(8,128)(2,1)}, u32[]{:S(2)}) copy-start(bf16[304,3584]{1,0:T(8,128)(2,1)} %param.6) | copy-start | bytes 6537220
  2.7 10.8 %collective-permute-start.2 = (bf16[4,3584]{1,0:T(4,128)(2,1)S(1)}, bf16[4,3584]{1,0:T(4,128)(2,1)S(1)}, u32[]{:S(2)}, u32[]{:S(2)}) collective-permute-start(bf16[4,3584]{1,0:T(4,128)(2,1)S(1)} %broadcast_select_fusion.1), channel_id=1, source_target_pairs={{0,12},{4,8},{8,4},{12,0},{1,13},{5,9},{9,5},{13,1},{2,14},{6,10},... | collective-permute-start | bytes 86024 | tf_op jit(solution)/shard_map/ppermute | solution.py:44
  7.8 5.7 %collective-permute-start.1 = (bf16[4,3584]{1,0:T(4,128)(2,1)S(1)}, bf16[4,3584]{1,0:T(4,128)(2,1)S(1)}, u32[]{:S(2)}, u32[]{:S(2)}) collective-permute-start(bf16[4,3584]{1,0:T(4,128)(2,1)S(1)} %broadcast_select_fusion.1), channel_id=1, source_target_pairs={{0,8},{4,12},{8,0},{12,4},{1,9},{5,13},{9,1},{13,5},{2,10},{6,14},... | collective-permute-start | bytes 86024 | tf_op jit(solution)/shard_map/ppermute | solution.py:44
  7.8 5.7 %collective-permute-start = (bf16[4,3584]{1,0:T(4,128)(2,1)S(1)}, bf16[4,3584]{1,0:T(4,128)(2,1)S(1)}, u32[]{:S(2)}, u32[]{:S(2)}) collective-permute-start(bf16[4,3584]{1,0:T(4,128)(2,1)S(1)} %broadcast_select_fusion.1), channel_id=1, source_target_pairs={{0,4},{4,0},{8,12},{12,8},{1,5},{5,1},{9,13},{13,9},{2,6},{6,2},{1... | collective-permute-start | bytes 86024 | tf_op jit(solution)/shard_map/ppermute | solution.py:44
  9.3 2.2 %collective-permute-start.3 = (f32[8,304]{1,0:T(8,128)S(1)}, f32[8,304]{1,0:T(8,128)S(1)}, u32[]{:S(2)}, u32[]{:S(2)}) collective-permute-start(f32[8,304]{1,0:T(8,128)S(1)} %slice_select_fusion), channel_id=1, source_target_pairs={{0,1},{1,0},{2,3},{3,2},{4,5},{5,4},{6,7},{7,6},{8,9},{9,8},{10,11... | collective-permute-start | bytes 29192 | tf_op jit(solution)/shard_map/ppermute | solution.py:52
  14.6 1.8 %collective-permute-start.4 = (f32[5,16]{1,0:T(8,128)S(1)}, f32[5,16]{1,0:T(8,128)S(1)}, u32[]{:S(2)}, u32[]{:S(2)}) collective-permute-start(f32[5,16]{1,0:T(8,128)S(1)} %stack.28), channel_id=1, source_target_pairs={{0,1},{1,0},{2,3},{3,2},{4,5},{5,4},{6,7},{7,6},{8,9},{9,8},{10,11... | collective-permute-start | bytes 968 | tf_op jit(solution)/shard_map/ppermute | solution.py:107
  15.8 18.6 %collective-permute-start.9 = (f32[2,4,2,1,1,3584]{5,3,2,1,0,4:T(1,128)S(1)}, f32[2,4,2,1,1,3584]{5,3,2,1,0,4:T(1,128)S(1)}, u32[]{:S(2)}, u32[]{:S(2)}) collective-permute-start(f32[2,4,2,1,1,3584]{5,3,2,1,0,4:T(1,128)S(1)} %slice.440), channel_id=1, source_target_pairs={{0,1},{1,0},{2,3},{3,2},{4,5},{5,4},{6,7},{7,6},{8,9},{9,8},{10,11... | collective-permute-start | bytes 688136 | tf_op jit(solution)/shard_map/ppermute | solution.py:106
  16.9 3.6 %collective-permute-start.5 = (f32[5,16]{1,0:T(8,128)S(1)}, f32[5,16]{1,0:T(8,128)S(1)}, u32[]{:S(2)}, u32[]{:S(2)}) collective-permute-start(f32[5,16]{1,0:T(8,128)S(1)} %pad_maximum_fusion.16), channel_id=1, source_target_pairs={{0,2},{2,0},{1,3},{3,1},{4,6},{6,4},{5,7},{7,5},{8,10},{10,8},{9,1... | collective-permute-start | bytes 968 | tf_op jit(solution)/shard_map/ppermute | solution.py:107
  21.0 5.5 %collective-permute-start.8 = (f32[5,16]{1,0:T(8,128)S(1)}, f32[5,16]{1,0:T(8,128)S(1)}, u32[]{:S(2)}, u32[]{:S(2)}) collective-permute-start(f32[5,16]{1,0:T(8,128)S(1)} %pad_maximum_fusion.17), channel_id=1, source_target_pairs={{0,12},{4,8},{8,4},{12,0},{1,13},{5,9},{9,5},{13,1},{2,14},{6,10},... | collective-permute-start | bytes 968 | tf_op jit(solution)/shard_map/ppermute | solution.py:107
  24.8 4.5 %collective-permute-start.7 = (f32[5,16]{1,0:T(8,128)S(1)}, f32[5,16]{1,0:T(8,128)S(1)}, u32[]{:S(2)}, u32[]{:S(2)}) collective-permute-start(f32[5,16]{1,0:T(8,128)S(1)} %pad_maximum_fusion.17), channel_id=1, source_target_pairs={{0,8},{4,12},{8,0},{12,4},{1,9},{5,13},{9,1},{13,5},{2,10},{6,14},... | collective-permute-start | bytes 968 | tf_op jit(solution)/shard_map/ppermute | solution.py:107
  24.8 4.8 %collective-permute-start.6 = (f32[5,16]{1,0:T(8,128)S(1)}, f32[5,16]{1,0:T(8,128)S(1)}, u32[]{:S(2)}, u32[]{:S(2)}) collective-permute-start(f32[5,16]{1,0:T(8,128)S(1)} %pad_maximum_fusion.17), channel_id=1, source_target_pairs={{0,4},{4,0},{8,12},{12,8},{1,5},{5,1},{9,13},{13,9},{2,6},{6,2},{1... | collective-permute-start | bytes 968 | tf_op jit(solution)/shard_map/ppermute | solution.py:107
  34.7 4.9 %collective-permute-start.10 = (f32[2,4,1,1,1,3584]{5,3,2,1,0,4:T(1,128)S(1)}, f32[2,4,1,1,1,3584]{5,3,2,1,0,4:T(1,128)S(1)}, u32[]{:S(2)}, u32[]{:S(2)}) collective-permute-start(f32[2,4,1,1,1,3584]{5,3,2,1,0,4:T(1,128)S(1)} %slice.444), channel_id=1, source_target_pairs={{0,2},{2,0},{1,3},{3,1},{4,6},{6,4},{5,7},{7,5},{8,10},{10,8},{9,1... | collective-permute-start | bytes 344072 | tf_op jit(solution)/shard_map/ppermute | solution.py:106
  39.8 3.9 %collective-permute-start.11 = (f32[2,1,1,1,1,3584]{5,3,2,1,0,4:T(1,128)S(1)}, f32[2,1,1,1,1,3584]{5,3,2,1,0,4:T(1,128)S(1)}, u32[]{:S(2)}, u32[]{:S(2)}) collective-permute-start(f32[2,1,1,1,1,3584]{5,3,2,1,0,4:T(1,128)S(1)} %get-tuple-element.33), channel_id=1, source_target_pairs={{0,4},{4,0},{8,12},{12,8},{1,5},{5,1},{9,13},{13,9},{2,6},{6,2},{1... | collective-permute-start | bytes 86024 | tf_op jit(solution)/shard_map/ppermute | solution.py:106
  39.8 5.7 %collective-permute-start.13 = (f32[2,1,1,1,1,3584]{5,3,2,1,0,4:T(1,128)S(1)}, f32[2,1,1,1,1,3584]{5,3,2,1,0,4:T(1,128)S(1)}, u32[]{:S(2)}, u32[]{:S(2)}) collective-permute-start(f32[2,1,1,1,1,3584]{5,3,2,1,0,4:T(1,128)S(1)} %get-tuple-element.34), channel_id=1, source_target_pairs={{0,12},{4,8},{8,4},{12,0},{1,13},{5,9},{9,5},{13,1},{2,14},{6,10},... | collective-permute-start | bytes 86024 | tf_op jit(solution)/shard_map/ppermute | solution.py:106
  43.0 4.8 %collective-permute-start.12 = (f32[2,1,1,1,1,3584]{5,3,2,1,0,4:T(1,128)S(1)}, f32[2,1,1,1,1,3584]{5,3,2,1,0,4:T(1,128)S(1)}, u32[]{:S(2)}, u32[]{:S(2)}) collective-permute-start(f32[2,1,1,1,1,3584]{5,3,2,1,0,4:T(1,128)S(1)} %get-tuple-element.35), channel_id=1, source_target_pairs={{0,8},{4,12},{8,0},{12,4},{1,9},{5,13},{9,1},{13,5},{2,10},{6,14},... | collective-permute-start | bytes 86024 | tf_op jit(solution)/shard_map/ppermute | solution.py:106

commit v2 on v1

--- a/solution.py
+++ b/solution.py
@@ -1,6 +1,8 @@
 import jax
 import jax.numpy as jnp
 from jax import lax
+from jax.experimental import pallas as pl
+from jax.experimental.pallas import tpu as pltpu
 from jax.sharding import PartitionSpec as P
 
 smoothing_divisor = 2.0
@@ -146,8 +148,248 @@
     return body
 
 
+ROWS = 16
+STATS = 128
+
+
+def pack(columns):
+    lane = lax.broadcasted_iota(jnp.int32, (ROWS, STATS), 1)
+    out = jnp.zeros((ROWS, STATS), jnp.float32)
+    for i, column in enumerate(columns):
+        out = jnp.where(lane == i, column, out)
+    return out
+
+
+def unite(parts):
+    top = parts[0]
+    for s in parts[1:]:
+        top = jnp.maximum(top, s)
+    factors = [jnp.exp(s - top) for s in parts]
+    ls = sum(s[:, 2:3] * f[:, 0:1] for s, f in zip(parts, factors))
+    lt = sum(s[:, 3:4] * f[:, 1:2] for s, f in zip(parts, factors))
+    cross = sum(s[:, 4:5] * f[:, 1:2] for s, f in zip(parts, factors))
+    return factors, [top[:, 0:1], top[:, 1:2], ls, lt, cross]
+
+
+def places():
+    return lax.axis_index("vocab"), lax.axis_index("rows"), lax.axis_index("teach")
+
+
+def row_of(b, x, c):
+    return 2 * (x ^ (b & 1)) + (c ^ (b >> 1))
+
+
+def first_kernel(h0, h1, h2, h3, w, own_t, got_t, student, scaled, stats, keep, send, hf, raw, tt, e):
+    z, x, c = places()
+    for k, h in enumerate((h0, h1, h2, h3)):
+        hf[4 * k : 4 * k + 4, :] = h[...].astype(jnp.float32)
+    raw[...] = 0.5 * lax.dot_general(
+        hf[...].astype(jnp.bfloat16), w[...], (((1,), (1,)), ((), ())), preferred_element_type=jnp.float32
+    )
+    tt[pl.ds(8 * c, 8), :] = own_t[...]
+    tt[pl.ds(8 * (1 - c), 8), :] = got_t[...]
+    for b in range(4):
+        j = row_of(b, x, c)
+        for k in range(4):
+            student[4 * b + k : 4 * b + k + 1, :] = raw[pl.ds(4 * k + j, 1), :]
+            scaled[4 * b + k : 4 * b + k + 1, :] = 0.5 * tt[pl.ds(4 * (k ^ z) + j, 1), :]
+    s = student[...]
+    t = scaled[...]
+    ms = jnp.max(s, axis=1, keepdims=True)
+    mt = jnp.max(t, axis=1, keepdims=True)
+    es = jnp.exp(s - ms)
+    et = jnp.exp(t - mt)
+    st = pack(
+        [
+            ms,
+            mt,
+            jnp.sum(es, axis=1, keepdims=True),
+            jnp.sum(et, axis=1, keepdims=True),
+            jnp.sum(et * (t - s), axis=1, keepdims=True),
+        ]
+    )
+    stats[...] = st
+    for b in range(4):
+        e[8 * b : 8 * b + 4, :] = es[4 * b : 4 * b + 4, :]
+        e[8 * b + 4 : 8 * b + 8, :] = et[4 * b : 4 * b + 4, :]
+    both = e[...]
+    high = both.astype(jnp.bfloat16)
+    low = (both - high.astype(jnp.float32)).astype(jnp.bfloat16)
+    part = jnp.dot(jnp.concatenate([high, low], 0), w[...], preferred_element_type=jnp.float32)
+    d = part.shape[1]
+    keep[...] = part[0:16] + part[32:48]
+    send[:, 0:d] = part[16:32] + part[48:64]
+    send[0:8, d:] = st[8:16]
+    send[8:16, d:] = st[0:8]
+
+
+def second_kernel(part, stats, got, stats_out, keep, send):
+    d = part.shape[1]
+    factors, columns = unite([stats[...], got[:, d:]])
+    st = pack(columns)
+    stats_out[...] = st
+    scale = [
+        jnp.concatenate([f[0:4, 0:1], f[0:4, 1:2], f[4:8, 0:1], f[4:8, 1:2]], 0) for f in factors
+    ]
+    total = part[...] * scale[0] + got[:, 0:d] * scale[1]
+    keep[...] = total[0:8]
+    send[:, 0:d] = total[8:16]
+    for i in range(2):
+        send[0:4, d + 128 * i : d + 128 * i + 128] = st[8 * i + 4 : 8 * i + 8]
+        send[4:8, d + 128 * i : d + 128 * i + 128] = st[8 * i : 8 * i + 4]
+
+
+def third_kernel(part, stats, got, stats_out, keep, send1, send2, send3, gs):
+    d = part.shape[1]
+    for i in range(2):
+        gs[8 * i : 8 * i + 8, :] = got[:, d + 128 * i : d + 128 * i + 128]
+    factors, columns = unite([stats[...], gs[...]])
+    st = pack(columns)
+    stats_out[...] = st
+    scale = [jnp.concatenate([f[0:4, 0:1], f[0:4, 1:2]], 0) for f in factors]
+    total = part[...] * scale[0] + got[:, 0:d] * scale[1]
+    keep[0:1, :] = total[0:1]
+    keep[1:2, :] = total[4:5]
+    for k, send in enumerate((send1, send2, send3), 1):
+        send[0:1, 0:d] = total[k : k + 1]
+        send[1:2, 0:d] = total[4 + k : 5 + k]
+        for p in range(ROWS):
+            at = d + 128 * (p // 2)
+            r = p ^ k
+            send[p % 2 : p % 2 + 1, at : at + 128] = st[r : r + 1]
+
+
+def make_last_kernel(chunk):
+    def last_kernel(
+        mask, part, stats, got1, got2, got3, student, scaled, h0, h1, h2, h3,
+        divergence, hidden_grad, weight_grad, gs, hf, gr, out, sems,
+    ):
+        z, x, c = places()
+        d = part.shape[1]
+        parts = [stats[...]]
+        for k, got in enumerate((got1, got2, got3)):
+            for i in range(8):
+                gs[k, 2 * i : 2 * i + 2, :] = got[:, d + 128 * i : d + 128 * i + 128]
+            parts.append(gs[k])
+        factors, (ms, mt, ls, lt, cross) = unite(parts)
+        lse_s = ms + jnp.log(ls)
+        lse_t = mt + jnp.log(lt)
+        row = lax.broadcasted_iota(jnp.int32, (ROWS, 1), 0)
+        valid = jnp.zeros((ROWS, 1), jnp.float32)
+        for r in range(ROWS):
+            b, k = r // 4, r % 4
+            valid = jnp.where(
+                row == r, mask[4 * (k ^ z) + row_of(b, x, c)].astype(jnp.float32), valid
+            )
+        gain = valid * (objective_scale * smoothing_divisor)
+        grad = gain * (jnp.exp(student[...] - lse_s) - jnp.exp(scaled[...] - lse_t))
+        for b in range(4):
+            j = row_of(b, x, c)
+            for k in range(4):
+                gr[pl.ds(4 * k + j, 1), :] = grad[4 * b + k : 4 * b + k + 1, :]
+        for k, h in enumerate((h0, h1, h2, h3)):
+            hf[4 * k : 4 * k + 4, :] = h[...].astype(jnp.float32)
+        g = gr[...].astype(jnp.bfloat16)
+        copies = []
+        for i in range(d // chunk):
+            at = pl.ds(i * chunk, chunk)
+            out[:, at] = lax.dot_general(
+                g,
+                hf[:, at].astype(jnp.bfloat16),
+                (((0,), (0,)), ((), ())),
+                preferred_element_type=jnp.float32,
+            ).astype(jnp.bfloat16)
+            copy = pltpu.make_async_copy(out.at[:, at], weight_grad.at[:, at], sems.at[i])
+            copy.start()
+            copies.append(copy)
+        home = 4 * (z ^ (row & 3)) + 2 * (x ^ ((row >> 2) & 1)) + (c ^ (row >> 3))
+        value = valid * (cross / lt - lse_t + lse_s)
+        lane = lax.broadcasted_iota(jnp.int32, (ROWS, STATS), 1)
+        divergence[...] = jnp.sum(jnp.where(lane == home, value, 0.0), axis=0, keepdims=True)
+        a_s = part[0:1, :] * factors[0][0:1, 0:1]
+        a_t = part[1:2, :] * factors[0][0:1, 1:2]
+        for got, f in zip((got1, got2, got3), factors[1:]):
+            a_s = a_s + got[0:1, 0:d] * f[0:1, 0:1]
+            a_t = a_t + got[1:2, 0:d] * f[0:1, 1:2]
+        hidden_grad[...] = (
+            gain[0:1] * (a_s / ls[0:1] - a_t / lt[0:1])
+        ).astype(jnp.bfloat16)
+        for copy in copies:
+            copy.wait()
+
+    return last_kernel
+
+
+VMEM = pl.BlockSpec(memory_space=pltpu.VMEM)
+SMEM = pl.BlockSpec(memory_space=pltpu.SMEM)
+PARAMS = pltpu.CompilerParams(vmem_limit_bytes=32 << 20)
+
+
+def call(kernel, out, scratch=(), in_specs=None, out_specs=None):
+    shapes = [jax.ShapeDtypeStruct(s, t) for s, t in out]
+    return lambda *a: pl.pallas_call(
+        kernel,
+        out_shape=shapes,
+        in_specs=in_specs or [VMEM] * len(a),
+        out_specs=out_specs or [VMEM] * len(out),
+        scratch_shapes=list(scratch),
+        compiler_params=PARAMS,
+    )(*a)
+
+
+def small_body(hidden_rows, mentor, head_weight, row_mask):
+    f32, bf16 = jnp.float32, jnp.bfloat16
+    v, d = head_weight.shape
+    c = lax.axis_index("teach")
+    pieces = [hidden_rows] + [lax.ppermute(hidden_rows, "vocab", flip(4, k)) for k in (1, 2, 3)]
+    left, right = mentor[:, :v], mentor[:, v:]
+    got_t = lax.ppermute(jnp.where(c == 0, right, left), "teach", flip(2, 1))
+    own_t = jnp.where(c == 0, left, right)
+    student, scaled, stats, keep, send = call(
+        first_kernel,
+        [((ROWS, v), f32), ((ROWS, v), f32), ((ROWS, STATS), f32), ((16, d), f32), ((16, d + STATS), f32)],
+        [
+            pltpu.VMEM((ROWS, d), f32),
+            pltpu.VMEM((ROWS, v), f32),
+            pltpu.VMEM((ROWS, v), f32),
+            pltpu.VMEM((2 * ROWS, v), f32),
+        ],
+    )(*pieces, head_weight, own_t, got_t)
+    got = lax.ppermute(send, "teach", flip(2, 1))
+    stats, keep, send = call(
+        second_kernel, [((ROWS, STATS), f32), ((8, d), f32), ((8, d + 2 * STATS), f32)]
+    )(keep, stats, got)
+    got = lax.ppermute(send, "rows", flip(2, 1))
+    stats, keep, *sends = call(
+        third_kernel,
+        [((ROWS, STATS), f32), ((2, d), f32)] + [((2, d + 8 * STATS), f32)] * 3,
+        [pltpu.VMEM((ROWS, STATS), f32)],
+    )(keep, stats, got)
+    gots = [lax.ppermute(a, "vocab", flip(4, k)) for k, a in enumerate(sends, 1)]
+    chunk = 512
+    divergence, hidden_grad, weight_grad = call(
+        make_last_kernel(chunk),
+        [((1, STATS), f32), ((1, d), bf16), ((v, d), bf16)],
+        [
+            pltpu.VMEM((3, ROWS, STATS), f32),
+            pltpu.VMEM((ROWS, d), f32),
+            pltpu.VMEM((ROWS, v), f32),
+            pltpu.VMEM((v, d), bf16),
+            pltpu.SemaphoreType.DMA((d // chunk,)),
+        ],
+        [SMEM] + [VMEM] * 11,
+        [VMEM, VMEM, pl.BlockSpec(memory_space=pl.ANY)],
+    )(row_mask, keep, stats, *gots, student, scaled, *pieces)
+    return divergence[0, :ROWS], hidden_grad, weight_grad
+
+
 def solution(mesh):
-    body = make_body(mesh.shape["vocab"], mesh.shape["rows"], mesh.shape["teach"])
+    sizes = mesh.shape["vocab"], mesh.shape["rows"], mesh.shape["teach"]
+    general = make_body(*sizes)
+
+    def body(hidden_rows, mentor, head_weight, row_mask):
+        small = sizes == (4, 2, 2) and row_mask.shape[0] == ROWS and head_weight.shape[1] % 512 == 0
+        return (small_body if small else general)(hidden_rows, mentor, head_weight, row_mask)
     return jax.shard_map(
         body,
         mesh=mesh,

time: 50.3 us -> 34.3 us (0.68)
  other arithmetic: 7.5 us -> 0.85 us
  starting transfers between devices: 17.6 us -> 11.8 us
  Pallas kernels: 0 us -> 5.53 us
  local copies, waits for them, and re-layouts: 7.54 us -> 2.89 us
  matrix products: 3.54 us -> 0 us
  between operations: 1.24 us -> 0.7 us
    ppermute x14 -> x9, starting transfers between devices: 17.6 us -> 11.8 us  [the longest x3 5.76 us: small_body(): lax.ppermute(hidden_rows, 'vocab', flip(4, k))]
    pallas_call x0 -> x4, Pallas kernels: none -> 5.53 us  [call(): pl.pallas_call(kernel, out_shape=shapes, in_specs=in_specs or [VMEM] * le...]
    reshape x46 -> x0, local copies, waits for them, and re-layouts: 4.7 us -> none  [the longest x14 2.51 us: swap(): b = a.reshape((n // (2 * d), 2, d) + a.shape[1:])]
    dot_general x3 -> x0, matrix products: 3.54 us -> none  [the longest x1 2.18 us: body(): lax.dot_general(grad, gathered, (((0,), (0,)), ((), ())), preferred_eleme...]
    select_n x14 -> x1, other arithmetic: 3.77 us -> 0.85 us  [small_body(): got_t = lax.ppermute(jnp.where(c == 0, right, left), 'teach', flip(2, 1))]
    unnamed x2 -> x8, local copies, waits for them, and re-layouts: 0.01 us -> 2.37 us
    slice x32 -> x0, local copies, waits for them, and re-layouts: 2.06 us -> none  [the longest x8 0.86 us: cut(): f = lax.slice_in_dim(f, 0, shape[ax], axis=ax)]
    convert_element_type x3 -> x0, other arithmetic: 1.87 us -> none  [the longest x1 1.86 us: body(): hidden_grad.astype(jnp.bfloat16)]
  transfers between devices with their start and end apart: 14 -> 9, of which waited for: 7 -> 6; matrix products, arithmetic and copies ran while one was open for 26% -> 3% of each run, Pallas kernels for 0% -> 0%
where the time goes in v2:
time: 34.3 us; the launch traced here: 34.1 us
  waiting for transfers between devices  12.3 us (36%)
  starting transfers between devices  11.8 us (34%)
  Pallas kernels  5.53 us (16%)
  local copies, waits for them, and re-layouts  2.89 us (8%)
  other arithmetic  0.85 us (2%)
  between operations  0.7 us (2%)
    ppermute x3, starting transfers between devices, small_body(): lax.ppermute(hidden_rows, 'vocab', flip(4, k))  5.76 us
    pallas_call x4, Pallas kernels, call(): pl.pallas_call(kernel, out_shape=shapes, in_specs=in_specs or [VMEM] * le...  5.53 us
    ppermute x3, starting transfers between devices, small_body(): lax.ppermute(a, 'vocab', flip(4, k))  4.44 us
    ppermute x1, waiting for transfers between devices, small_body(): got = lax.ppermute(send, 'rows', flip(2, 1))  3.87 us
    ppermute x3, waiting for transfers between devices, small_body(): lax.ppermute(a, 'vocab', flip(4, k))  3.47 us
    unnamed x8, local copies, waits for them, and re-layouts  2.37 us
    ppermute x3, waiting for transfers between devices, small_body(): lax.ppermute(hidden_rows, 'vocab', flip(4, k))  2.3 us
    ppermute x1, starting transfers between devices, small_body(): got = lax.ppermute(send, 'rows', flip(2, 1))  1.56 us
  transfers between devices with their start and end apart: 9, of which 6 were waited for; matrix products, arithmetic and copies ran while one was open for 3% of the time, Pallas kernels for 0%

profile of v2, /device:TPU:0, one launch (start us, length us, event | category | flops | bytes accessed | tf_op | source)
XLA Modules:
  0.0 34.1 jit_solution(8764612448450029054)
XLA Ops:
  0.6 0.0 copy-start.2
  0.6 0.0 copy-start.3
  0.7 5.1 %collective-permute-start.2 = (bf16[4,3584]{1,0:T(4,128)(2,1)}, bf16[4,3584]{1,0:T(4,128)(2,1)S(1)}, u32[]{:S(2)}, u32[]{:S(2)}) collective-permute-start(bf16[4,3584]{1,0:T(4,128)(2,1)} %h0.3), channel_id=1, source_target_pairs={{0,12},{4,8},{8,4},{12,0},{1,13},{5,9},{9,5},{13,1},{2,14},{6,10},... | collective-permute-start | bytes 86024 | tf_op jit(solution)/shard_map/ppermute | solution.py:344
  5.8 0.0 collective-permute-start.1
  5.8 0.6 %collective-permute-start = (bf16[4,3584]{1,0:T(4,128)(2,1)}, bf16[4,3584]{1,0:T(4,128)(2,1)S(1)}, u32[]{:S(2)}, u32[]{:S(2)}) collective-permute-start(bf16[4,3584]{1,0:T(4,128)(2,1)} %h0.3), channel_id=1, source_target_pairs={{0,4},{4,0},{8,12},{12,8},{1,5},{5,1},{9,13},{13,9},{2,6},{6,2},{1... | collective-permute-start | bytes 86024 | tf_op jit(solution)/shard_map/ppermute | solution.py:344
  6.4 0.9 %slice_select_fusion = (f32[8,304]{1,0:T(8,128)S(1)}, f32[8,304]{1,0:T(8,128)S(1)}) fusion(f32[8,608]{1,0:T(8,128)} %param.5, pred[]{:T(512)S(6)} %eq.4), kind=kLoop, calls=%fused_computation | loop fusion | flops 4864 | bytes 38913 | tf_op jit(solution)/shard_map/jit(_where)/select_n | solution.py:346
  7.3 0.0 collective-permute-start.3
  7.3 1.2 %collective-permute-done.3.got_t = f32[8,304]{1,0:T(8,128)S(1)} collective-permute-done((f32[8,304]{1,0:T(8,128)S(1)}, f32[8,304]{1,0:T(8,128)S(1)}, u32[]{:S(2)}, u32[]{:S(2)}) %collective-permute-start.3) | collective-permute-done | bytes 9760 | tf_op jit(solution)/shard_map/ppermute | solution.py:346
  8.4 0.0 collective-permute-done.2.h3
  8.5 2.3 %collective-permute-done.1.h2 = bf16[4,3584]{1,0:T(4,128)(2,1)S(1)} collective-permute-done((bf16[4,3584]{1,0:T(4,128)(2,1)}, bf16[4,3584]{1,0:T(4,128)(2,1)S(1)}, u32[]{:S(2)}, u32[]{:S(2)}) %collective-permute-start.1) | collective-permute-done | bytes 28704 | tf_op jit(solution)/shard_map/ppermute | solution.py:344
  10.7 0.0 collective-permute-done.h1
  10.8 0.0 copy-start
  10.8 1.6 %copy-done = bf16[304,3584]{1,0:T(8,128)(2,1)S(1)} copy-done((bf16[304,3584]{1,0:T(8,128)(2,1)S(1)}, bf16[304,3584]{1,0:T(8,128)(2,1)}, u32[]{:S(2)}) %copy-start) | copy-done | bytes 2179096
  12.4 0.0 copy-start.1
  12.4 0.7 %copy-done.1 = bf16[4,3584]{1,0:T(4,128)(2,1)S(1)} copy-done((bf16[4,3584]{1,0:T(4,128)(2,1)S(1)}, bf16[4,3584]{1,0:T(4,128)(2,1)}, u32[]{:S(2)}) %copy-start.1) | copy-done | bytes 28696
  13.1 2.1 %shard_map.67 = (f32[16,304]{1,0:T(8,128)S(1)}, f32[16,304]{1,0:T(8,128)S(1)}, f32[16,128]{1,0:T(8,128)S(1)}, f32[16,3584]{1,0:T(8,128)S(1)}, f32[16,3712]{1,0:T(8,128)S(1)}) custom-call(bf16[4,3584]{1,0:T(4,128)(2,1)S(1)} %copy-done.1, bf16[4,3584]{1,0:T(4,128)(2,1)S(1)} %collective-permute-done.h1, bf16[4,3584]{1,0:T(4,128)(2,1)S(1)} %collective-permute-done.1.h2, ...), custom_call_target="tpu_custom_call" | custom-call | tf_op jit(solution)/shard_map/pallas_call | solution.py:330
  15.2 0.0 collective-permute-start.4
  15.2 1.5 %collective-permute-done.4.got = f32[16,3712]{1,0:T(8,128)S(1)} collective-permute-done((f32[16,3712]{1,0:T(8,128)S(1)}, f32[16,3712]{1,0:T(8,128)S(1)}, u32[]{:S(2)}, u32[]{:S(2)}) %collective-permute-start.4) | collective-permute-done | bytes 237600 | tf_op jit(solution)/shard_map/ppermute | solution.py:358
  16.7 0.2 shard_map.68
  16.9 1.6 %collective-permute-start.5 = (f32[8,3840]{1,0:T(8,128)S(1)}, f32[8,3840]{1,0:T(8,128)S(1)}, u32[]{:S(2)}, u32[]{:S(2)}) collective-permute-start(f32[8,3840]{1,0:T(8,128)S(1)} %get-tuple-element.24), channel_id=1, source_target_pairs={{0,2},{2,0},{1,3},{3,1},{4,6},{6,4},{5,7},{7,5},{8,10},{10,8},{9,1... | collective-permute-start | bytes 368648 | tf_op jit(solution)/shard_map/ppermute | solution.py:362
  18.5 3.9 %collective-permute-done.5.got = f32[8,3840]{1,0:T(8,128)S(1)} collective-permute-done((f32[8,3840]{1,0:T(8,128)S(1)}, f32[8,3840]{1,0:T(8,128)S(1)}, u32[]{:S(2)}, u32[]{:S(2)}) %collective-permute-start.5) | collective-permute-done | bytes 122912 | tf_op jit(solution)/shard_map/ppermute | solution.py:362
  22.3 0.2 shard_map.69
  22.5 0.1 collective-permute-start.6
  22.6 2.1 %collective-permute-start.7 = (f32[2,4608]{1,0:T(2,128)S(1)}, f32[2,4608]{1,0:T(2,128)S(1)}, u32[]{:S(2)}, u32[]{:S(2)}) collective-permute-start(f32[2,4608]{1,0:T(2,128)S(1)} %get-tuple-element.28), channel_id=1, source_target_pairs={{0,8},{4,12},{8,0},{12,4},{1,9},{5,13},{9,1},{13,5},{2,10},{6,14},... | collective-permute-start | bytes 110600 | tf_op jit(solution)/shard_map/ppermute | solution.py:368
  24.7 2.3 %collective-permute-start.8 = (f32[2,4608]{1,0:T(2,128)S(1)}, f32[2,4608]{1,0:T(2,128)S(1)}, u32[]{:S(2)}, u32[]{:S(2)}) collective-permute-start(f32[2,4608]{1,0:T(2,128)S(1)} %get-tuple-element.29), channel_id=1, source_target_pairs={{0,12},{4,8},{8,4},{12,0},{1,13},{5,9},{9,5},{13,1},{2,14},{6,10},... | collective-permute-start | bytes 110600 | tf_op jit(solution)/shard_map/ppermute | solution.py:368
  27.0 0.0 collective-permute-done.6.got1
  27.0 0.7 %collective-permute-done.7.got2 = f32[2,4608]{1,0:T(2,128)S(1)} collective-permute-done((f32[2,4608]{1,0:T(2,128)S(1)}, f32[2,4608]{1,0:T(2,128)S(1)}, u32[]{:S(2)}, u32[]{:S(2)}) %collective-permute-start.7) | collective-permute-done | bytes 36896 | tf_op jit(solution)/shard_map/ppermute | solution.py:368
  27.7 2.8 %collective-permute-done.8.got3 = f32[2,4608]{1,0:T(2,128)S(1)} collective-permute-done((f32[2,4608]{1,0:T(2,128)S(1)}, f32[2,4608]{1,0:T(2,128)S(1)}, u32[]{:S(2)}, u32[]{:S(2)}) %collective-permute-start.8) | collective-permute-done | bytes 36896 | tf_op jit(solution)/shard_map/ppermute | solution.py:368
  30.5 0.0 copy-done.2
  30.5 0.0 copy-done.3
  30.5 3.1 %shard_map.70 = (f32[1,128]{1,0:T(1,128)S(1)}, bf16[1,3584]{1,0:T(2,128)(2,1)}, bf16[304,3584]{1,0:T(8,128)(2,1)}) custom-call(s32[16]{0:T(128)S(1)} %copy-done.3, f32[2,3584]{1,0:T(2,128)S(1)} %get-tuple-element.25.part, f32[16,128]{1,0:T(8,128)S(1)} %get-tuple-element.26.stats, f32[2,4608]{1,0:T(2,128)S(1)} %collective-permute-done.6.got1, ...), custom_call_target="tpu_custom_call" | custom-call | tf_op jit(solution)/shard_map/pallas_call | solution.py:330
  33.6 0.5 %slice_bitcast_fusion = f32[16]{0:T(128)} fusion(f32[1,128]{1,0:T(1,128)S(1)} %get-tuple-element.32), kind=kLoop, calls=%fused_computation.2 | loop fusion | bytes 128 | tf_op jit(solution)/shard_map/squeeze | solution.py:383
Async XLA Ops:
  0.6 29.8 %copy-start.2 = (bf16[4,3584]{1,0:T(4,128)(2,1)S(1)}, bf16[4,3584]{1,0:T(4,128)(2,1)}, u32[]{:S(2)}) copy-start(bf16[4,3584]{1,0:T(4,128)(2,1)} %h0.3) | copy-start | bytes 86020
  0.6 29.8 %copy-start.3 = (s32[16]{0:T(128)S(1)}, s32[16]{0:T(128)}, u32[]{:S(2)}) copy-start(s32[16]{0:T(128)} %mask.1) | copy-start | bytes 196
  0.7 7.8 %collective-permute-start.2 = (bf16[4,3584]{1,0:T(4,128)(2,1)}, bf16[4,3584]{1,0:T(4,128)(2,1)S(1)}, u32[]{:S(2)}, u32[]{:S(2)}) collective-permute-start(bf16[4,3584]{1,0:T(4,128)(2,1)} %h0.3), channel_id=1, source_target_pairs={{0,12},{4,8},{8,4},{12,0},{1,13},{5,9},{9,5},{13,1},{2,14},{6,10},... | collective-permute-start | bytes 86024 | tf_op jit(solution)/shard_map/ppermute | solution.py:344
  5.8 5.0 %collective-permute-start.1 = (bf16[4,3584]{1,0:T(4,128)(2,1)}, bf16[4,3584]{1,0:T(4,128)(2,1)S(1)}, u32[]{:S(2)}, u32[]{:S(2)}) collective-permute-start(bf16[4,3584]{1,0:T(4,128)(2,1)} %h0.3), channel_id=1, source_target_pairs={{0,8},{4,12},{8,0},{12,4},{1,9},{5,13},{9,1},{13,5},{2,10},{6,14},... | collective-permute-start | bytes 86024 | tf_op jit(solution)/shard_map/ppermute | solution.py:344
  5.8 5.0 %collective-permute-start = (bf16[4,3584]{1,0:T(4,128)(2,1)}, bf16[4,3584]{1,0:T(4,128)(2,1)S(1)}, u32[]{:S(2)}, u32[]{:S(2)}) collective-permute-start(bf16[4,3584]{1,0:T(4,128)(2,1)} %h0.3), channel_id=1, source_target_pairs={{0,4},{4,0},{8,12},{12,8},{1,5},{5,1},{9,13},{13,9},{2,6},{6,2},{1... | collective-permute-start | bytes 86024 | tf_op jit(solution)/shard_map/ppermute | solution.py:344
  7.3 1.2 %collective-permute-start.3 = (f32[8,304]{1,0:T(8,128)S(1)}, f32[8,304]{1,0:T(8,128)S(1)}, u32[]{:S(2)}, u32[]{:S(2)}) collective-permute-start(f32[8,304]{1,0:T(8,128)S(1)} %get-tuple-element.35), channel_id=1, source_target_pairs={{0,1},{1,0},{2,3},{3,2},{4,5},{5,4},{6,7},{7,6},{8,9},{9,8},{10,11... | collective-permute-start | bytes 29192 | tf_op jit(solution)/shard_map/ppermute | solution.py:346
  10.8 1.6 %copy-start = (bf16[304,3584]{1,0:T(8,128)(2,1)S(1)}, bf16[304,3584]{1,0:T(8,128)(2,1)}, u32[]{:S(2)}) copy-start(bf16[304,3584]{1,0:T(8,128)(2,1)} %w.1) | copy-start | bytes 6537220
  12.4 0.7 %copy-start.1 = (bf16[4,3584]{1,0:T(4,128)(2,1)S(1)}, bf16[4,3584]{1,0:T(4,128)(2,1)}, u32[]{:S(2)}) copy-start(bf16[4,3584]{1,0:T(4,128)(2,1)} %h0.3) | copy-start | bytes 86020
  15.2 1.5 %collective-permute-start.4 = (f32[16,3712]{1,0:T(8,128)S(1)}, f32[16,3712]{1,0:T(8,128)S(1)}, u32[]{:S(2)}, u32[]{:S(2)}) collective-permute-start(f32[16,3712]{1,0:T(8,128)S(1)} %get-tuple-element.21), channel_id=1, source_target_pairs={{0,1},{1,0},{2,3},{3,2},{4,5},{5,4},{6,7},{7,6},{8,9},{9,8},{10,11... | collective-permute-start | bytes 712712 | tf_op jit(solution)/shard_map/ppermute | solution.py:358
  16.9 5.4 %collective-permute-start.5 = (f32[8,3840]{1,0:T(8,128)S(1)}, f32[8,3840]{1,0:T(8,128)S(1)}, u32[]{:S(2)}, u32[]{:S(2)}) collective-permute-start(f32[8,3840]{1,0:T(8,128)S(1)} %get-tuple-element.24), channel_id=1, source_target_pairs={{0,2},{2,0},{1,3},{3,1},{4,6},{6,4},{5,7},{7,5},{8,10},{10,8},{9,1... | collective-permute-start | bytes 368648 | tf_op jit(solution)/shard_map/ppermute | solution.py:362
  22.5 4.5 %collective-permute-start.6 = (f32[2,4608]{1,0:T(2,128)S(1)}, f32[2,4608]{1,0:T(2,128)S(1)}, u32[]{:S(2)}, u32[]{:S(2)}) collective-permute-start(f32[2,4608]{1,0:T(2,128)S(1)} %get-tuple-element.27), channel_id=1, source_target_pairs={{0,4},{4,0},{8,12},{12,8},{1,5},{5,1},{9,13},{13,9},{2,6},{6,2},{1... | collective-permute-start | bytes 110600 | tf_op jit(solution)/shard_map/ppermute | solution.py:368
  22.6 5.0 %collective-permute-start.7 = (f32[2,4608]{1,0:T(2,128)S(1)}, f32[2,4608]{1,0:T(2,128)S(1)}, u32[]{:S(2)}, u32[]{:S(2)}) collective-permute-start(f32[2,4608]{1,0:T(2,128)S(1)} %get-tuple-element.28), channel_id=1, source_target_pairs={{0,8},{4,12},{8,0},{12,4},{1,9},{5,13},{9,1},{13,5},{2,10},{6,14},... | collective-permute-start | bytes 110600 | tf_op jit(solution)/shard_map/ppermute | solution.py:368
  24.7 5.8 %collective-permute-start.8 = (f32[2,4608]{1,0:T(2,128)S(1)}, f32[2,4608]{1,0:T(2,128)S(1)}, u32[]{:S(2)}, u32[]{:S(2)}) collective-permute-start(f32[2,4608]{1,0:T(2,128)S(1)} %get-tuple-element.29), channel_id=1, source_target_pairs={{0,12},{4,8},{8,4},{12,0},{1,13},{5,9},{9,5},{13,1},{2,14},{6,10},... | collective-permute-start | bytes 110600 | tf_op jit(solution)/shard_map/ppermute | solution.py:368

commit v3 on v2

--- a/solution.py
+++ b/solution.py
@@ -168,7 +168,7 @@
     ls = sum(s[:, 2:3] * f[:, 0:1] for s, f in zip(parts, factors))
     lt = sum(s[:, 3:4] * f[:, 1:2] for s, f in zip(parts, factors))
     cross = sum(s[:, 4:5] * f[:, 1:2] for s, f in zip(parts, factors))
-    return factors, [top[:, 0:1], top[:, 1:2], ls, lt, cross]
+    return factors, [top[:, 0:1], top[:, 1:2], ls, lt, cross, top[:, 5:6]]
 
 
 def places():
@@ -179,33 +179,60 @@
     return 2 * (x ^ (b & 1)) + (c ^ (b >> 1))
 
 
-def first_kernel(h0, h1, h2, h3, w, own_t, got_t, student, scaled, stats, keep, send, hf, raw, tt, e):
+def teacher_kernel(mask_in, own_in, got, h, scaled, et, stats, h_out, tt, mask, own, sems):
+    copies = [
+        pltpu.make_async_copy(a, b, sems.at[i])
+        for i, (a, b) in enumerate(((own_in, own), (mask_in, mask), (h, h_out)))
+    ]
+    for copy in copies:
+        copy.start()
+    z, x, c = places()
+    v = scaled.shape[1]
+    copies[0].wait()
+    copies[1].wait()
+    for i, tile in ((c, own[...]), (1 - c, got[...])):
+        tt[pl.ds(pl.multiple_of(8 * i, 8), 8), :] = 0.5 * jnp.where(c == 0, tile[:, 0:v], tile[:, v : 2 * v])
+    row = lax.broadcasted_iota(jnp.int32, (ROWS, 1), 0)
+    valid = jnp.zeros((ROWS, 1), jnp.float32)
+    for r in range(ROWS):
+        at = 4 * ((r & 3) ^ z) + row_of(r >> 2, x, c)
+        scaled[r : r + 1, :] = tt[pl.ds(at, 1), :]
+        valid = jnp.where(row == r, mask[at].astype(jnp.float32), valid)
+    t = scaled[...]
+    mt = jnp.max(t, axis=1, keepdims=True)
+    e = jnp.exp(t - mt)
+    et[...] = e
+    none = jnp.zeros_like(mt)
+    stats[...] = pack([none, mt, none, jnp.sum(e, axis=1, keepdims=True), none, valid])
+    copies[2].wait()
+
+
+def first_kernel(h0, h1, h2, h3, w, scaled, et_in, teacher, student, stats, hb, keep, send, hf, raw, e):
     z, x, c = places()
     for k, h in enumerate((h0, h1, h2, h3)):
         hf[4 * k : 4 * k + 4, :] = h[...].astype(jnp.float32)
+    rows = hf[...].astype(jnp.bfloat16)
+    hb[...] = rows
     raw[...] = 0.5 * lax.dot_general(
-        hf[...].astype(jnp.bfloat16), w[...], (((1,), (1,)), ((), ())), preferred_element_type=jnp.float32
+        rows, w[...], (((1,), (1,)), ((), ())), preferred_element_type=jnp.float32
     )
-    tt[pl.ds(8 * c, 8), :] = own_t[...]
-    tt[pl.ds(8 * (1 - c), 8), :] = got_t[...]
     for b in range(4):
         j = row_of(b, x, c)
         for k in range(4):
             student[4 * b + k : 4 * b + k + 1, :] = raw[pl.ds(4 * k + j, 1), :]
-            scaled[4 * b + k : 4 * b + k + 1, :] = 0.5 * tt[pl.ds(4 * (k ^ z) + j, 1), :]
     s = student[...]
     t = scaled[...]
+    et = et_in[...]
     ms = jnp.max(s, axis=1, keepdims=True)
-    mt = jnp.max(t, axis=1, keepdims=True)
     es = jnp.exp(s - ms)
-    et = jnp.exp(t - mt)
     st = pack(
         [
             ms,
-            mt,
+            teacher[:, 1:2],
             jnp.sum(es, axis=1, keepdims=True),
-            jnp.sum(et, axis=1, keepdims=True),
+            teacher[:, 3:4],
             jnp.sum(et * (t - s), axis=1, keepdims=True),
+            teacher[:, 5:6],
         ]
     )
     stats[...] = st
@@ -261,8 +288,8 @@
 
 def make_last_kernel(chunk):
     def last_kernel(
-        mask, part, stats, got1, got2, got3, student, scaled, h0, h1, h2, h3,
-        divergence, hidden_grad, weight_grad, gs, hf, gr, out, sems,
+        part, stats, got1, got2, got3, student, scaled, hb,
+        divergence, hidden_grad, weight_grad, gs, gr, out, sems,
     ):
         z, x, c = places()
         d = part.shape[1]
@@ -271,41 +298,30 @@
             for i in range(8):
                 gs[k, 2 * i : 2 * i + 2, :] = got[:, d + 128 * i : d + 128 * i + 128]
             parts.append(gs[k])
-        factors, (ms, mt, ls, lt, cross) = unite(parts)
+        factors, (ms, mt, ls, lt, cross, valid) = unite(parts)
         lse_s = ms + jnp.log(ls)
         lse_t = mt + jnp.log(lt)
-        row = lax.broadcasted_iota(jnp.int32, (ROWS, 1), 0)
-        valid = jnp.zeros((ROWS, 1), jnp.float32)
-        for r in range(ROWS):
-            b, k = r // 4, r % 4
-            valid = jnp.where(
-                row == r, mask[4 * (k ^ z) + row_of(b, x, c)].astype(jnp.float32), valid
-            )
         gain = valid * (objective_scale * smoothing_divisor)
         grad = gain * (jnp.exp(student[...] - lse_s) - jnp.exp(scaled[...] - lse_t))
         for b in range(4):
             j = row_of(b, x, c)
             for k in range(4):
                 gr[pl.ds(4 * k + j, 1), :] = grad[4 * b + k : 4 * b + k + 1, :]
-        for k, h in enumerate((h0, h1, h2, h3)):
-            hf[4 * k : 4 * k + 4, :] = h[...].astype(jnp.float32)
         g = gr[...].astype(jnp.bfloat16)
         copies = []
         for i in range(d // chunk):
             at = pl.ds(i * chunk, chunk)
             out[:, at] = lax.dot_general(
-                g,
-                hf[:, at].astype(jnp.bfloat16),
-                (((0,), (0,)), ((), ())),
-                preferred_element_type=jnp.float32,
+                g, hb[:, at], (((0,), (0,)), ((), ())), preferred_element_type=jnp.float32
             ).astype(jnp.bfloat16)
             copy = pltpu.make_async_copy(out.at[:, at], weight_grad.at[:, at], sems.at[i])
             copy.start()
             copies.append(copy)
+        row = lax.broadcasted_iota(jnp.int32, (ROWS, 1), 0)
         home = 4 * (z ^ (row & 3)) + 2 * (x ^ ((row >> 2) & 1)) + (c ^ (row >> 3))
         value = valid * (cross / lt - lse_t + lse_s)
         lane = lax.broadcasted_iota(jnp.int32, (ROWS, STATS), 1)
-        divergence[...] = jnp.sum(jnp.where(lane == home, value, 0.0), axis=0, keepdims=True)
+        divergence[...] = jnp.sum(jnp.where(lane == home, value, 0.0), axis=0)[0:ROWS]
         a_s = part[0:1, :] * factors[0][0:1, 0:1]
         a_t = part[1:2, :] * factors[0][0:1, 1:2]
         for got, f in zip((got1, got2, got3), factors[1:]):
@@ -321,11 +337,11 @@
 
 
 VMEM = pl.BlockSpec(memory_space=pltpu.VMEM)
-SMEM = pl.BlockSpec(memory_space=pltpu.SMEM)
+ANY = pl.BlockSpec(memory_space=pl.ANY)
 PARAMS = pltpu.CompilerParams(vmem_limit_bytes=32 << 20)
 
 
-def call(kernel, out, scratch=(), in_specs=None, out_specs=None):
+def call(kernel, out, scratch=(), in_specs=None, out_specs=None, cost=None):
     shapes = [jax.ShapeDtypeStruct(s, t) for s, t in out]
     return lambda *a: pl.pallas_call(
         kernel,
@@ -334,27 +350,35 @@
         out_specs=out_specs or [VMEM] * len(out),
         scratch_shapes=list(scratch),
         compiler_params=PARAMS,
+        cost_estimate=cost,
     )(*a)
 
 
 def small_body(hidden_rows, mentor, head_weight, row_mask):
     f32, bf16 = jnp.float32, jnp.bfloat16
     v, d = head_weight.shape
-    c = lax.axis_index("teach")
-    pieces = [hidden_rows] + [lax.ppermute(hidden_rows, "vocab", flip(4, k)) for k in (1, 2, 3)]
-    left, right = mentor[:, :v], mentor[:, v:]
-    got_t = lax.ppermute(jnp.where(c == 0, right, left), "teach", flip(2, 1))
-    own_t = jnp.where(c == 0, left, right)
-    student, scaled, stats, keep, send = call(
+    pieces = [lax.ppermute(hidden_rows, "vocab", flip(4, k)) for k in (1, 2, 3)]
+    scaled, et, teacher, own = call(
+        teacher_kernel,
+        [((ROWS, v), f32), ((ROWS, v), f32), ((ROWS, STATS), f32), ((4, d), bf16)],
+        [
+            pltpu.VMEM((ROWS, v), f32),
+            pltpu.SMEM((ROWS,), jnp.int32),
+            pltpu.VMEM((ROWS // 2, 2 * v), f32),
+            pltpu.SemaphoreType.DMA((3,)),
+        ],
+        [ANY, ANY, VMEM, ANY],
+        cost=pl.CostEstimate(flops=2_000_000_000, transcendentals=ROWS * v, bytes_accessed=2 << 20),
+    )(row_mask, mentor, lax.ppermute(mentor, "teach", flip(2, 1)), hidden_rows)
+    student, stats, hb, keep, send = call(
         first_kernel,
-        [((ROWS, v), f32), ((ROWS, v), f32), ((ROWS, STATS), f32), ((16, d), f32), ((16, d + STATS), f32)],
+        [((ROWS, v), f32), ((ROWS, STATS), f32), ((ROWS, d), bf16), ((16, d), f32), ((16, d + STATS), f32)],
         [
             pltpu.VMEM((ROWS, d), f32),
             pltpu.VMEM((ROWS, v), f32),
-            pltpu.VMEM((ROWS, v), f32),
             pltpu.VMEM((2 * ROWS, v), f32),
         ],
-    )(*pieces, head_weight, own_t, got_t)
+    )(own, *pieces, head_weight, scaled, et, teacher)
     got = lax.ppermute(send, "teach", flip(2, 1))
     stats, keep, send = call(
         second_kernel, [((ROWS, STATS), f32), ((8, d), f32), ((8, d + 2 * STATS), f32)]
@@ -367,20 +391,20 @@
     )(keep, stats, got)
     gots = [lax.ppermute(a, "vocab", flip(4, k)) for k, a in enumerate(sends, 1)]
     chunk = 512
-    divergence, hidden_grad, weight_grad = call(
-        make_last_kernel(chunk),
-        [((1, STATS), f32), ((1, d), bf16), ((v, d), bf16)],
-        [
-            pltpu.VMEM((3, ROWS, STATS), f32),
-            pltpu.VMEM((ROWS, d), f32),
-            pltpu.VMEM((ROWS, v), f32),
-            pltpu.VMEM((v, d), bf16),
-            pltpu.SemaphoreType.DMA((d // chunk,)),
-        ],
-        [SMEM] + [VMEM] * 11,
-        [VMEM, VMEM, pl.BlockSpec(memory_space=pl.ANY)],
-    )(row_mask, keep, stats, *gots, student, scaled, *pieces)
-    return divergence[0, :ROWS], hidden_grad, weight_grad
+    return tuple(
+        call(
+            make_last_kernel(chunk),
+            [((ROWS,), f32), ((1, d), bf16), ((v, d), bf16)],
+            [
+                pltpu.VMEM((3, ROWS, STATS), f32),
+                pltpu.VMEM((ROWS, v), f32),
+                pltpu.VMEM((v, d), bf16),
+                pltpu.SemaphoreType.DMA((d // chunk,)),
+            ],
+            [VMEM] * 8,
+            [VMEM, VMEM, ANY],
+        )(keep, stats, *gots, student, scaled, hb)
+    )
 
 
 def solution(mesh):

time: 34.3 us -> 31.8 us (0.927)
  waiting for transfers between devices: 12.3 us -> 11.1 us
  other arithmetic: 0.85 us -> 0 us
  local copies, waits for them, and re-layouts: 2.89 us -> 2.16 us
    ppermute x4, waiting for transfers between devices: 3.48 us -> 2.16 us  [the longest x3 2.16 us: small_body(): pieces = [lax.ppermute(hidden_rows, 'vocab', flip(4, k)) for k in (1, 2, 3)]]
    select_n x1 -> x0, other arithmetic: 0.85 us -> none  [small_body(): got_t = lax.ppermute(jnp.where(c == 0, right, left), 'teach', flip(2, 1))]
    squeeze x1 -> x0, local copies, waits for them, and re-layouts: 0.51 us -> none  [small_body(): return (divergence[0, :ROWS], hidden_grad, weight_grad)]
    pallas_call x4 -> x5, Pallas kernels: 5.53 us -> 5.81 us  [call(): pl.pallas_call(kernel, out_shape=shapes, in_specs=in_specs or [VMEM] * le...]
  transfers between devices with their start and end apart: 9 -> 9, of which waited for: 6 -> 6; matrix products, arithmetic and copies ran while one was open for 3% -> 0% of each run, Pallas kernels for 0% -> 3%
where the time goes in v3:
time: 31.8 us; the launch traced here: 31.6 us
  starting transfers between devices  11.8 us (37%)
  waiting for transfers between devices  11.1 us (35%)
  Pallas kernels  5.81 us (18%)
  local copies, waits for them, and re-layouts  2.16 us (7%)
  between operations  0.69 us (2%)
    pallas_call x5, Pallas kernels, call(): pl.pallas_call(kernel, out_shape=shapes, in_specs=in_specs or [VMEM] * le...  5.81 us
    ppermute x3, starting transfers between devices, small_body(): pieces = [lax.ppermute(hidden_rows, 'vocab', flip(4, k)) for k in (1, 2, 3)]  5.24 us
    ppermute x3, starting transfers between devices, small_body(): lax.ppermute(a, 'vocab', flip(4, k))  4.45 us
    ppermute x1, waiting for transfers between devices, small_body(): got = lax.ppermute(send, 'rows', flip(2, 1))  3.87 us
    ppermute x3, waiting for transfers between devices, small_body(): lax.ppermute(a, 'vocab', flip(4, k))  3.56 us
    unnamed x8, local copies, waits for them, and re-layouts  2.16 us
    ppermute x3, waiting for transfers between devices, small_body(): pieces = [lax.ppermute(hidden_rows, 'vocab', flip(4, k)) for k in (1, 2, 3)]  2.16 us
    ppermute x1, starting transfers between devices, small_body(): got = lax.ppermute(send, 'rows', flip(2, 1))  1.56 us
  transfers between devices with their start and end apart: 9, of which 6 were waited for; matrix products, arithmetic and copies ran while one was open for 0% of the time, Pallas kernels for 3%

profile of v3, /device:TPU:0, one launch (start us, length us, event | category | flops | bytes accessed | tf_op | source)
XLA Modules:
  0.0 31.6 jit_solution(15728141113937280129)
XLA Ops:
  0.6 0.0 copy-start
  0.6 0.5 %collective-permute-start = (f32[8,608]{1,0:T(8,128)}, f32[8,608]{1,0:T(8,128)S(1)}, u32[]{:S(2)}, u32[]{:S(2)}) collective-permute-start(f32[8,608]{1,0:T(8,128)} %own_in.1), channel_id=1, source_target_pairs={{0,1},{1,0},{2,3},{3,2},{4,5},{5,4},{6,7},{7,6},{8,9},{9,8},{10,11... | collective-permute-start | bytes 58376 | tf_op jit(solution)/shard_map/ppermute | solution.py:372
  1.2 2.6 %collective-permute-start.1 = (bf16[4,3584]{1,0:T(4,128)(2,1)}, bf16[4,3584]{1,0:T(4,128)(2,1)S(1)}, u32[]{:S(2)}, u32[]{:S(2)}) collective-permute-start(bf16[4,3584]{1,0:T(4,128)(2,1)} %h.1), channel_id=1, source_target_pairs={{0,4},{4,0},{8,12},{12,8},{1,5},{5,1},{9,13},{13,9},{2,6},{6,2},{1... | collective-permute-start | bytes 86024 | tf_op jit(solution)/shard_map/ppermute | solution.py:360
  3.8 2.5 %collective-permute-start.3 = (bf16[4,3584]{1,0:T(4,128)(2,1)}, bf16[4,3584]{1,0:T(4,128)(2,1)S(1)}, u32[]{:S(2)}, u32[]{:S(2)}) collective-permute-start(bf16[4,3584]{1,0:T(4,128)(2,1)} %h.1), channel_id=1, source_target_pairs={{0,12},{4,8},{8,4},{12,0},{1,13},{5,9},{9,5},{13,1},{2,14},{6,10},... | collective-permute-start | bytes 86024 | tf_op jit(solution)/shard_map/ppermute | solution.py:360
  6.3 0.1 collective-permute-start.2
  6.4 0.0 collective-permute-done.got
  6.4 0.0 copy-start.1
  6.4 0.8 %copy-done.1 = bf16[4,3584]{1,0:T(4,128)(2,1)S(1)} copy-done((bf16[4,3584]{1,0:T(4,128)(2,1)S(1)}, bf16[4,3584]{1,0:T(4,128)(2,1)}, u32[]{:S(2)}) %copy-start.1) | copy-done | bytes 28696
  7.2 0.0 copy-start.2
  7.2 0.7 %copy-done.2 = f32[8,608]{1,0:T(8,128)S(1)} copy-done((f32[8,608]{1,0:T(8,128)S(1)}, f32[8,608]{1,0:T(8,128)}, u32[]{:S(2)}) %copy-start.2) | copy-done | bytes 19480
  7.9 0.0 copy-start.3
  7.9 0.7 %copy-done.3 = s32[16]{0:T(128)S(1)} copy-done((s32[16]{0:T(128)S(1)}, s32[16]{0:T(128)}, u32[]{:S(2)}) %copy-start.3) | copy-done | bytes 88
  8.6 0.8 %shard_map.67 = (f32[16,304]{1,0:T(8,128)S(1)}, f32[16,304]{1,0:T(8,128)S(1)}, f32[16,128]{1,0:T(8,128)S(1)}, bf16[4,3584]{1,0:T(4,128)(2,1)S(1)}) custom-call(s32[16]{0:T(128)S(1)} %copy-done.3, f32[8,608]{1,0:T(8,128)S(1)} %copy-done.2, f32[8,608]{1,0:T(8,128)S(1)} %collective-permute-done.got, bf16[4,3584]{1,0:T(4,128)(2,1)S(1)} %copy-done.1), custom_call_target="tpu_custom_call" | custom-call | flops 2000000000 | bytes 2097152 | tf_op jit(solution)/shard_map/pallas_call | solution.py:346
  9.4 0.0 collective-permute-done.1.h1
  9.4 0.3 collective-permute-done.3.h3
  9.7 1.9 %collective-permute-done.2.h2 = bf16[4,3584]{1,0:T(4,128)(2,1)S(1)} collective-permute-done((bf16[4,3584]{1,0:T(4,128)(2,1)}, bf16[4,3584]{1,0:T(4,128)(2,1)S(1)}, u32[]{:S(2)}, u32[]{:S(2)}) %collective-permute-start.2) | collective-permute-done | bytes 28704 | tf_op jit(solution)/shard_map/ppermute | solution.py:360
  11.6 0.0 copy-done
  11.6 2.1 %shard_map.68 = (f32[16,304]{1,0:T(8,128)S(1)}, f32[16,128]{1,0:T(8,128)S(1)}, bf16[16,3584]{1,0:T(8,128)(2,1)S(1)}, f32[16,3584]{1,0:T(8,128)S(1)}, f32[16,3712]{1,0:T(8,128)S(1)}) custom-call(bf16[4,3584]{1,0:T(4,128)(2,1)S(1)} %get-tuple-element.20.h0, bf16[4,3584]{1,0:T(4,128)(2,1)S(1)} %collective-permute-done.1.h1, ...), custom_call_target="tpu_custom_call" | custom-call | tf_op jit(solution)/shard_map/pallas_call | solution.py:346
  13.6 0.0 collective-permute-start.4
  13.7 1.5 %collective-permute-done.4.got = f32[16,3712]{1,0:T(8,128)S(1)} collective-permute-done((f32[16,3712]{1,0:T(8,128)S(1)}, f32[16,3712]{1,0:T(8,128)S(1)}, u32[]{:S(2)}, u32[]{:S(2)}) %collective-permute-start.4) | collective-permute-done | bytes 237600 | tf_op jit(solution)/shard_map/ppermute | solution.py:382
  15.2 0.2 shard_map.69
  15.4 1.6 %collective-permute-start.5 = (f32[8,3840]{1,0:T(8,128)S(1)}, f32[8,3840]{1,0:T(8,128)S(1)}, u32[]{:S(2)}, u32[]{:S(2)}) collective-permute-start(f32[8,3840]{1,0:T(8,128)S(1)} %get-tuple-element.29), channel_id=1, source_target_pairs={{0,2},{2,0},{1,3},{3,1},{4,6},{6,4},{5,7},{7,5},{8,10},{10,8},{9,1... | collective-permute-start | bytes 368648 | tf_op jit(solution)/shard_map/ppermute | solution.py:386
  16.9 3.9 %collective-permute-done.5.got = f32[8,3840]{1,0:T(8,128)S(1)} collective-permute-done((f32[8,3840]{1,0:T(8,128)S(1)}, f32[8,3840]{1,0:T(8,128)S(1)}, u32[]{:S(2)}, u32[]{:S(2)}) %collective-permute-start.5) | collective-permute-done | bytes 122912 | tf_op jit(solution)/shard_map/ppermute | solution.py:386
  20.8 0.2 shard_map.70
  21.0 0.5 %collective-permute-start.6 = (f32[2,4608]{1,0:T(2,128)S(1)}, f32[2,4608]{1,0:T(2,128)S(1)}, u32[]{:S(2)}, u32[]{:S(2)}) collective-permute-start(f32[2,4608]{1,0:T(2,128)S(1)} %get-tuple-element.32), channel_id=1, source_target_pairs={{0,4},{4,0},{8,12},{12,8},{1,5},{5,1},{9,13},{13,9},{2,6},{6,2},{1... | collective-permute-start | bytes 110600 | tf_op jit(solution)/shard_map/ppermute | solution.py:392
  21.5 1.7 %collective-permute-start.7 = (f32[2,4608]{1,0:T(2,128)S(1)}, f32[2,4608]{1,0:T(2,128)S(1)}, u32[]{:S(2)}, u32[]{:S(2)}) collective-permute-start(f32[2,4608]{1,0:T(2,128)S(1)} %get-tuple-element.33), channel_id=1, source_target_pairs={{0,8},{4,12},{8,0},{12,4},{1,9},{5,13},{9,1},{13,5},{2,10},{6,14},... | collective-permute-start | bytes 110600 | tf_op jit(solution)/shard_map/ppermute | solution.py:392
  23.3 2.2 %collective-permute-start.8 = (f32[2,4608]{1,0:T(2,128)S(1)}, f32[2,4608]{1,0:T(2,128)S(1)}, u32[]{:S(2)}, u32[]{:S(2)}) collective-permute-start(f32[2,4608]{1,0:T(2,128)S(1)} %get-tuple-element.34), channel_id=1, source_target_pairs={{0,12},{4,8},{8,4},{12,0},{1,13},{5,9},{9,5},{13,1},{2,14},{6,10},... | collective-permute-start | bytes 110600 | tf_op jit(solution)/shard_map/ppermute | solution.py:392
  25.5 0.0 collective-permute-done.6.got1
  25.5 0.9 %collective-permute-done.7.got2 = f32[2,4608]{1,0:T(2,128)S(1)} collective-permute-done((f32[2,4608]{1,0:T(2,128)S(1)}, f32[2,4608]{1,0:T(2,128)S(1)}, u32[]{:S(2)}, u32[]{:S(2)}) %collective-permute-start.7) | collective-permute-done | bytes 36896 | tf_op jit(solution)/shard_map/ppermute | solution.py:392
  26.4 2.6 %collective-permute-done.8.got3 = f32[2,4608]{1,0:T(2,128)S(1)} collective-permute-done((f32[2,4608]{1,0:T(2,128)S(1)}, f32[2,4608]{1,0:T(2,128)S(1)}, u32[]{:S(2)}, u32[]{:S(2)}) %collective-permute-start.8) | collective-permute-done | bytes 36896 | tf_op jit(solution)/shard_map/ppermute | solution.py:392
  29.0 2.5 %shard_map.71 = (f32[16]{0:T(128)}, bf16[1,3584]{1,0:T(2,128)(2,1)}, bf16[304,3584]{1,0:T(8,128)(2,1)}) custom-call(f32[2,3584]{1,0:T(2,128)S(1)} %get-tuple-element.30.part, f32[16,128]{1,0:T(8,128)S(1)} %get-tuple-element.31.stats, f32[2,4608]{1,0:T(2,128)S(1)} %collective-permute-done.6.got1, f32[2,4608]{1,0:T(2,128)S(1)} %collective-permute-done.7.got2, ...), custom_call_target="tpu_custom_call" | custom-call | tf_op jit(solution)/shard_map/pallas_call | solution.py:346
Async XLA Ops:
  0.6 10.9 %copy-start = (bf16[304,3584]{1,0:T(8,128)(2,1)S(1)}, bf16[304,3584]{1,0:T(8,128)(2,1)}, u32[]{:S(2)}) copy-start(bf16[304,3584]{1,0:T(8,128)(2,1)} %w.1) | copy-start | bytes 6537220
  0.6 5.8 %collective-permute-start = (f32[8,608]{1,0:T(8,128)}, f32[8,608]{1,0:T(8,128)S(1)}, u32[]{:S(2)}, u32[]{:S(2)}) collective-permute-start(f32[8,608]{1,0:T(8,128)} %own_in.1), channel_id=1, source_target_pairs={{0,1},{1,0},{2,3},{3,2},{4,5},{5,4},{6,7},{7,6},{8,9},{9,8},{10,11... | collective-permute-start | bytes 58376 | tf_op jit(solution)/shard_map/ppermute | solution.py:372
  1.2 8.3 %collective-permute-start.1 = (bf16[4,3584]{1,0:T(4,128)(2,1)}, bf16[4,3584]{1,0:T(4,128)(2,1)S(1)}, u32[]{:S(2)}, u32[]{:S(2)}) collective-permute-start(bf16[4,3584]{1,0:T(4,128)(2,1)} %h.1), channel_id=1, source_target_pairs={{0,4},{4,0},{8,12},{12,8},{1,5},{5,1},{9,13},{13,9},{2,6},{6,2},{1... | collective-permute-start | bytes 86024 | tf_op jit(solution)/shard_map/ppermute | solution.py:360
  3.8 5.9 %collective-permute-start.3 = (bf16[4,3584]{1,0:T(4,128)(2,1)}, bf16[4,3584]{1,0:T(4,128)(2,1)S(1)}, u32[]{:S(2)}, u32[]{:S(2)}) collective-permute-start(bf16[4,3584]{1,0:T(4,128)(2,1)} %h.1), channel_id=1, source_target_pairs={{0,12},{4,8},{8,4},{12,0},{1,13},{5,9},{9,5},{13,1},{2,14},{6,10},... | collective-permute-start | bytes 86024 | tf_op jit(solution)/shard_map/ppermute | solution.py:360
  6.3 5.3 %collective-permute-start.2 = (bf16[4,3584]{1,0:T(4,128)(2,1)}, bf16[4,3584]{1,0:T(4,128)(2,1)S(1)}, u32[]{:S(2)}, u32[]{:S(2)}) collective-permute-start(bf16[4,3584]{1,0:T(4,128)(2,1)} %h.1), channel_id=1, source_target_pairs={{0,8},{4,12},{8,0},{12,4},{1,9},{5,13},{9,1},{13,5},{2,10},{6,14},... | collective-permute-start | bytes 86024 | tf_op jit(solution)/shard_map/ppermute | solution.py:360
  6.4 0.8 %copy-start.1 = (bf16[4,3584]{1,0:T(4,128)(2,1)S(1)}, bf16[4,3584]{1,0:T(4,128)(2,1)}, u32[]{:S(2)}) copy-start(bf16[4,3584]{1,0:T(4,128)(2,1)} %h.1) | copy-start | bytes 86020
  7.2 0.7 %copy-start.2 = (f32[8,608]{1,0:T(8,128)S(1)}, f32[8,608]{1,0:T(8,128)}, u32[]{:S(2)}) copy-start(f32[8,608]{1,0:T(8,128)} %own_in.1) | copy-start | bytes 58372
  7.9 0.7 %copy-start.3 = (s32[16]{0:T(128)S(1)}, s32[16]{0:T(128)}, u32[]{:S(2)}) copy-start(s32[16]{0:T(128)} %mask_in.1) | copy-start | bytes 196
  13.6 1.5 %collective-permute-start.4 = (f32[16,3712]{1,0:T(8,128)S(1)}, f32[16,3712]{1,0:T(8,128)S(1)}, u32[]{:S(2)}, u32[]{:S(2)}) collective-permute-start(f32[16,3712]{1,0:T(8,128)S(1)} %get-tuple-element.26), channel_id=1, source_target_pairs={{0,1},{1,0},{2,3},{3,2},{4,5},{5,4},{6,7},{7,6},{8,9},{9,8},{10,11... | collective-permute-start | bytes 712712 | tf_op jit(solution)/shard_map/ppermute | solution.py:382
  15.4 5.4 %collective-permute-start.5 = (f32[8,3840]{1,0:T(8,128)S(1)}, f32[8,3840]{1,0:T(8,128)S(1)}, u32[]{:S(2)}, u32[]{:S(2)}) collective-permute-start(f32[8,3840]{1,0:T(8,128)S(1)} %get-tuple-element.29), channel_id=1, source_target_pairs={{0,2},{2,0},{1,3},{3,1},{4,6},{6,4},{5,7},{7,5},{8,10},{10,8},{9,1... | collective-permute-start | bytes 368648 | tf_op jit(solution)/shard_map/ppermute | solution.py:386
  21.0 4.5 %collective-permute-start.6 = (f32[2,4608]{1,0:T(2,128)S(1)}, f32[2,4608]{1,0:T(2,128)S(1)}, u32[]{:S(2)}, u32[]{:S(2)}) collective-permute-start(f32[2,4608]{1,0:T(2,128)S(1)} %get-tuple-element.32), channel_id=1, source_target_pairs={{0,4},{4,0},{8,12},{12,8},{1,5},{5,1},{9,13},{13,9},{2,6},{6,2},{1... | collective-permute-start | bytes 110600 | tf_op jit(solution)/shard_map/ppermute | solution.py:392
  21.5 4.9 %collective-permute-start.7 = (f32[2,4608]{1,0:T(2,128)S(1)}, f32[2,4608]{1,0:T(2,128)S(1)}, u32[]{:S(2)}, u32[]{:S(2)}) collective-permute-start(f32[2,4608]{1,0:T(2,128)S(1)} %get-tuple-element.33), channel_id=1, source_target_pairs={{0,8},{4,12},{8,0},{12,4},{1,9},{5,13},{9,1},{13,5},{2,10},{6,14},... | collective-permute-start | bytes 110600 | tf_op jit(solution)/shard_map/ppermute | solution.py:392
  23.3 5.8 %collective-permute-start.8 = (f32[2,4608]{1,0:T(2,128)S(1)}, f32[2,4608]{1,0:T(2,128)S(1)}, u32[]{:S(2)}, u32[]{:S(2)}) collective-permute-start(f32[2,4608]{1,0:T(2,128)S(1)} %get-tuple-element.34), channel_id=1, source_target_pairs={{0,12},{4,8},{8,4},{12,0},{1,13},{5,9},{9,5},{13,1},{2,14},{6,10},... | collective-permute-start | bytes 110600 | tf_op jit(solution)/shard_map/ppermute | solution.py:392

commit v4 on v3

--- a/solution.py
+++ b/solution.py
@@ -337,7 +337,7 @@
 
 
 VMEM = pl.BlockSpec(memory_space=pltpu.VMEM)
-ANY = pl.BlockSpec(memory_space=pl.ANY)
+ANY = pl.BlockSpec(memory_space=pltpu.HBM)
 PARAMS = pltpu.CompilerParams(vmem_limit_bytes=32 << 20)
 
 
@@ -369,7 +369,12 @@
         ],
         [ANY, ANY, VMEM, ANY],
         cost=pl.CostEstimate(flops=2_000_000_000, transcendentals=ROWS * v, bytes_accessed=2 << 20),
-    )(row_mask, mentor, lax.ppermute(mentor, "teach", flip(2, 1)), hidden_rows)
+    )(
+        pltpu.with_memory_space_constraint(row_mask, pltpu.HBM),
+        pltpu.with_memory_space_constraint(mentor, pltpu.HBM),
+        lax.ppermute(mentor, "teach", flip(2, 1)),
+        pltpu.with_memory_space_constraint(hidden_rows, pltpu.HBM),
+    )
     student, stats, hb, keep, send = call(
         first_kernel,
         [((ROWS, v), f32), ((ROWS, STATS), f32), ((ROWS, d), bf16), ((16, d), f32), ((16, d + STATS), f32)],

time: 31.8 us -> 31.7 us (level)
  local copies, waits for them, and re-layouts: 2.16 us -> 0.01 us
  waiting for transfers between devices: 11.1 us -> 13 us
    unnamed x8 -> x2, local copies, waits for them, and re-layouts: 2.16 us -> 0.01 us
    ppermute x3, waiting for transfers between devices: 2.16 us -> 4.07 us  [small_body(): pieces = [lax.ppermute(hidden_rows, 'vocab', flip(4, k)) for k in (1, 2, 3)]]
where the time goes in v4:
time: 31.7 us; the launch traced here: 31.6 us
  waiting for transfers between devices  13 us (41%)
  starting transfers between devices  11.8 us (37%)
  Pallas kernels  6.06 us (19%)
  between operations  0.69 us (2%)
    pallas_call x5, Pallas kernels, call(): pl.pallas_call(kernel, out_shape=shapes, in_specs=in_specs or [VMEM] * le...  6.06 us
    ppermute x3, starting transfers between devices, small_body(): pieces = [lax.ppermute(hidden_rows, 'vocab', flip(4, k)) for k in (1, 2, 3)]  5.24 us
    ppermute x3, starting transfers between devices, small_body(): lax.ppermute(a, 'vocab', flip(4, k))  4.45 us
    ppermute x3, waiting for transfers between devices, small_body(): pieces = [lax.ppermute(hidden_rows, 'vocab', flip(4, k)) for k in (1, 2, 3)]  4.07 us
    ppermute x1, waiting for transfers between devices, small_body(): got = lax.ppermute(send, 'rows', flip(2, 1))  3.87 us
    ppermute x3, waiting for transfers between devices, small_body(): lax.ppermute(a, 'vocab', flip(4, k))  3.56 us
    ppermute x1, starting transfers between devices, small_body(): got = lax.ppermute(send, 'rows', flip(2, 1))  1.56 us
    ppermute x1, waiting for transfers between devices, small_body(): got = lax.ppermute(send, 'teach', flip(2, 1))  1.49 us
  transfers between devices with their start and end apart: 9, of which 6 were waited for; matrix products, arithmetic and copies ran while one was open for 0% of the time, Pallas kernels for 3%

profile of v4, /device:TPU:0, one launch (start us, length us, event | category | flops | bytes accessed | tf_op | source)
XLA Modules:
  0.0 31.6 jit_solution(10950161997987875796)
XLA Ops:
  0.6 0.0 copy-start
  0.6 0.5 %collective-permute-start = (f32[8,608]{1,0:T(8,128)}, f32[8,608]{1,0:T(8,128)S(1)}, u32[]{:S(2)}, u32[]{:S(2)}) collective-permute-start(f32[8,608]{1,0:T(8,128)} %own_in.1), channel_id=1, source_target_pairs={{0,1},{1,0},{2,3},{3,2},{4,5},{5,4},{6,7},{7,6},{8,9},{9,8},{10,11... | collective-permute-start | bytes 58376 | tf_op jit(solution)/shard_map/ppermute | solution.py:375
  1.2 2.6 %collective-permute-start.1 = (bf16[4,3584]{1,0:T(4,128)(2,1)}, bf16[4,3584]{1,0:T(4,128)(2,1)S(1)}, u32[]{:S(2)}, u32[]{:S(2)}) collective-permute-start(bf16[4,3584]{1,0:T(4,128)(2,1)} %h.1), channel_id=1, source_target_pairs={{0,4},{4,0},{8,12},{12,8},{1,5},{5,1},{9,13},{13,9},{2,6},{6,2},{1... | collective-permute-start | bytes 86024 | tf_op jit(solution)/shard_map/ppermute | solution.py:360
  3.8 2.5 %collective-permute-start.3 = (bf16[4,3584]{1,0:T(4,128)(2,1)}, bf16[4,3584]{1,0:T(4,128)(2,1)S(1)}, u32[]{:S(2)}, u32[]{:S(2)}) collective-permute-start(bf16[4,3584]{1,0:T(4,128)(2,1)} %h.1), channel_id=1, source_target_pairs={{0,12},{4,8},{8,4},{12,0},{1,13},{5,9},{9,5},{13,1},{2,14},{6,10},... | collective-permute-start | bytes 86024 | tf_op jit(solution)/shard_map/ppermute | solution.py:360
  6.3 0.1 collective-permute-start.2
  6.4 0.0 collective-permute-done.got
  6.4 1.1 %shard_map.67 = (f32[16,304]{1,0:T(8,128)S(1)}, f32[16,304]{1,0:T(8,128)S(1)}, f32[16,128]{1,0:T(8,128)S(1)}, bf16[4,3584]{1,0:T(4,128)(2,1)S(1)}) custom-call(s32[16]{0:T(128)} %mask_in.1, f32[8,608]{1,0:T(8,128)} %own_in.1, f32[8,608]{1,0:T(8,128)S(1)} %collective-permute-done.got, bf16[4,3584]{1,0:T(4,128)(2,1)} %h.1), custom_call_target="tpu_custom_call" | custom-call | flops 2000000000 | bytes 2097152 | tf_op jit(solution)/shard_map/pallas_call | solution.py:346
  7.5 0.0 collective-permute-done.1.h1
  7.5 2.2 %collective-permute-done.3.h3 = bf16[4,3584]{1,0:T(4,128)(2,1)S(1)} collective-permute-done((bf16[4,3584]{1,0:T(4,128)(2,1)}, bf16[4,3584]{1,0:T(4,128)(2,1)S(1)}, u32[]{:S(2)}, u32[]{:S(2)}) %collective-permute-start.3) | collective-permute-done | bytes 28704 | tf_op jit(solution)/shard_map/ppermute | solution.py:360
  9.7 1.9 %collective-permute-done.2.h2 = bf16[4,3584]{1,0:T(4,128)(2,1)S(1)} collective-permute-done((bf16[4,3584]{1,0:T(4,128)(2,1)}, bf16[4,3584]{1,0:T(4,128)(2,1)S(1)}, u32[]{:S(2)}, u32[]{:S(2)}) %collective-permute-start.2) | collective-permute-done | bytes 28704 | tf_op jit(solution)/shard_map/ppermute | solution.py:360
  11.6 0.0 copy-done
  11.6 2.1 %shard_map.68 = (f32[16,304]{1,0:T(8,128)S(1)}, f32[16,128]{1,0:T(8,128)S(1)}, bf16[16,3584]{1,0:T(8,128)(2,1)S(1)}, f32[16,3584]{1,0:T(8,128)S(1)}, f32[16,3712]{1,0:T(8,128)S(1)}) custom-call(bf16[4,3584]{1,0:T(4,128)(2,1)S(1)} %get-tuple-element.20.h0, bf16[4,3584]{1,0:T(4,128)(2,1)S(1)} %collective-permute-done.1.h1, ...), custom_call_target="tpu_custom_call" | custom-call | tf_op jit(solution)/shard_map/pallas_call | solution.py:346
  13.6 0.0 collective-permute-start.4
  13.7 1.5 %collective-permute-done.4.got = f32[16,3712]{1,0:T(8,128)S(1)} collective-permute-done((f32[16,3712]{1,0:T(8,128)S(1)}, f32[16,3712]{1,0:T(8,128)S(1)}, u32[]{:S(2)}, u32[]{:S(2)}) %collective-permute-start.4) | collective-permute-done | bytes 237600 | tf_op jit(solution)/shard_map/ppermute | solution.py:387
  15.2 0.2 shard_map.69
  15.4 1.6 %collective-permute-start.5 = (f32[8,3840]{1,0:T(8,128)S(1)}, f32[8,3840]{1,0:T(8,128)S(1)}, u32[]{:S(2)}, u32[]{:S(2)}) collective-permute-start(f32[8,3840]{1,0:T(8,128)S(1)} %get-tuple-element.29), channel_id=1, source_target_pairs={{0,2},{2,0},{1,3},{3,1},{4,6},{6,4},{5,7},{7,5},{8,10},{10,8},{9,1... | collective-permute-start | bytes 368648 | tf_op jit(solution)/shard_map/ppermute | solution.py:391
  16.9 3.9 %collective-permute-done.5.got = f32[8,3840]{1,0:T(8,128)S(1)} collective-permute-done((f32[8,3840]{1,0:T(8,128)S(1)}, f32[8,3840]{1,0:T(8,128)S(1)}, u32[]{:S(2)}, u32[]{:S(2)}) %collective-permute-start.5) | collective-permute-done | bytes 122912 | tf_op jit(solution)/shard_map/ppermute | solution.py:391
  20.8 0.2 shard_map.70
  21.0 0.5 %collective-permute-start.6 = (f32[2,4608]{1,0:T(2,128)S(1)}, f32[2,4608]{1,0:T(2,128)S(1)}, u32[]{:S(2)}, u32[]{:S(2)}) collective-permute-start(f32[2,4608]{1,0:T(2,128)S(1)} %get-tuple-element.32), channel_id=1, source_target_pairs={{0,4},{4,0},{8,12},{12,8},{1,5},{5,1},{9,13},{13,9},{2,6},{6,2},{1... | collective-permute-start | bytes 110600 | tf_op jit(solution)/shard_map/ppermute | solution.py:397
  21.5 1.7 %collective-permute-start.7 = (f32[2,4608]{1,0:T(2,128)S(1)}, f32[2,4608]{1,0:T(2,128)S(1)}, u32[]{:S(2)}, u32[]{:S(2)}) collective-permute-start(f32[2,4608]{1,0:T(2,128)S(1)} %get-tuple-element.33), channel_id=1, source_target_pairs={{0,8},{4,12},{8,0},{12,4},{1,9},{5,13},{9,1},{13,5},{2,10},{6,14},... | collective-permute-start | bytes 110600 | tf_op jit(solution)/shard_map/ppermute | solution.py:397
  23.3 2.2 %collective-permute-start.8 = (f32[2,4608]{1,0:T(2,128)S(1)}, f32[2,4608]{1,0:T(2,128)S(1)}, u32[]{:S(2)}, u32[]{:S(2)}) collective-permute-start(f32[2,4608]{1,0:T(2,128)S(1)} %get-tuple-element.34), channel_id=1, source_target_pairs={{0,12},{4,8},{8,4},{12,0},{1,13},{5,9},{9,5},{13,1},{2,14},{6,10},... | collective-permute-start | bytes 110600 | tf_op jit(solution)/shard_map/ppermute | solution.py:397
  25.5 0.0 collective-permute-done.6.got1
  25.5 0.9 %collective-permute-done.7.got2 = f32[2,4608]{1,0:T(2,128)S(1)} collective-permute-done((f32[2,4608]{1,0:T(2,128)S(1)}, f32[2,4608]{1,0:T(2,128)S(1)}, u32[]{:S(2)}, u32[]{:S(2)}) %collective-permute-start.7) | collective-permute-done | bytes 36896 | tf_op jit(solution)/shard_map/ppermute | solution.py:397
  26.4 2.6 %collective-permute-done.8.got3 = f32[2,4608]{1,0:T(2,128)S(1)} collective-permute-done((f32[2,4608]{1,0:T(2,128)S(1)}, f32[2,4608]{1,0:T(2,128)S(1)}, u32[]{:S(2)}, u32[]{:S(2)}) %collective-permute-start.8) | collective-permute-done | bytes 36896 | tf_op jit(solution)/shard_map/ppermute | solution.py:397
  29.0 2.5 %shard_map.71 = (f32[16]{0:T(128)}, bf16[1,3584]{1,0:T(2,128)(2,1)}, bf16[304,3584]{1,0:T(8,128)(2,1)}) custom-call(f32[2,3584]{1,0:T(2,128)S(1)} %get-tuple-element.30.part, f32[16,128]{1,0:T(8,128)S(1)} %get-tuple-element.31.stats, f32[2,4608]{1,0:T(2,128)S(1)} %collective-permute-done.6.got1, f32[2,4608]{1,0:T(2,128)S(1)} %collective-permute-done.7.got2, ...), custom_call_target="tpu_custom_call" | custom-call | tf_op jit(solution)/shard_map/pallas_call | solution.py:346
Async XLA Ops:
  0.6 10.9 %copy-start = (bf16[304,3584]{1,0:T(8,128)(2,1)S(1)}, bf16[304,3584]{1,0:T(8,128)(2,1)}, u32[]{:S(2)}) copy-start(bf16[304,3584]{1,0:T(8,128)(2,1)} %w.1) | copy-start | bytes 6537220
  0.6 5.8 %collective-permute-start = (f32[8,608]{1,0:T(8,128)}, f32[8,608]{1,0:T(8,128)S(1)}, u32[]{:S(2)}, u32[]{:S(2)}) collective-permute-start(f32[8,608]{1,0:T(8,128)} %own_in.1), channel_id=1, source_target_pairs={{0,1},{1,0},{2,3},{3,2},{4,5},{5,4},{6,7},{7,6},{8,9},{9,8},{10,11... | collective-permute-start | bytes 58376 | tf_op jit(solution)/shard_map/ppermute | solution.py:375
  1.2 6.3 %collective-permute-start.1 = (bf16[4,3584]{1,0:T(4,128)(2,1)}, bf16[4,3584]{1,0:T(4,128)(2,1)S(1)}, u32[]{:S(2)}, u32[]{:S(2)}) collective-permute-start(bf16[4,3584]{1,0:T(4,128)(2,1)} %h.1), channel_id=1, source_target_pairs={{0,4},{4,0},{8,12},{12,8},{1,5},{5,1},{9,13},{13,9},{2,6},{6,2},{1... | collective-permute-start | bytes 86024 | tf_op jit(solution)/shard_map/ppermute | solution.py:360
  3.8 5.9 %collective-permute-start.3 = (bf16[4,3584]{1,0:T(4,128)(2,1)}, bf16[4,3584]{1,0:T(4,128)(2,1)S(1)}, u32[]{:S(2)}, u32[]{:S(2)}) collective-permute-start(bf16[4,3584]{1,0:T(4,128)(2,1)} %h.1), channel_id=1, source_target_pairs={{0,12},{4,8},{8,4},{12,0},{1,13},{5,9},{9,5},{13,1},{2,14},{6,10},... | collective-permute-start | bytes 86024 | tf_op jit(solution)/shard_map/ppermute | solution.py:360
  6.3 5.3 %collective-permute-start.2 = (bf16[4,3584]{1,0:T(4,128)(2,1)}, bf16[4,3584]{1,0:T(4,128)(2,1)S(1)}, u32[]{:S(2)}, u32[]{:S(2)}) collective-permute-start(bf16[4,3584]{1,0:T(4,128)(2,1)} %h.1), channel_id=1, source_target_pairs={{0,8},{4,12},{8,0},{12,4},{1,9},{5,13},{9,1},{13,5},{2,10},{6,14},... | collective-permute-start | bytes 86024 | tf_op jit(solution)/shard_map/ppermute | solution.py:360
  13.6 1.5 %collective-permute-start.4 = (f32[16,3712]{1,0:T(8,128)S(1)}, f32[16,3712]{1,0:T(8,128)S(1)}, u32[]{:S(2)}, u32[]{:S(2)}) collective-permute-start(f32[16,3712]{1,0:T(8,128)S(1)} %get-tuple-element.26), channel_id=1, source_target_pairs={{0,1},{1,0},{2,3},{3,2},{4,5},{5,4},{6,7},{7,6},{8,9},{9,8},{10,11... | collective-permute-start | bytes 712712 | tf_op jit(solution)/shard_map/ppermute | solution.py:387
  15.4 5.4 %collective-permute-start.5 = (f32[8,3840]{1,0:T(8,128)S(1)}, f32[8,3840]{1,0:T(8,128)S(1)}, u32[]{:S(2)}, u32[]{:S(2)}) collective-permute-start(f32[8,3840]{1,0:T(8,128)S(1)} %get-tuple-element.29), channel_id=1, source_target_pairs={{0,2},{2,0},{1,3},{3,1},{4,6},{6,4},{5,7},{7,5},{8,10},{10,8},{9,1... | collective-permute-start | bytes 368648 | tf_op jit(solution)/shard_map/ppermute | solution.py:391
  21.0 4.5 %collective-permute-start.6 = (f32[2,4608]{1,0:T(2,128)S(1)}, f32[2,4608]{1,0:T(2,128)S(1)}, u32[]{:S(2)}, u32[]{:S(2)}) collective-permute-start(f32[2,4608]{1,0:T(2,128)S(1)} %get-tuple-element.32), channel_id=1, source_target_pairs={{0,4},{4,0},{8,12},{12,8},{1,5},{5,1},{9,13},{13,9},{2,6},{6,2},{1... | collective-permute-start | bytes 110600 | tf_op jit(solution)/shard_map/ppermute | solution.py:397
  21.5 4.9 %collective-permute-start.7 = (f32[2,4608]{1,0:T(2,128)S(1)}, f32[2,4608]{1,0:T(2,128)S(1)}, u32[]{:S(2)}, u32[]{:S(2)}) collective-permute-start(f32[2,4608]{1,0:T(2,128)S(1)} %get-tuple-element.33), channel_id=1, source_target_pairs={{0,8},{4,12},{8,0},{12,4},{1,9},{5,13},{9,1},{13,5},{2,10},{6,14},... | collective-permute-start | bytes 110600 | tf_op jit(solution)/shard_map/ppermute | solution.py:397
  23.3 5.8 %collective-permute-start.8 = (f32[2,4608]{1,0:T(2,128)S(1)}, f32[2,4608]{1,0:T(2,128)S(1)}, u32[]{:S(2)}, u32[]{:S(2)}) collective-permute-start(f32[2,4608]{1,0:T(2,128)S(1)} %get-tuple-element.34), channel_id=1, source_target_pairs={{0,12},{4,8},{8,4},{12,0},{1,13},{5,9},{9,5},{13,1},{2,14},{6,10},... | collective-permute-start | bytes 110600 | tf_op jit(solution)/shard_map/ppermute | solution.py:397

commit v5 on v4

--- a/solution.py
+++ b/solution.py
@@ -216,38 +216,41 @@
     raw[...] = 0.5 * lax.dot_general(
         rows, w[...], (((1,), (1,)), ((), ())), preferred_element_type=jnp.float32
     )
-    for b in range(4):
-        j = row_of(b, x, c)
-        for k in range(4):
-            student[4 * b + k : 4 * b + k + 1, :] = raw[pl.ds(4 * k + j, 1), :]
-    s = student[...]
-    t = scaled[...]
-    et = et_in[...]
-    ms = jnp.max(s, axis=1, keepdims=True)
-    es = jnp.exp(s - ms)
-    st = pack(
-        [
-            ms,
-            teacher[:, 1:2],
-            jnp.sum(es, axis=1, keepdims=True),
-            teacher[:, 3:4],
-            jnp.sum(et * (t - s), axis=1, keepdims=True),
-            teacher[:, 5:6],
-        ]
-    )
-    stats[...] = st
-    for b in range(4):
-        e[8 * b : 8 * b + 4, :] = es[4 * b : 4 * b + 4, :]
-        e[8 * b + 4 : 8 * b + 8, :] = et[4 * b : 4 * b + 4, :]
-    both = e[...]
-    high = both.astype(jnp.bfloat16)
-    low = (both - high.astype(jnp.float32)).astype(jnp.bfloat16)
-    part = jnp.dot(jnp.concatenate([high, low], 0), w[...], preferred_element_type=jnp.float32)
-    d = part.shape[1]
-    keep[...] = part[0:16] + part[32:48]
-    send[:, 0:d] = part[16:32] + part[48:64]
-    send[0:8, d:] = st[8:16]
-    send[8:16, d:] = st[0:8]
+
+    @pl.when(z >= 0)
+    def _():
+        for b in range(4):
+            j = row_of(b, x, c)
+            for k in range(4):
+                student[4 * b + k : 4 * b + k + 1, :] = raw[pl.ds(4 * k + j, 1), :]
+        s = student[...]
+        t = scaled[...]
+        et = et_in[...]
+        ms = jnp.max(s, axis=1, keepdims=True)
+        es = jnp.exp(s - ms)
+        st = pack(
+            [
+                ms,
+                teacher[:, 1:2],
+                jnp.sum(es, axis=1, keepdims=True),
+                teacher[:, 3:4],
+                jnp.sum(et * (t - s), axis=1, keepdims=True),
+                teacher[:, 5:6],
+            ]
+        )
+        stats[...] = st
+        for b in range(4):
+            e[8 * b : 8 * b + 4, :] = es[4 * b : 4 * b + 4, :]
+            e[8 * b + 4 : 8 * b + 8, :] = et[4 * b : 4 * b + 4, :]
+        both = e[...]
+        high = both.astype(jnp.bfloat16)
+        low = (both - high.astype(jnp.float32)).astype(jnp.bfloat16)
+        part = jnp.dot(jnp.concatenate([high, low], 0), w[...], preferred_element_type=jnp.float32)
+        d = part.shape[1]
+        keep[...] = part[0:16] + part[32:48]
+        send[:, 0:d] = part[16:32] + part[48:64]
+        send[0:8, d:] = st[8:16]
+        send[8:16, d:] = st[0:8]
 
 
 def second_kernel(part, stats, got, stats_out, keep, send):
@@ -289,7 +292,7 @@
 def make_last_kernel(chunk):
     def last_kernel(
         part, stats, got1, got2, got3, student, scaled, hb,
-        divergence, hidden_grad, weight_grad, gs, gr, out, sems,
+        divergence, hidden_grad, weight_grad, gs, gr, out, div, hid, sems,
     ):
         z, x, c = places()
         d = part.shape[1]
@@ -309,27 +312,37 @@
                 gr[pl.ds(4 * k + j, 1), :] = grad[4 * b + k : 4 * b + k + 1, :]
         g = gr[...].astype(jnp.bfloat16)
         copies = []
-        for i in range(d // chunk):
+
+        def emit(source, target):
+            copy = pltpu.make_async_copy(source, target, sems.at[len(copies)])
+            copy.start()
+            copies.append(copy)
+
+        def weight_chunk(i):
             at = pl.ds(i * chunk, chunk)
             out[:, at] = lax.dot_general(
                 g, hb[:, at], (((0,), (0,)), ((), ())), preferred_element_type=jnp.float32
             ).astype(jnp.bfloat16)
-            copy = pltpu.make_async_copy(out.at[:, at], weight_grad.at[:, at], sems.at[i])
-            copy.start()
-            copies.append(copy)
+            emit(out.at[:, at], weight_grad.at[:, at])
+
+        n = d // chunk
+        for i in range(n // 2):
+            weight_chunk(i)
         row = lax.broadcasted_iota(jnp.int32, (ROWS, 1), 0)
         home = 4 * (z ^ (row & 3)) + 2 * (x ^ ((row >> 2) & 1)) + (c ^ (row >> 3))
         value = valid * (cross / lt - lse_t + lse_s)
         lane = lax.broadcasted_iota(jnp.int32, (ROWS, STATS), 1)
-        divergence[...] = jnp.sum(jnp.where(lane == home, value, 0.0), axis=0)[0:ROWS]
+        div[...] = jnp.sum(jnp.where(lane == home, value, 0.0), axis=0)[0:ROWS]
+        emit(div, divergence)
         a_s = part[0:1, :] * factors[0][0:1, 0:1]
         a_t = part[1:2, :] * factors[0][0:1, 1:2]
         for got, f in zip((got1, got2, got3), factors[1:]):
             a_s = a_s + got[0:1, 0:d] * f[0:1, 0:1]
             a_t = a_t + got[1:2, 0:d] * f[0:1, 1:2]
-        hidden_grad[...] = (
-            gain[0:1] * (a_s / ls[0:1] - a_t / lt[0:1])
-        ).astype(jnp.bfloat16)
+        hid[...] = (gain[0:1] * (a_s / ls[0:1] - a_t / lt[0:1])).astype(jnp.bfloat16)
+        emit(hid, hidden_grad)
+        for i in range(n // 2, n):
+            weight_chunk(i)
         for copy in copies:
             copy.wait()
 
@@ -404,10 +417,12 @@
                 pltpu.VMEM((3, ROWS, STATS), f32),
                 pltpu.VMEM((ROWS, v), f32),
                 pltpu.VMEM((v, d), bf16),
-                pltpu.SemaphoreType.DMA((d // chunk,)),
+                pltpu.VMEM((ROWS,), f32),
+                pltpu.VMEM((1, d), bf16),
+                pltpu.SemaphoreType.DMA((d // chunk + 2,)),
             ],
             [VMEM] * 8,
-            [VMEM, VMEM, ANY],
+            [ANY] * 3,
         )(keep, stats, *gots, student, scaled, hb)
     )
 

time: 31.7 us -> 30.4 us (0.959)
  Pallas kernels: 6.06 us -> 4.76 us
    pallas_call x5, Pallas kernels: 6.06 us -> 4.76 us  [call(): pl.pallas_call(kernel, out_shape=shapes, in_specs=in_specs or [VMEM] * le...]
  transfers between devices with their start and end apart: 9 -> 9, of which waited for: 6 -> 6; matrix products, arithmetic and copies ran while one was open for 0% -> 0% of each run, Pallas kernels for 3% -> 4%
where the time goes in v5:
time: 30.4 us; the launch traced here: 30.2 us
  waiting for transfers between devices  13 us (43%)
  starting transfers between devices  11.8 us (39%)
  Pallas kernels  4.76 us (16%)
  between operations  0.69 us (2%)
    ppermute x3, starting transfers between devices, small_body(): pieces = [lax.ppermute(hidden_rows, 'vocab', flip(4, k)) for k in (1, 2, 3)]  5.24 us
    pallas_call x5, Pallas kernels, call(): pl.pallas_call(kernel, out_shape=shapes, in_specs=in_specs or [VMEM] * le...  4.76 us
    ppermute x3, starting transfers between devices, small_body(): lax.ppermute(a, 'vocab', flip(4, k))  4.45 us
    ppermute x3, waiting for transfers between devices, small_body(): pieces = [lax.ppermute(hidden_rows, 'vocab', flip(4, k)) for k in (1, 2, 3)]  4.07 us
    ppermute x1, waiting for transfers between devices, small_body(): got = lax.ppermute(send, 'rows', flip(2, 1))  3.87 us
    ppermute x3, waiting for transfers between devices, small_body(): lax.ppermute(a, 'vocab', flip(4, k))  3.56 us
    ppermute x1, starting transfers between devices, small_body(): got = lax.ppermute(send, 'rows', flip(2, 1))  1.56 us
    ppermute x1, waiting for transfers between devices, small_body(): got = lax.ppermute(send, 'teach', flip(2, 1))  1.49 us
  transfers between devices with their start and end apart: 9, of which 6 were waited for; matrix products, arithmetic and copies ran while one was open for 0% of the time, Pallas kernels for 4%

profile of v5, /device:TPU:0, one launch (start us, length us, event | category | flops | bytes accessed | tf_op | source)
XLA Modules:
  0.0 30.2 jit_solution(17416112977733140707)
XLA Ops:
  0.6 0.0 copy-start
  0.6 0.5 %collective-permute-start = (f32[8,608]{1,0:T(8,128)}, f32[8,608]{1,0:T(8,128)S(1)}, u32[]{:S(2)}, u32[]{:S(2)}) collective-permute-start(f32[8,608]{1,0:T(8,128)} %own_in.1), channel_id=1, source_target_pairs={{0,1},{1,0},{2,3},{3,2},{4,5},{5,4},{6,7},{7,6},{8,9},{9,8},{10,11... | collective-permute-start | bytes 58376 | tf_op jit(solution)/shard_map/ppermute | solution.py:388
  1.2 2.6 %collective-permute-start.1 = (bf16[4,3584]{1,0:T(4,128)(2,1)}, bf16[4,3584]{1,0:T(4,128)(2,1)S(1)}, u32[]{:S(2)}, u32[]{:S(2)}) collective-permute-start(bf16[4,3584]{1,0:T(4,128)(2,1)} %h.1), channel_id=1, source_target_pairs={{0,4},{4,0},{8,12},{12,8},{1,5},{5,1},{9,13},{13,9},{2,6},{6,2},{1... | collective-permute-start | bytes 86024 | tf_op jit(solution)/shard_map/ppermute | solution.py:373
  3.8 2.5 %collective-permute-start.3 = (bf16[4,3584]{1,0:T(4,128)(2,1)}, bf16[4,3584]{1,0:T(4,128)(2,1)S(1)}, u32[]{:S(2)}, u32[]{:S(2)}) collective-permute-start(bf16[4,3584]{1,0:T(4,128)(2,1)} %h.1), channel_id=1, source_target_pairs={{0,12},{4,8},{8,4},{12,0},{1,13},{5,9},{9,5},{13,1},{2,14},{6,10},... | collective-permute-start | bytes 86024 | tf_op jit(solution)/shard_map/ppermute | solution.py:373
  6.3 0.1 collective-permute-start.2
  6.4 0.0 collective-permute-done.got
  6.4 1.1 %shard_map.67 = (f32[16,304]{1,0:T(8,128)S(1)}, f32[16,304]{1,0:T(8,128)S(1)}, f32[16,128]{1,0:T(8,128)S(1)}, bf16[4,3584]{1,0:T(4,128)(2,1)S(1)}) custom-call(s32[16]{0:T(128)} %mask_in.1, f32[8,608]{1,0:T(8,128)} %own_in.1, f32[8,608]{1,0:T(8,128)S(1)} %collective-permute-done.got, bf16[4,3584]{1,0:T(4,128)(2,1)} %h.1), custom_call_target="tpu_custom_call" | custom-call | flops 2000000000 | bytes 2097152 | tf_op jit(solution)/shard_map/pallas_call | solution.py:359
  7.5 0.0 collective-permute-done.1.h1
  7.5 2.2 %collective-permute-done.3.h3 = bf16[4,3584]{1,0:T(4,128)(2,1)S(1)} collective-permute-done((bf16[4,3584]{1,0:T(4,128)(2,1)}, bf16[4,3584]{1,0:T(4,128)(2,1)S(1)}, u32[]{:S(2)}, u32[]{:S(2)}) %collective-permute-start.3) | collective-permute-done | bytes 28704 | tf_op jit(solution)/shard_map/ppermute | solution.py:373
  9.7 1.9 %collective-permute-done.2.h2 = bf16[4,3584]{1,0:T(4,128)(2,1)S(1)} collective-permute-done((bf16[4,3584]{1,0:T(4,128)(2,1)}, bf16[4,3584]{1,0:T(4,128)(2,1)S(1)}, u32[]{:S(2)}, u32[]{:S(2)}) %collective-permute-start.2) | collective-permute-done | bytes 28704 | tf_op jit(solution)/shard_map/ppermute | solution.py:373
  11.6 0.0 copy-done
  11.6 1.3 %shard_map.68 = (f32[16,304]{1,0:T(8,128)S(1)}, f32[16,128]{1,0:T(8,128)S(1)}, bf16[16,3584]{1,0:T(8,128)(2,1)S(1)}, f32[16,3584]{1,0:T(8,128)S(1)}, f32[16,3712]{1,0:T(8,128)S(1)}) custom-call(bf16[4,3584]{1,0:T(4,128)(2,1)S(1)} %get-tuple-element.20.h0, bf16[4,3584]{1,0:T(4,128)(2,1)S(1)} %collective-permute-done.1.h1, ...), custom_call_target="tpu_custom_call" | custom-call | tf_op jit(solution)/shard_map/pallas_call | solution.py:359
  12.9 0.0 collective-permute-start.4
  12.9 1.5 %collective-permute-done.4.got = f32[16,3712]{1,0:T(8,128)S(1)} collective-permute-done((f32[16,3712]{1,0:T(8,128)S(1)}, f32[16,3712]{1,0:T(8,128)S(1)}, u32[]{:S(2)}, u32[]{:S(2)}) %collective-permute-start.4) | collective-permute-done | bytes 237600 | tf_op jit(solution)/shard_map/ppermute | solution.py:400
  14.4 0.2 shard_map.69
  14.6 1.6 %collective-permute-start.5 = (f32[8,3840]{1,0:T(8,128)S(1)}, f32[8,3840]{1,0:T(8,128)S(1)}, u32[]{:S(2)}, u32[]{:S(2)}) collective-permute-start(f32[8,3840]{1,0:T(8,128)S(1)} %get-tuple-element.29), channel_id=1, source_target_pairs={{0,2},{2,0},{1,3},{3,1},{4,6},{6,4},{5,7},{7,5},{8,10},{10,8},{9,1... | collective-permute-start | bytes 368648 | tf_op jit(solution)/shard_map/ppermute | solution.py:404
  16.2 3.9 %collective-permute-done.5.got = f32[8,3840]{1,0:T(8,128)S(1)} collective-permute-done((f32[8,3840]{1,0:T(8,128)S(1)}, f32[8,3840]{1,0:T(8,128)S(1)}, u32[]{:S(2)}, u32[]{:S(2)}) %collective-permute-start.5) | collective-permute-done | bytes 122912 | tf_op jit(solution)/shard_map/ppermute | solution.py:404
  20.1 0.2 shard_map.70
  20.3 0.5 %collective-permute-start.6 = (f32[2,4608]{1,0:T(2,128)S(1)}, f32[2,4608]{1,0:T(2,128)S(1)}, u32[]{:S(2)}, u32[]{:S(2)}) collective-permute-start(f32[2,4608]{1,0:T(2,128)S(1)} %get-tuple-element.32), channel_id=1, source_target_pairs={{0,4},{4,0},{8,12},{12,8},{1,5},{5,1},{9,13},{13,9},{2,6},{6,2},{1... | collective-permute-start | bytes 110600 | tf_op jit(solution)/shard_map/ppermute | solution.py:410
  20.8 1.7 %collective-permute-start.7 = (f32[2,4608]{1,0:T(2,128)S(1)}, f32[2,4608]{1,0:T(2,128)S(1)}, u32[]{:S(2)}, u32[]{:S(2)}) collective-permute-start(f32[2,4608]{1,0:T(2,128)S(1)} %get-tuple-element.33), channel_id=1, source_target_pairs={{0,8},{4,12},{8,0},{12,4},{1,9},{5,13},{9,1},{13,5},{2,10},{6,14},... | collective-permute-start | bytes 110600 | tf_op jit(solution)/shard_map/ppermute | solution.py:410
  22.5 2.2 %collective-permute-start.8 = (f32[2,4608]{1,0:T(2,128)S(1)}, f32[2,4608]{1,0:T(2,128)S(1)}, u32[]{:S(2)}, u32[]{:S(2)}) collective-permute-start(f32[2,4608]{1,0:T(2,128)S(1)} %get-tuple-element.34), channel_id=1, source_target_pairs={{0,12},{4,8},{8,4},{12,0},{1,13},{5,9},{9,5},{13,1},{2,14},{6,10},... | collective-permute-start | bytes 110600 | tf_op jit(solution)/shard_map/ppermute | solution.py:410
  24.7 0.0 collective-permute-done.6.got1
  24.7 0.9 %collective-permute-done.7.got2 = f32[2,4608]{1,0:T(2,128)S(1)} collective-permute-done((f32[2,4608]{1,0:T(2,128)S(1)}, f32[2,4608]{1,0:T(2,128)S(1)}, u32[]{:S(2)}, u32[]{:S(2)}) %collective-permute-start.7) | collective-permute-done | bytes 36896 | tf_op jit(solution)/shard_map/ppermute | solution.py:410
  25.7 2.6 %collective-permute-done.8.got3 = f32[2,4608]{1,0:T(2,128)S(1)} collective-permute-done((f32[2,4608]{1,0:T(2,128)S(1)}, f32[2,4608]{1,0:T(2,128)S(1)}, u32[]{:S(2)}, u32[]{:S(2)}) %collective-permute-start.8) | collective-permute-done | bytes 36896 | tf_op jit(solution)/shard_map/ppermute | solution.py:410
  28.3 2.0 %shard_map.71 = (f32[16]{0:T(128)}, bf16[1,3584]{1,0:T(2,128)(2,1)}, bf16[304,3584]{1,0:T(8,128)(2,1)}) custom-call(f32[2,3584]{1,0:T(2,128)S(1)} %get-tuple-element.30.part, f32[16,128]{1,0:T(8,128)S(1)} %get-tuple-element.31.stats, f32[2,4608]{1,0:T(2,128)S(1)} %collective-permute-done.6.got1, f32[2,4608]{1,0:T(2,128)S(1)} %collective-permute-done.7.got2, ...), custom_call_target="tpu_custom_call" | custom-call | tf_op jit(solution)/shard_map/pallas_call | solution.py:359
Async XLA Ops:
  0.6 10.9 %copy-start = (bf16[304,3584]{1,0:T(8,128)(2,1)S(1)}, bf16[304,3584]{1,0:T(8,128)(2,1)}, u32[]{:S(2)}) copy-start(bf16[304,3584]{1,0:T(8,128)(2,1)} %w.1) | copy-start | bytes 6537220
  0.6 5.8 %collective-permute-start = (f32[8,608]{1,0:T(8,128)}, f32[8,608]{1,0:T(8,128)S(1)}, u32[]{:S(2)}, u32[]{:S(2)}) collective-permute-start(f32[8,608]{1,0:T(8,128)} %own_in.1), channel_id=1, source_target_pairs={{0,1},{1,0},{2,3},{3,2},{4,5},{5,4},{6,7},{7,6},{8,9},{9,8},{10,11... | collective-permute-start | bytes 58376 | tf_op jit(solution)/shard_map/ppermute | solution.py:388
  1.2 6.3 %collective-permute-start.1 = (bf16[4,3584]{1,0:T(4,128)(2,1)}, bf16[4,3584]{1,0:T(4,128)(2,1)S(1)}, u32[]{:S(2)}, u32[]{:S(2)}) collective-permute-start(bf16[4,3584]{1,0:T(4,128)(2,1)} %h.1), channel_id=1, source_target_pairs={{0,4},{4,0},{8,12},{12,8},{1,5},{5,1},{9,13},{13,9},{2,6},{6,2},{1... | collective-permute-start | bytes 86024 | tf_op jit(solution)/shard_map/ppermute | solution.py:373
  3.8 5.9 %collective-permute-start.3 = (bf16[4,3584]{1,0:T(4,128)(2,1)}, bf16[4,3584]{1,0:T(4,128)(2,1)S(1)}, u32[]{:S(2)}, u32[]{:S(2)}) collective-permute-start(bf16[4,3584]{1,0:T(4,128)(2,1)} %h.1), channel_id=1, source_target_pairs={{0,12},{4,8},{8,4},{12,0},{1,13},{5,9},{9,5},{13,1},{2,14},{6,10},... | collective-permute-start | bytes 86024 | tf_op jit(solution)/shard_map/ppermute | solution.py:373
  6.3 5.3 %collective-permute-start.2 = (bf16[4,3584]{1,0:T(4,128)(2,1)}, bf16[4,3584]{1,0:T(4,128)(2,1)S(1)}, u32[]{:S(2)}, u32[]{:S(2)}) collective-permute-start(bf16[4,3584]{1,0:T(4,128)(2,1)} %h.1), channel_id=1, source_target_pairs={{0,8},{4,12},{8,0},{12,4},{1,9},{5,13},{9,1},{13,5},{2,10},{6,14},... | collective-permute-start | bytes 86024 | tf_op jit(solution)/shard_map/ppermute | solution.py:373
  12.9 1.5 %collective-permute-start.4 = (f32[16,3712]{1,0:T(8,128)S(1)}, f32[16,3712]{1,0:T(8,128)S(1)}, u32[]{:S(2)}, u32[]{:S(2)}) collective-permute-start(f32[16,3712]{1,0:T(8,128)S(1)} %get-tuple-element.26), channel_id=1, source_target_pairs={{0,1},{1,0},{2,3},{3,2},{4,5},{5,4},{6,7},{7,6},{8,9},{9,8},{10,11... | collective-permute-start | bytes 712712 | tf_op jit(solution)/shard_map/ppermute | solution.py:400
  14.6 5.4 %collective-permute-start.5 = (f32[8,3840]{1,0:T(8,128)S(1)}, f32[8,3840]{1,0:T(8,128)S(1)}, u32[]{:S(2)}, u32[]{:S(2)}) collective-permute-start(f32[8,3840]{1,0:T(8,128)S(1)} %get-tuple-element.29), channel_id=1, source_target_pairs={{0,2},{2,0},{1,3},{3,1},{4,6},{6,4},{5,7},{7,5},{8,10},{10,8},{9,1... | collective-permute-start | bytes 368648 | tf_op jit(solution)/shard_map/ppermute | solution.py:404
  20.3 4.5 %collective-permute-start.6 = (f32[2,4608]{1,0:T(2,128)S(1)}, f32[2,4608]{1,0:T(2,128)S(1)}, u32[]{:S(2)}, u32[]{:S(2)}) collective-permute-start(f32[2,4608]{1,0:T(2,128)S(1)} %get-tuple-element.32), channel_id=1, source_target_pairs={{0,4},{4,0},{8,12},{12,8},{1,5},{5,1},{9,13},{13,9},{2,6},{6,2},{1... | collective-permute-start | bytes 110600 | tf_op jit(solution)/shard_map/ppermute | solution.py:410
  20.8 4.9 %collective-permute-start.7 = (f32[2,4608]{1,0:T(2,128)S(1)}, f32[2,4608]{1,0:T(2,128)S(1)}, u32[]{:S(2)}, u32[]{:S(2)}) collective-permute-start(f32[2,4608]{1,0:T(2,128)S(1)} %get-tuple-element.33), channel_id=1, source_target_pairs={{0,8},{4,12},{8,0},{12,4},{1,9},{5,13},{9,1},{13,5},{2,10},{6,14},... | collective-permute-start | bytes 110600 | tf_op jit(solution)/shard_map/ppermute | solution.py:410
  22.5 5.8 %collective-permute-start.8 = (f32[2,4608]{1,0:T(2,128)S(1)}, f32[2,4608]{1,0:T(2,128)S(1)}, u32[]{:S(2)}, u32[]{:S(2)}) collective-permute-start(f32[2,4608]{1,0:T(2,128)S(1)} %get-tuple-element.34), channel_id=1, source_target_pairs={{0,12},{4,8},{8,4},{12,0},{1,13},{5,9},{9,5},{13,1},{2,14},{6,10},... | collective-permute-start | bytes 110600 | tf_op jit(solution)/shard_map/ppermute | solution.py:410

commit v6 on v5

--- a/solution.py
+++ b/solution.py
@@ -179,32 +179,36 @@
     return 2 * (x ^ (b & 1)) + (c ^ (b >> 1))
 
 
-def teacher_kernel(mask_in, own_in, got, h, scaled, et, stats, h_out, tt, mask, own, sems):
-    copies = [
-        pltpu.make_async_copy(a, b, sems.at[i])
-        for i, (a, b) in enumerate(((own_in, own), (mask_in, mask), (h, h_out)))
-    ]
+def entry_kernel(mask_in, own_in, h_in, valid_out, own, h, mask, sems):
+    pairs = ((mask_in, mask), (h_in, h), (own_in, own))
+    copies = [pltpu.make_async_copy(a, b, sems.at[i]) for i, (a, b) in enumerate(pairs)]
     for copy in copies:
         copy.start()
     z, x, c = places()
+    copies[0].wait()
+    row = lax.broadcasted_iota(jnp.int32, (ROWS, STATS), 0)
+    valid = jnp.zeros((ROWS, STATS), jnp.float32)
+    for r in range(ROWS):
+        at = 4 * ((r & 3) ^ z) + row_of(r >> 2, x, c)
+        valid = jnp.where(row == r, mask[at].astype(jnp.float32), valid)
+    valid_out[...] = valid
+    copies[1].wait()
+    copies[2].wait()
+
+
+def teacher_kernel(valid, own, got, scaled, et, stats, tt):
+    z, x, c = places()
     v = scaled.shape[1]
-    copies[0].wait()
-    copies[1].wait()
     for i, tile in ((c, own[...]), (1 - c, got[...])):
         tt[pl.ds(pl.multiple_of(8 * i, 8), 8), :] = 0.5 * jnp.where(c == 0, tile[:, 0:v], tile[:, v : 2 * v])
-    row = lax.broadcasted_iota(jnp.int32, (ROWS, 1), 0)
-    valid = jnp.zeros((ROWS, 1), jnp.float32)
     for r in range(ROWS):
-        at = 4 * ((r & 3) ^ z) + row_of(r >> 2, x, c)
-        scaled[r : r + 1, :] = tt[pl.ds(at, 1), :]
-        valid = jnp.where(row == r, mask[at].astype(jnp.float32), valid)
+        scaled[r : r + 1, :] = tt[pl.ds(4 * ((r & 3) ^ z) + row_of(r >> 2, x, c), 1), :]
     t = scaled[...]
     mt = jnp.max(t, axis=1, keepdims=True)
     e = jnp.exp(t - mt)
     et[...] = e
     none = jnp.zeros_like(mt)
-    stats[...] = pack([none, mt, none, jnp.sum(e, axis=1, keepdims=True), none, valid])
-    copies[2].wait()
+    stats[...] = pack([none, mt, none, jnp.sum(e, axis=1, keepdims=True), none, valid[:, 5:6]])
 
 
 def first_kernel(h0, h1, h2, h3, w, scaled, et_in, teacher, student, stats, hb, keep, send, hf, raw, e):
@@ -370,24 +374,19 @@
 def small_body(hidden_rows, mentor, head_weight, row_mask):
     f32, bf16 = jnp.float32, jnp.bfloat16
     v, d = head_weight.shape
-    pieces = [lax.ppermute(hidden_rows, "vocab", flip(4, k)) for k in (1, 2, 3)]
-    scaled, et, teacher, own = call(
+    valid, tile, own = call(
+        entry_kernel,
+        [((ROWS, STATS), f32), (mentor.shape, f32), ((4, d), bf16)],
+        [pltpu.SMEM((ROWS,), jnp.int32), pltpu.SemaphoreType.DMA((3,))],
+        [ANY] * 3,
+    )(*(pltpu.with_memory_space_constraint(a, pltpu.HBM) for a in (row_mask, mentor, hidden_rows)))
+    pieces = [lax.ppermute(own, "vocab", flip(4, k)) for k in (1, 2, 3)]
+    scaled, et, teacher = call(
         teacher_kernel,
-        [((ROWS, v), f32), ((ROWS, v), f32), ((ROWS, STATS), f32), ((4, d), bf16)],
-        [
-            pltpu.VMEM((ROWS, v), f32),
-            pltpu.SMEM((ROWS,), jnp.int32),
-            pltpu.VMEM((ROWS // 2, 2 * v), f32),
-            pltpu.SemaphoreType.DMA((3,)),
-        ],
-        [ANY, ANY, VMEM, ANY],
+        [((ROWS, v), f32), ((ROWS, v), f32), ((ROWS, STATS), f32)],
+        [pltpu.VMEM((ROWS, v), f32)],
         cost=pl.CostEstimate(flops=2_000_000_000, transcendentals=ROWS * v, bytes_accessed=2 << 20),
-    )(
-        pltpu.with_memory_space_constraint(row_mask, pltpu.HBM),
-        pltpu.with_memory_space_constraint(mentor, pltpu.HBM),
-        lax.ppermute(mentor, "teach", flip(2, 1)),
-        pltpu.with_memory_space_constraint(hidden_rows, pltpu.HBM),
-    )
+    )(valid, tile, lax.ppermute(tile, "teach", flip(2, 1)))
     student, stats, hb, keep, send = call(
         first_kernel,
         [((ROWS, v), f32), ((ROWS, STATS), f32), ((ROWS, d), bf16), ((16, d), f32), ((16, d + STATS), f32)],

time: 30.4 us -> 30.1 us (level)
    pallas_call x5 -> x6, Pallas kernels: 4.76 us -> 4.7 us  [call(): pl.pallas_call(kernel, out_shape=shapes, in_specs=in_specs or [VMEM] * le...]
  transfers between devices with their start and end apart: 9 -> 9, of which waited for: 6 -> 6; matrix products, arithmetic and copies ran while one was open for 0% -> 0% of each run, Pallas kernels for 4% -> 1%
where the time goes in v6:
time: 30.1 us; the launch traced here: 30 us
  waiting for transfers between devices  12.7 us (42%)
  starting transfers between devices  11.9 us (40%)
  Pallas kernels  4.7 us (16%)
  between operations  0.67 us (2%)
    ppermute x3, starting transfers between devices, small_body(): pieces = [lax.ppermute(own, 'vocab', flip(4, k)) for k in (1, 2, 3)]  5.32 us
    pallas_call x6, Pallas kernels, call(): pl.pallas_call(kernel, out_shape=shapes, in_specs=in_specs or [VMEM] * le...  4.7 us
    ppermute x3, starting transfers between devices, small_body(): lax.ppermute(a, 'vocab', flip(4, k))  4.45 us
    ppermute x3, waiting for transfers between devices, small_body(): pieces = [lax.ppermute(own, 'vocab', flip(4, k)) for k in (1, 2, 3)]  3.87 us
    ppermute x1, waiting for transfers between devices, small_body(): got = lax.ppermute(send, 'rows', flip(2, 1))  3.87 us
    ppermute x3, waiting for transfers between devices, small_body(): lax.ppermute(a, 'vocab', flip(4, k))  3.47 us
    ppermute x1, starting transfers between devices, small_body(): got = lax.ppermute(send, 'rows', flip(2, 1))  1.56 us
    ppermute x1, waiting for transfers between devices, small_body(): got = lax.ppermute(send, 'teach', flip(2, 1))  1.49 us
  transfers between devices with their start and end apart: 9, of which 6 were waited for; matrix products, arithmetic and copies ran while one was open for 0% of the time, Pallas kernels for 1%

profile of v6, /device:TPU:0, one launch (start us, length us, event | category | flops | bytes accessed | tf_op | source)
XLA Modules:
  0.0 30.0 jit_solution(203073922797048073)
XLA Ops:
  0.6 0.8 %shard_map.67 = (f32[16,128]{1,0:T(8,128)S(1)}, f32[8,608]{1,0:T(8,128)S(1)}, bf16[4,3584]{1,0:T(4,128)(2,1)S(1)}) custom-call(s32[16]{0:T(128)} %mask_in.1, f32[8,608]{1,0:T(8,128)} %own_in.1, bf16[4,3584]{1,0:T(4,128)(2,1)} %h_in.1), custom_call_target="tpu_custom_call" | custom-call | tf_op jit(solution)/shard_map/pallas_call | solution.py:363
  1.4 0.5 %collective-permute-start.3 = (f32[8,608]{1,0:T(8,128)S(1)}, f32[8,608]{1,0:T(8,128)S(1)}, u32[]{:S(2)}, u32[]{:S(2)}) collective-permute-start(f32[8,608]{1,0:T(8,128)S(1)} %get-tuple-element.24.own), channel_id=1, source_target_pairs={{0,1},{1,0},{2,3},{3,2},{4,5},{5,4},{6,7},{7,6},{8,9},{9,8},{10,11... | collective-permute-start | bytes 58376 | tf_op jit(solution)/shard_map/ppermute | solution.py:389
  1.9 4.7 %collective-permute-start.2 = (bf16[4,3584]{1,0:T(4,128)(2,1)S(1)}, bf16[4,3584]{1,0:T(4,128)(2,1)S(1)}, u32[]{:S(2)}, u32[]{:S(2)}) collective-permute-start(bf16[4,3584]{1,0:T(4,128)(2,1)S(1)} %get-tuple-element.22.h0), channel_id=1, source_target_pairs={{0,12},{4,8},{8,4},{12,0},{1,13},{5,9},{9,5},{13,1},{2,14},{6,10},... | collective-permute-start | bytes 86024 | tf_op jit(solution)/shard_map/ppermute | solution.py:383
  6.6 0.0 collective-permute-start.1
  6.6 0.6 %collective-permute-start = (bf16[4,3584]{1,0:T(4,128)(2,1)S(1)}, bf16[4,3584]{1,0:T(4,128)(2,1)S(1)}, u32[]{:S(2)}, u32[]{:S(2)}) collective-permute-start(bf16[4,3584]{1,0:T(4,128)(2,1)S(1)} %get-tuple-element.22.h0), channel_id=1, source_target_pairs={{0,4},{4,0},{8,12},{12,8},{1,5},{5,1},{9,13},{13,9},{2,6},{6,2},{1... | collective-permute-start | bytes 86024 | tf_op jit(solution)/shard_map/ppermute | solution.py:383
  7.3 0.0 collective-permute-done.3.got
  7.3 0.0 copy-start
  7.3 0.2 shard_map.68
  7.5 1.0 %collective-permute-done.2.h3 = bf16[4,3584]{1,0:T(4,128)(2,1)S(1)} collective-permute-done((bf16[4,3584]{1,0:T(4,128)(2,1)S(1)}, bf16[4,3584]{1,0:T(4,128)(2,1)S(1)}, u32[]{:S(2)}, u32[]{:S(2)}) %collective-permute-start.2) | collective-permute-done | bytes 28704 | tf_op jit(solution)/shard_map/ppermute | solution.py:383
  8.5 2.9 %collective-permute-done.1.h2 = bf16[4,3584]{1,0:T(4,128)(2,1)S(1)} collective-permute-done((bf16[4,3584]{1,0:T(4,128)(2,1)S(1)}, bf16[4,3584]{1,0:T(4,128)(2,1)S(1)}, u32[]{:S(2)}, u32[]{:S(2)}) %collective-permute-start.1) | collective-permute-done | bytes 28704 | tf_op jit(solution)/shard_map/ppermute | solution.py:383
  11.4 0.0 collective-permute-done.h1
  11.4 0.0 copy-done
  11.4 1.3 %shard_map.69 = (f32[16,304]{1,0:T(8,128)S(1)}, f32[16,128]{1,0:T(8,128)S(1)}, bf16[16,3584]{1,0:T(8,128)(2,1)S(1)}, f32[16,3584]{1,0:T(8,128)S(1)}, f32[16,3712]{1,0:T(8,128)S(1)}) custom-call(bf16[4,3584]{1,0:T(4,128)(2,1)S(1)} %get-tuple-element.22.h0, bf16[4,3584]{1,0:T(4,128)(2,1)S(1)} %collective-permute-done.h1, ...), custom_call_target="tpu_custom_call" | custom-call | tf_op jit(solution)/shard_map/pallas_call | solution.py:363
  12.7 0.0 collective-permute-start.4
  12.8 1.5 %collective-permute-done.4.got = f32[16,3712]{1,0:T(8,128)S(1)} collective-permute-done((f32[16,3712]{1,0:T(8,128)S(1)}, f32[16,3712]{1,0:T(8,128)S(1)}, u32[]{:S(2)}, u32[]{:S(2)}) %collective-permute-start.4) | collective-permute-done | bytes 237600 | tf_op jit(solution)/shard_map/ppermute | solution.py:399
  14.2 0.2 shard_map.70
  14.4 1.6 %collective-permute-start.5 = (f32[8,3840]{1,0:T(8,128)S(1)}, f32[8,3840]{1,0:T(8,128)S(1)}, u32[]{:S(2)}, u32[]{:S(2)}) collective-permute-start(f32[8,3840]{1,0:T(8,128)S(1)} %get-tuple-element.33), channel_id=1, source_target_pairs={{0,2},{2,0},{1,3},{3,1},{4,6},{6,4},{5,7},{7,5},{8,10},{10,8},{9,1... | collective-permute-start | bytes 368648 | tf_op jit(solution)/shard_map/ppermute | solution.py:403
  16.0 3.9 %collective-permute-done.5.got = f32[8,3840]{1,0:T(8,128)S(1)} collective-permute-done((f32[8,3840]{1,0:T(8,128)S(1)}, f32[8,3840]{1,0:T(8,128)S(1)}, u32[]{:S(2)}, u32[]{:S(2)}) %collective-permute-start.5) | collective-permute-done | bytes 122912 | tf_op jit(solution)/shard_map/ppermute | solution.py:403
  19.9 0.2 shard_map.71
  20.1 0.2 collective-permute-start.6
  20.2 2.0 %collective-permute-start.7 = (f32[2,4608]{1,0:T(2,128)S(1)}, f32[2,4608]{1,0:T(2,128)S(1)}, u32[]{:S(2)}, u32[]{:S(2)}) collective-permute-start(f32[2,4608]{1,0:T(2,128)S(1)} %get-tuple-element.37), channel_id=1, source_target_pairs={{0,8},{4,12},{8,0},{12,4},{1,9},{5,13},{9,1},{13,5},{2,10},{6,14},... | collective-permute-start | bytes 110600 | tf_op jit(solution)/shard_map/ppermute | solution.py:409
  22.2 2.3 %collective-permute-start.8 = (f32[2,4608]{1,0:T(2,128)S(1)}, f32[2,4608]{1,0:T(2,128)S(1)}, u32[]{:S(2)}, u32[]{:S(2)}) collective-permute-start(f32[2,4608]{1,0:T(2,128)S(1)} %get-tuple-element.38), channel_id=1, source_target_pairs={{0,12},{4,8},{8,4},{12,0},{1,13},{5,9},{9,5},{13,1},{2,14},{6,10},... | collective-permute-start | bytes 110600 | tf_op jit(solution)/shard_map/ppermute | solution.py:409
  24.5 0.0 collective-permute-done.6.got1
  24.5 0.7 %collective-permute-done.7.got2 = f32[2,4608]{1,0:T(2,128)S(1)} collective-permute-done((f32[2,4608]{1,0:T(2,128)S(1)}, f32[2,4608]{1,0:T(2,128)S(1)}, u32[]{:S(2)}, u32[]{:S(2)}) %collective-permute-start.7) | collective-permute-done | bytes 36896 | tf_op jit(solution)/shard_map/ppermute | solution.py:409
  25.2 2.8 %collective-permute-done.8.got3 = f32[2,4608]{1,0:T(2,128)S(1)} collective-permute-done((f32[2,4608]{1,0:T(2,128)S(1)}, f32[2,4608]{1,0:T(2,128)S(1)}, u32[]{:S(2)}, u32[]{:S(2)}) %collective-permute-start.8) | collective-permute-done | bytes 36896 | tf_op jit(solution)/shard_map/ppermute | solution.py:409
  28.0 2.0 %shard_map.72 = (f32[16]{0:T(128)}, bf16[1,3584]{1,0:T(2,128)(2,1)}, bf16[304,3584]{1,0:T(8,128)(2,1)}) custom-call(f32[2,3584]{1,0:T(2,128)S(1)} %get-tuple-element.34.part, f32[16,128]{1,0:T(8,128)S(1)} %get-tuple-element.35.stats, f32[2,4608]{1,0:T(2,128)S(1)} %collective-permute-done.6.got1, f32[2,4608]{1,0:T(2,128)S(1)} %collective-permute-done.7.got2, ...), custom_call_target="tpu_custom_call" | custom-call | tf_op jit(solution)/shard_map/pallas_call | solution.py:363
Async XLA Ops:
  1.4 5.8 %collective-permute-start.3 = (f32[8,608]{1,0:T(8,128)S(1)}, f32[8,608]{1,0:T(8,128)S(1)}, u32[]{:S(2)}, u32[]{:S(2)}) collective-permute-start(f32[8,608]{1,0:T(8,128)S(1)} %get-tuple-element.24.own), channel_id=1, source_target_pairs={{0,1},{1,0},{2,3},{3,2},{4,5},{5,4},{6,7},{7,6},{8,9},{9,8},{10,11... | collective-permute-start | bytes 58376 | tf_op jit(solution)/shard_map/ppermute | solution.py:389
  1.9 6.6 %collective-permute-start.2 = (bf16[4,3584]{1,0:T(4,128)(2,1)S(1)}, bf16[4,3584]{1,0:T(4,128)(2,1)S(1)}, u32[]{:S(2)}, u32[]{:S(2)}) collective-permute-start(bf16[4,3584]{1,0:T(4,128)(2,1)S(1)} %get-tuple-element.22.h0), channel_id=1, source_target_pairs={{0,12},{4,8},{8,4},{12,0},{1,13},{5,9},{9,5},{13,1},{2,14},{6,10},... | collective-permute-start | bytes 86024 | tf_op jit(solution)/shard_map/ppermute | solution.py:383
  6.6 4.8 %collective-permute-start.1 = (bf16[4,3584]{1,0:T(4,128)(2,1)S(1)}, bf16[4,3584]{1,0:T(4,128)(2,1)S(1)}, u32[]{:S(2)}, u32[]{:S(2)}) collective-permute-start(bf16[4,3584]{1,0:T(4,128)(2,1)S(1)} %get-tuple-element.22.h0), channel_id=1, source_target_pairs={{0,8},{4,12},{8,0},{12,4},{1,9},{5,13},{9,1},{13,5},{2,10},{6,14},... | collective-permute-start | bytes 86024 | tf_op jit(solution)/shard_map/ppermute | solution.py:383
  6.6 4.8 %collective-permute-start = (bf16[4,3584]{1,0:T(4,128)(2,1)S(1)}, bf16[4,3584]{1,0:T(4,128)(2,1)S(1)}, u32[]{:S(2)}, u32[]{:S(2)}) collective-permute-start(bf16[4,3584]{1,0:T(4,128)(2,1)S(1)} %get-tuple-element.22.h0), channel_id=1, source_target_pairs={{0,4},{4,0},{8,12},{12,8},{1,5},{5,1},{9,13},{13,9},{2,6},{6,2},{1... | collective-permute-start | bytes 86024 | tf_op jit(solution)/shard_map/ppermute | solution.py:383
  7.3 4.1 %copy-start = (bf16[304,3584]{1,0:T(8,128)(2,1)S(1)}, bf16[304,3584]{1,0:T(8,128)(2,1)}, u32[]{:S(2)}) copy-start(bf16[304,3584]{1,0:T(8,128)(2,1)} %w.1) | copy-start | bytes 6537220
  12.7 1.5 %collective-permute-start.4 = (f32[16,3712]{1,0:T(8,128)S(1)}, f32[16,3712]{1,0:T(8,128)S(1)}, u32[]{:S(2)}, u32[]{:S(2)}) collective-permute-start(f32[16,3712]{1,0:T(8,128)S(1)} %get-tuple-element.30), channel_id=1, source_target_pairs={{0,1},{1,0},{2,3},{3,2},{4,5},{5,4},{6,7},{7,6},{8,9},{9,8},{10,11... | collective-permute-start | bytes 712712 | tf_op jit(solution)/shard_map/ppermute | solution.py:399
  14.4 5.4 %collective-permute-start.5 = (f32[8,3840]{1,0:T(8,128)S(1)}, f32[8,3840]{1,0:T(8,128)S(1)}, u32[]{:S(2)}, u32[]{:S(2)}) collective-permute-start(f32[8,3840]{1,0:T(8,128)S(1)} %get-tuple-element.33), channel_id=1, source_target_pairs={{0,2},{2,0},{1,3},{3,1},{4,6},{6,4},{5,7},{7,5},{8,10},{10,8},{9,1... | collective-permute-start | bytes 368648 | tf_op jit(solution)/shard_map/ppermute | solution.py:403
  20.1 4.5 %collective-permute-start.6 = (f32[2,4608]{1,0:T(2,128)S(1)}, f32[2,4608]{1,0:T(2,128)S(1)}, u32[]{:S(2)}, u32[]{:S(2)}) collective-permute-start(f32[2,4608]{1,0:T(2,128)S(1)} %get-tuple-element.36), channel_id=1, source_target_pairs={{0,4},{4,0},{8,12},{12,8},{1,5},{5,1},{9,13},{13,9},{2,6},{6,2},{1... | collective-permute-start | bytes 110600 | tf_op jit(solution)/shard_map/ppermute | solution.py:409
  20.2 5.0 %collective-permute-start.7 = (f32[2,4608]{1,0:T(2,128)S(1)}, f32[2,4608]{1,0:T(2,128)S(1)}, u32[]{:S(2)}, u32[]{:S(2)}) collective-permute-start(f32[2,4608]{1,0:T(2,128)S(1)} %get-tuple-element.37), channel_id=1, source_target_pairs={{0,8},{4,12},{8,0},{12,4},{1,9},{5,13},{9,1},{13,5},{2,10},{6,14},... | collective-permute-start | bytes 110600 | tf_op jit(solution)/shard_map/ppermute | solution.py:409
  22.2 5.8 %collective-permute-start.8 = (f32[2,4608]{1,0:T(2,128)S(1)}, f32[2,4608]{1,0:T(2,128)S(1)}, u32[]{:S(2)}, u32[]{:S(2)}) collective-permute-start(f32[2,4608]{1,0:T(2,128)S(1)} %get-tuple-element.38), channel_id=1, source_target_pairs={{0,12},{4,8},{8,4},{12,0},{1,13},{5,9},{9,5},{13,1},{2,14},{6,10},... | collective-permute-start | bytes 110600 | tf_op jit(solution)/shard_map/ppermute | solution.py:409

commit v7 on v6

--- a/solution.py
+++ b/solution.py
@@ -273,7 +273,7 @@
         send[4:8, d + 128 * i : d + 128 * i + 128] = st[8 * i : 8 * i + 4]
 
 
-def third_kernel(part, stats, got, stats_out, keep, send1, send2, send3, gs):
+def third_kernel(part, stats, got, stats_out, keep, send3, send2, send1, gs):
     d = part.shape[1]
     for i in range(2):
         gs[8 * i : 8 * i + 8, :] = got[:, d + 128 * i : d + 128 * i + 128]
@@ -295,7 +295,7 @@
 
 def make_last_kernel(chunk):
     def last_kernel(
-        part, stats, got1, got2, got3, student, scaled, hb,
+        part, stats, got3, got2, got1, student, scaled, hb,
         divergence, hidden_grad, weight_grad, gs, gr, out, div, hid, sems,
     ):
         z, x, c = places()
@@ -379,13 +379,13 @@
         [((ROWS, STATS), f32), (mentor.shape, f32), ((4, d), bf16)],
         [pltpu.SMEM((ROWS,), jnp.int32), pltpu.SemaphoreType.DMA((3,))],
         [ANY] * 3,
+        cost=pl.CostEstimate(flops=2_000_000_000, transcendentals=0, bytes_accessed=2 << 20),
     )(*(pltpu.with_memory_space_constraint(a, pltpu.HBM) for a in (row_mask, mentor, hidden_rows)))
     pieces = [lax.ppermute(own, "vocab", flip(4, k)) for k in (1, 2, 3)]
     scaled, et, teacher = call(
         teacher_kernel,
         [((ROWS, v), f32), ((ROWS, v), f32), ((ROWS, STATS), f32)],
         [pltpu.VMEM((ROWS, v), f32)],
-        cost=pl.CostEstimate(flops=2_000_000_000, transcendentals=ROWS * v, bytes_accessed=2 << 20),
     )(valid, tile, lax.ppermute(tile, "teach", flip(2, 1)))
     student, stats, hb, keep, send = call(
         first_kernel,
@@ -406,7 +406,7 @@
         [((ROWS, STATS), f32), ((2, d), f32)] + [((2, d + 8 * STATS), f32)] * 3,
         [pltpu.VMEM((ROWS, STATS), f32)],
     )(keep, stats, got)
-    gots = [lax.ppermute(a, "vocab", flip(4, k)) for k, a in enumerate(sends, 1)]
+    gots = [lax.ppermute(a, "vocab", flip(4, k)) for k, a in zip((3, 2, 1), sends)]
     chunk = 512
     return tuple(
         call(

time: 30.1 us -> 29.1 us (0.967)
  waiting for transfers between devices: 12.7 us -> 11.6 us
    ppermute x1, waiting for transfers between devices: 0.01 us -> 1.19 us  [small_body(): lax.ppermute(tile, 'teach', flip(2, 1))]
    ppermute x3, waiting for transfers between devices: 3.87 us -> 2.69 us  [small_body(): pieces = [lax.ppermute(own, 'vocab', flip(4, k)) for k in (1, 2, 3)]]
    ppermute x3, waiting for transfers between devices: 3.47 us -> 2.35 us  [small_body(): lax.ppermute(a, 'vocab', flip(4, k))]
    ppermute x1, starting transfers between devices: 0.52 us -> 0.01 us  [small_body(): lax.ppermute(tile, 'teach', flip(2, 1))]
    ppermute x3, starting transfers between devices: 5.32 us -> 5.76 us  [small_body(): pieces = [lax.ppermute(own, 'vocab', flip(4, k)) for k in (1, 2, 3)]]
  transfers between devices with their start and end apart: 9 -> 9, of which waited for: 6 -> 7; matrix products, arithmetic and copies ran while one was open for 0% -> 0% of each run, Pallas kernels for 1% -> 1%
where the time goes in v7:
time: 29.1 us; the launch traced here: 28.9 us
  starting transfers between devices  11.8 us (41%)
  waiting for transfers between devices  11.6 us (40%)
  Pallas kernels  4.85 us (17%)
  between operations  0.68 us (2%)
    ppermute x3, starting transfers between devices, small_body(): pieces = [lax.ppermute(own, 'vocab', flip(4, k)) for k in (1, 2, 3)]  5.76 us
    pallas_call x6, Pallas kernels, call(): pl.pallas_call(kernel, out_shape=shapes, in_specs=in_specs or [VMEM] * le...  4.85 us
    ppermute x3, starting transfers between devices, small_body(): lax.ppermute(a, 'vocab', flip(4, k))  4.45 us
    ppermute x1, waiting for transfers between devices, small_body(): got = lax.ppermute(send, 'rows', flip(2, 1))  3.87 us
    ppermute x3, waiting for transfers between devices, small_body(): pieces = [lax.ppermute(own, 'vocab', flip(4, k)) for k in (1, 2, 3)]  2.69 us
    ppermute x3, waiting for transfers between devices, small_body(): lax.ppermute(a, 'vocab', flip(4, k))  2.35 us
    ppermute x1, starting transfers between devices, small_body(): got = lax.ppermute(send, 'rows', flip(2, 1))  1.55 us
    ppermute x1, waiting for transfers between devices, small_body(): got = lax.ppermute(send, 'teach', flip(2, 1))  1.49 us
  transfers between devices with their start and end apart: 9, of which 7 were waited for; matrix products, arithmetic and copies ran while one was open for 0% of the time, Pallas kernels for 1%

profile of v7, /device:TPU:0, one launch (start us, length us, event | category | flops | bytes accessed | tf_op | source)
XLA Modules:
  0.0 28.9 jit_solution(11044510726038916128)
XLA Ops:
  0.6 0.0 copy-start
  0.6 0.9 %shard_map.67 = (f32[16,128]{1,0:T(8,128)S(1)}, f32[8,608]{1,0:T(8,128)S(1)}, bf16[4,3584]{1,0:T(4,128)(2,1)S(1)}) custom-call(s32[16]{0:T(128)} %mask_in.1, f32[8,608]{1,0:T(8,128)} %own_in.1, bf16[4,3584]{1,0:T(4,128)(2,1)} %h_in.1), custom_call_target="tpu_custom_call" | custom-call | flops 2000000000 | bytes 2097152 | tf_op jit(solution)/shard_map/pallas_call | solution.py:363
  1.6 5.1 %collective-permute-start.2 = (bf16[4,3584]{1,0:T(4,128)(2,1)S(1)}, bf16[4,3584]{1,0:T(4,128)(2,1)S(1)}, u32[]{:S(2)}, u32[]{:S(2)}) collective-permute-start(bf16[4,3584]{1,0:T(4,128)(2,1)S(1)} %get-tuple-element.22.h0), channel_id=1, source_target_pairs={{0,12},{4,8},{8,4},{12,0},{1,13},{5,9},{9,5},{13,1},{2,14},{6,10},... | collective-permute-start | bytes 86024 | tf_op jit(solution)/shard_map/ppermute | solution.py:384
  6.7 0.0 collective-permute-start.1
  6.7 0.6 %collective-permute-start = (bf16[4,3584]{1,0:T(4,128)(2,1)S(1)}, bf16[4,3584]{1,0:T(4,128)(2,1)S(1)}, u32[]{:S(2)}, u32[]{:S(2)}) collective-permute-start(bf16[4,3584]{1,0:T(4,128)(2,1)S(1)} %get-tuple-element.22.h0), channel_id=1, source_target_pairs={{0,4},{4,0},{8,12},{12,8},{1,5},{5,1},{9,13},{13,9},{2,6},{6,2},{1... | collective-permute-start | bytes 86024 | tf_op jit(solution)/shard_map/ppermute | solution.py:384
  7.3 0.0 collective-permute-start.3
  7.3 1.2 %collective-permute-done.3.got = f32[8,608]{1,0:T(8,128)S(1)} collective-permute-done((f32[8,608]{1,0:T(8,128)S(1)}, f32[8,608]{1,0:T(8,128)S(1)}, u32[]{:S(2)}, u32[]{:S(2)}) %collective-permute-start.3) | collective-permute-done | bytes 19488 | tf_op jit(solution)/shard_map/ppermute | solution.py:389
  8.5 0.2 shard_map.68
  8.8 0.0 collective-permute-done.2.h3
  8.8 2.7 %collective-permute-done.1.h2 = bf16[4,3584]{1,0:T(4,128)(2,1)S(1)} collective-permute-done((bf16[4,3584]{1,0:T(4,128)(2,1)S(1)}, bf16[4,3584]{1,0:T(4,128)(2,1)S(1)}, u32[]{:S(2)}, u32[]{:S(2)}) %collective-permute-start.1) | collective-permute-done | bytes 28704 | tf_op jit(solution)/shard_map/ppermute | solution.py:384
  11.5 0.0 collective-permute-done.h1
  11.5 0.0 copy-done
  11.5 1.3 %shard_map.69 = (f32[16,304]{1,0:T(8,128)S(1)}, f32[16,128]{1,0:T(8,128)S(1)}, bf16[16,3584]{1,0:T(8,128)(2,1)S(1)}, f32[16,3584]{1,0:T(8,128)S(1)}, f32[16,3712]{1,0:T(8,128)S(1)}) custom-call(bf16[4,3584]{1,0:T(4,128)(2,1)S(1)} %get-tuple-element.22.h0, bf16[4,3584]{1,0:T(4,128)(2,1)S(1)} %collective-permute-done.h1, ...), custom_call_target="tpu_custom_call" | custom-call | tf_op jit(solution)/shard_map/pallas_call | solution.py:363
  12.8 0.0 collective-permute-start.4
  12.8 1.5 %collective-permute-done.4.got = f32[16,3712]{1,0:T(8,128)S(1)} collective-permute-done((f32[16,3712]{1,0:T(8,128)S(1)}, f32[16,3712]{1,0:T(8,128)S(1)}, u32[]{:S(2)}, u32[]{:S(2)}) %collective-permute-start.4) | collective-permute-done | bytes 237600 | tf_op jit(solution)/shard_map/ppermute | solution.py:399
  14.3 0.2 shard_map.70
  14.5 1.6 %collective-permute-start.5 = (f32[8,3840]{1,0:T(8,128)S(1)}, f32[8,3840]{1,0:T(8,128)S(1)}, u32[]{:S(2)}, u32[]{:S(2)}) collective-permute-start(f32[8,3840]{1,0:T(8,128)S(1)} %get-tuple-element.33), channel_id=1, source_target_pairs={{0,2},{2,0},{1,3},{3,1},{4,6},{6,4},{5,7},{7,5},{8,10},{10,8},{9,1... | collective-permute-start | bytes 368648 | tf_op jit(solution)/shard_map/ppermute | solution.py:403
  16.1 3.9 %collective-permute-done.5.got = f32[8,3840]{1,0:T(8,128)S(1)} collective-permute-done((f32[8,3840]{1,0:T(8,128)S(1)}, f32[8,3840]{1,0:T(8,128)S(1)}, u32[]{:S(2)}, u32[]{:S(2)}) %collective-permute-start.5) | collective-permute-done | bytes 122912 | tf_op jit(solution)/shard_map/ppermute | solution.py:403
  19.9 0.2 shard_map.71
  20.2 1.5 %collective-permute-start.6 = (f32[2,4608]{1,0:T(2,128)S(1)}, f32[2,4608]{1,0:T(2,128)S(1)}, u32[]{:S(2)}, u32[]{:S(2)}) collective-permute-start(f32[2,4608]{1,0:T(2,128)S(1)} %get-tuple-element.36), channel_id=1, source_target_pairs={{0,12},{4,8},{8,4},{12,0},{1,13},{5,9},{9,5},{13,1},{2,14},{6,10},... | collective-permute-start | bytes 110600 | tf_op jit(solution)/shard_map/ppermute | solution.py:409
  21.7 0.6 %collective-permute-start.7 = (f32[2,4608]{1,0:T(2,128)S(1)}, f32[2,4608]{1,0:T(2,128)S(1)}, u32[]{:S(2)}, u32[]{:S(2)}) collective-permute-start(f32[2,4608]{1,0:T(2,128)S(1)} %get-tuple-element.37), channel_id=1, source_target_pairs={{0,8},{4,12},{8,0},{12,4},{1,9},{5,13},{9,1},{13,5},{2,10},{6,14},... | collective-permute-start | bytes 110600 | tf_op jit(solution)/shard_map/ppermute | solution.py:409
  22.3 2.3 %collective-permute-start.8 = (f32[2,4608]{1,0:T(2,128)S(1)}, f32[2,4608]{1,0:T(2,128)S(1)}, u32[]{:S(2)}, u32[]{:S(2)}) collective-permute-start(f32[2,4608]{1,0:T(2,128)S(1)} %get-tuple-element.38), channel_id=1, source_target_pairs={{0,4},{4,0},{8,12},{12,8},{1,5},{5,1},{9,13},{13,9},{2,6},{6,2},{1... | collective-permute-start | bytes 110600 | tf_op jit(solution)/shard_map/ppermute | solution.py:409
  24.6 1.6 %collective-permute-done.6.got3 = f32[2,4608]{1,0:T(2,128)S(1)} collective-permute-done((f32[2,4608]{1,0:T(2,128)S(1)}, f32[2,4608]{1,0:T(2,128)S(1)}, u32[]{:S(2)}, u32[]{:S(2)}) %collective-permute-start.6) | collective-permute-done | bytes 36896 | tf_op jit(solution)/shard_map/ppermute | solution.py:409
  26.2 0.4 %collective-permute-done.7.got2 = f32[2,4608]{1,0:T(2,128)S(1)} collective-permute-done((f32[2,4608]{1,0:T(2,128)S(1)}, f32[2,4608]{1,0:T(2,128)S(1)}, u32[]{:S(2)}, u32[]{:S(2)}) %collective-permute-start.7) | collective-permute-done | bytes 36896 | tf_op jit(solution)/shard_map/ppermute | solution.py:409
  26.6 0.4 %collective-permute-done.8.got1 = f32[2,4608]{1,0:T(2,128)S(1)} collective-permute-done((f32[2,4608]{1,0:T(2,128)S(1)}, f32[2,4608]{1,0:T(2,128)S(1)}, u32[]{:S(2)}, u32[]{:S(2)}) %collective-permute-start.8) | collective-permute-done | bytes 36896 | tf_op jit(solution)/shard_map/ppermute | solution.py:409
  27.0 2.0 %shard_map.72 = (f32[16]{0:T(128)}, bf16[1,3584]{1,0:T(2,128)(2,1)}, bf16[304,3584]{1,0:T(8,128)(2,1)}) custom-call(f32[2,3584]{1,0:T(2,128)S(1)} %get-tuple-element.34.part, f32[16,128]{1,0:T(8,128)S(1)} %get-tuple-element.35.stats, f32[2,4608]{1,0:T(2,128)S(1)} %collective-permute-done.6.got3, f32[2,4608]{1,0:T(2,128)S(1)} %collective-permute-done.7.got2, ...), custom_call_target="tpu_custom_call" | custom-call | tf_op jit(solution)/shard_map/pallas_call | solution.py:363
Async XLA Ops:
  0.6 10.8 %copy-start = (bf16[304,3584]{1,0:T(8,128)(2,1)S(1)}, bf16[304,3584]{1,0:T(8,128)(2,1)}, u32[]{:S(2)}) copy-start(bf16[304,3584]{1,0:T(8,128)(2,1)} %w.1) | copy-start | bytes 6537220
  1.6 7.2 %collective-permute-start.2 = (bf16[4,3584]{1,0:T(4,128)(2,1)S(1)}, bf16[4,3584]{1,0:T(4,128)(2,1)S(1)}, u32[]{:S(2)}, u32[]{:S(2)}) collective-permute-start(bf16[4,3584]{1,0:T(4,128)(2,1)S(1)} %get-tuple-element.22.h0), channel_id=1, source_target_pairs={{0,12},{4,8},{8,4},{12,0},{1,13},{5,9},{9,5},{13,1},{2,14},{6,10},... | collective-permute-start | bytes 86024 | tf_op jit(solution)/shard_map/ppermute | solution.py:384
  6.7 4.8 %collective-permute-start.1 = (bf16[4,3584]{1,0:T(4,128)(2,1)S(1)}, bf16[4,3584]{1,0:T(4,128)(2,1)S(1)}, u32[]{:S(2)}, u32[]{:S(2)}) collective-permute-start(bf16[4,3584]{1,0:T(4,128)(2,1)S(1)} %get-tuple-element.22.h0), channel_id=1, source_target_pairs={{0,8},{4,12},{8,0},{12,4},{1,9},{5,13},{9,1},{13,5},{2,10},{6,14},... | collective-permute-start | bytes 86024 | tf_op jit(solution)/shard_map/ppermute | solution.py:384
  6.7 4.8 %collective-permute-start = (bf16[4,3584]{1,0:T(4,128)(2,1)S(1)}, bf16[4,3584]{1,0:T(4,128)(2,1)S(1)}, u32[]{:S(2)}, u32[]{:S(2)}) collective-permute-start(bf16[4,3584]{1,0:T(4,128)(2,1)S(1)} %get-tuple-element.22.h0), channel_id=1, source_target_pairs={{0,4},{4,0},{8,12},{12,8},{1,5},{5,1},{9,13},{13,9},{2,6},{6,2},{1... | collective-permute-start | bytes 86024 | tf_op jit(solution)/shard_map/ppermute | solution.py:384
  7.3 1.2 %collective-permute-start.3 = (f32[8,608]{1,0:T(8,128)S(1)}, f32[8,608]{1,0:T(8,128)S(1)}, u32[]{:S(2)}, u32[]{:S(2)}) collective-permute-start(f32[8,608]{1,0:T(8,128)S(1)} %get-tuple-element.24.own), channel_id=1, source_target_pairs={{0,1},{1,0},{2,3},{3,2},{4,5},{5,4},{6,7},{7,6},{8,9},{9,8},{10,11... | collective-permute-start | bytes 58376 | tf_op jit(solution)/shard_map/ppermute | solution.py:389
  12.8 1.5 %collective-permute-start.4 = (f32[16,3712]{1,0:T(8,128)S(1)}, f32[16,3712]{1,0:T(8,128)S(1)}, u32[]{:S(2)}, u32[]{:S(2)}) collective-permute-start(f32[16,3712]{1,0:T(8,128)S(1)} %get-tuple-element.30), channel_id=1, source_target_pairs={{0,1},{1,0},{2,3},{3,2},{4,5},{5,4},{6,7},{7,6},{8,9},{9,8},{10,11... | collective-permute-start | bytes 712712 | tf_op jit(solution)/shard_map/ppermute | solution.py:399
  14.5 5.4 %collective-permute-start.5 = (f32[8,3840]{1,0:T(8,128)S(1)}, f32[8,3840]{1,0:T(8,128)S(1)}, u32[]{:S(2)}, u32[]{:S(2)}) collective-permute-start(f32[8,3840]{1,0:T(8,128)S(1)} %get-tuple-element.33), channel_id=1, source_target_pairs={{0,2},{2,0},{1,3},{3,1},{4,6},{6,4},{5,7},{7,5},{8,10},{10,8},{9,1... | collective-permute-start | bytes 368648 | tf_op jit(solution)/shard_map/ppermute | solution.py:403
  20.2 6.0 %collective-permute-start.6 = (f32[2,4608]{1,0:T(2,128)S(1)}, f32[2,4608]{1,0:T(2,128)S(1)}, u32[]{:S(2)}, u32[]{:S(2)}) collective-permute-start(f32[2,4608]{1,0:T(2,128)S(1)} %get-tuple-element.36), channel_id=1, source_target_pairs={{0,12},{4,8},{8,4},{12,0},{1,13},{5,9},{9,5},{13,1},{2,14},{6,10},... | collective-permute-start | bytes 110600 | tf_op jit(solution)/shard_map/ppermute | solution.py:409
  21.7 4.9 %collective-permute-start.7 = (f32[2,4608]{1,0:T(2,128)S(1)}, f32[2,4608]{1,0:T(2,128)S(1)}, u32[]{:S(2)}, u32[]{:S(2)}) collective-permute-start(f32[2,4608]{1,0:T(2,128)S(1)} %get-tuple-element.37), channel_id=1, source_target_pairs={{0,8},{4,12},{8,0},{12,4},{1,9},{5,13},{9,1},{13,5},{2,10},{6,14},... | collective-permute-start | bytes 110600 | tf_op jit(solution)/shard_map/ppermute | solution.py:409
  22.3 4.6 %collective-permute-start.8 = (f32[2,4608]{1,0:T(2,128)S(1)}, f32[2,4608]{1,0:T(2,128)S(1)}, u32[]{:S(2)}, u32[]{:S(2)}) collective-permute-start(f32[2,4608]{1,0:T(2,128)S(1)} %get-tuple-element.38), channel_id=1, source_target_pairs={{0,4},{4,0},{8,12},{12,8},{1,5},{5,1},{9,13},{13,9},{2,6},{6,2},{1... | collective-permute-start | bytes 110600 | tf_op jit(solution)/shard_map/ppermute | solution.py:409

commit v8 on v7

--- a/solution.py
+++ b/solution.py
@@ -257,7 +257,7 @@
         send[8:16, d:] = st[0:8]
 
 
-def second_kernel(part, stats, got, stats_out, keep, send):
+def second_kernel(part, stats, got, stats_out, keep, send3, send2, send1):
     d = part.shape[1]
     factors, columns = unite([stats[...], got[:, d:]])
     st = pack(columns)
@@ -266,46 +266,52 @@
         jnp.concatenate([f[0:4, 0:1], f[0:4, 1:2], f[4:8, 0:1], f[4:8, 1:2]], 0) for f in factors
     ]
     total = part[...] * scale[0] + got[:, 0:d] * scale[1]
-    keep[...] = total[0:8]
-    send[:, 0:d] = total[8:16]
-    for i in range(2):
-        send[0:4, d + 128 * i : d + 128 * i + 128] = st[8 * i + 4 : 8 * i + 8]
-        send[4:8, d + 128 * i : d + 128 * i + 128] = st[8 * i : 8 * i + 4]
-
-
-def third_kernel(part, stats, got, stats_out, keep, send3, send2, send1, gs):
+    for i in range(4):
+        keep[i : i + 1, :] = total[4 * i : 4 * i + 1]
+    for k, send in ((3, send3), (2, send2), (1, send1)):
+        for i in range(4):
+            send[i : i + 1, 0:d] = total[4 * i + k : 4 * i + k + 1]
+        for p in range(ROWS):
+            at = d + 128 * (p // 4)
+            r = p ^ k
+            send[p % 4 : p % 4 + 1, at : at + 128] = st[r : r + 1]
+
+
+def third_kernel(part, stats, got3, got2, got1, stats_out, keep, send, gs):
     d = part.shape[1]
-    for i in range(2):
-        gs[8 * i : 8 * i + 8, :] = got[:, d + 128 * i : d + 128 * i + 128]
-    factors, columns = unite([stats[...], gs[...]])
+    parts = [stats[...]]
+    gots = (got1, got2, got3)
+    for k, got in enumerate(gots):
+        for i in range(4):
+            gs[k, 4 * i : 4 * i + 4, :] = got[:, d + 128 * i : d + 128 * i + 128]
+        parts.append(gs[k])
+    factors, columns = unite(parts)
     st = pack(columns)
     stats_out[...] = st
-    scale = [jnp.concatenate([f[0:4, 0:1], f[0:4, 1:2]], 0) for f in factors]
-    total = part[...] * scale[0] + got[:, 0:d] * scale[1]
-    keep[0:1, :] = total[0:1]
-    keep[1:2, :] = total[4:5]
-    for k, send in enumerate((send1, send2, send3), 1):
-        send[0:1, 0:d] = total[k : k + 1]
-        send[1:2, 0:d] = total[4 + k : 5 + k]
-        for p in range(ROWS):
-            at = d + 128 * (p // 2)
-            r = p ^ k
-            send[p % 2 : p % 2 + 1, at : at + 128] = st[r : r + 1]
+    scale = [
+        jnp.concatenate([f[0:1, 0:1], f[0:1, 1:2], f[4:5, 0:1], f[4:5, 1:2]], 0) for f in factors
+    ]
+    total = part[...] * scale[0]
+    for got, f in zip(gots, scale[1:]):
+        total = total + got[:, 0:d] * f
+    keep[...] = total[0:2]
+    send[:, 0:d] = total[2:4]
+    for p in range(ROWS):
+        at = d + 128 * (p // 2)
+        r = p ^ 4
+        send[p % 2 : p % 2 + 1, at : at + 128] = st[r : r + 1]
 
 
 def make_last_kernel(chunk):
     def last_kernel(
-        part, stats, got3, got2, got1, student, scaled, hb,
+        part, stats, got, student, scaled, hb,
         divergence, hidden_grad, weight_grad, gs, gr, out, div, hid, sems,
     ):
         z, x, c = places()
         d = part.shape[1]
-        parts = [stats[...]]
-        for k, got in enumerate((got1, got2, got3)):
-            for i in range(8):
-                gs[k, 2 * i : 2 * i + 2, :] = got[:, d + 128 * i : d + 128 * i + 128]
-            parts.append(gs[k])
-        factors, (ms, mt, ls, lt, cross, valid) = unite(parts)
+        for i in range(8):
+            gs[2 * i : 2 * i + 2, :] = got[:, d + 128 * i : d + 128 * i + 128]
+        factors, (ms, mt, ls, lt, cross, valid) = unite([stats[...], gs[...]])
         lse_s = ms + jnp.log(ls)
         lse_t = mt + jnp.log(lt)
         gain = valid * (objective_scale * smoothing_divisor)
@@ -338,11 +344,9 @@
         lane = lax.broadcasted_iota(jnp.int32, (ROWS, STATS), 1)
         div[...] = jnp.sum(jnp.where(lane == home, value, 0.0), axis=0)[0:ROWS]
         emit(div, divergence)
-        a_s = part[0:1, :] * factors[0][0:1, 0:1]
-        a_t = part[1:2, :] * factors[0][0:1, 1:2]
-        for got, f in zip((got1, got2, got3), factors[1:]):
-            a_s = a_s + got[0:1, 0:d] * f[0:1, 0:1]
-            a_t = a_t + got[1:2, 0:d] * f[0:1, 1:2]
+        own, other = factors
+        a_s = part[0:1, :] * own[0:1, 0:1] + got[0:1, 0:d] * other[0:1, 0:1]
+        a_t = part[1:2, :] * own[0:1, 1:2] + got[1:2, 0:d] * other[0:1, 1:2]
         hid[...] = (gain[0:1] * (a_s / ls[0:1] - a_t / lt[0:1])).astype(jnp.bfloat16)
         emit(hid, hidden_grad)
         for i in range(n // 2, n):
@@ -397,32 +401,33 @@
         ],
     )(own, *pieces, head_weight, scaled, et, teacher)
     got = lax.ppermute(send, "teach", flip(2, 1))
-    stats, keep, send = call(
-        second_kernel, [((ROWS, STATS), f32), ((8, d), f32), ((8, d + 2 * STATS), f32)]
-    )(keep, stats, got)
-    got = lax.ppermute(send, "rows", flip(2, 1))
     stats, keep, *sends = call(
-        third_kernel,
-        [((ROWS, STATS), f32), ((2, d), f32)] + [((2, d + 8 * STATS), f32)] * 3,
-        [pltpu.VMEM((ROWS, STATS), f32)],
+        second_kernel,
+        [((ROWS, STATS), f32), ((4, d), f32)] + [((4, d + 4 * STATS), f32)] * 3,
     )(keep, stats, got)
     gots = [lax.ppermute(a, "vocab", flip(4, k)) for k, a in zip((3, 2, 1), sends)]
+    stats, keep, send = call(
+        third_kernel,
+        [((ROWS, STATS), f32), ((2, d), f32), ((2, d + 8 * STATS), f32)],
+        [pltpu.VMEM((3, ROWS, STATS), f32)],
+    )(keep, stats, *gots)
+    got = lax.ppermute(send, "rows", flip(2, 1))
     chunk = 512
     return tuple(
         call(
             make_last_kernel(chunk),
             [((ROWS,), f32), ((1, d), bf16), ((v, d), bf16)],
             [
-                pltpu.VMEM((3, ROWS, STATS), f32),
+                pltpu.VMEM((ROWS, STATS), f32),
                 pltpu.VMEM((ROWS, v), f32),
                 pltpu.VMEM((v, d), bf16),
                 pltpu.VMEM((ROWS,), f32),
                 pltpu.VMEM((1, d), bf16),
                 pltpu.SemaphoreType.DMA((d // chunk + 2,)),
             ],
-            [VMEM] * 8,
+            [VMEM] * 6,
             [ANY] * 3,
-        )(keep, stats, *gots, student, scaled, hb)
+        )(keep, stats, got, student, scaled, hb)
     )
 
 

time: 29.1 us -> 29.7 us (1.021)
  waiting for transfers between devices: 11.6 us -> 12.2 us
    ppermute x3, waiting for transfers between devices: 2.35 us -> 4.35 us  [small_body(): lax.ppermute(a, 'vocab', flip(4, k))]
    ppermute x1, waiting for transfers between devices: 3.87 us -> 2.47 us  [small_body(): got = lax.ppermute(send, 'rows', flip(2, 1))]
  transfers between devices with their start and end apart: 9 -> 9, of which waited for: 7 -> 6; matrix products, arithmetic and copies ran while one was open for 0% -> 0% of each run, Pallas kernels for 1% -> 1%
where the time goes in v8:
time: 29.7 us; the launch traced here: 29.5 us
  waiting for transfers between devices  12.2 us (41%)
  starting transfers between devices  11.8 us (40%)
  Pallas kernels  4.88 us (16%)
  between operations  0.68 us (2%)
    ppermute x3, starting transfers between devices, small_body(): pieces = [lax.ppermute(own, 'vocab', flip(4, k)) for k in (1, 2, 3)]  5.76 us
    pallas_call x6, Pallas kernels, call(): pl.pallas_call(kernel, out_shape=shapes, in_specs=in_specs or [VMEM] * le...  4.88 us
    ppermute x3, starting transfers between devices, small_body(): lax.ppermute(a, 'vocab', flip(4, k))  4.45 us
    ppermute x3, waiting for transfers between devices, small_body(): lax.ppermute(a, 'vocab', flip(4, k))  4.35 us
    ppermute x3, waiting for transfers between devices, small_body(): pieces = [lax.ppermute(own, 'vocab', flip(4, k)) for k in (1, 2, 3)]  2.69 us
    ppermute x1, waiting for transfers between devices, small_body(): got = lax.ppermute(send, 'rows', flip(2, 1))  2.47 us
    ppermute x1, starting transfers between devices, small_body(): got = lax.ppermute(send, 'rows', flip(2, 1))  1.55 us
    ppermute x1, waiting for transfers between devices, small_body(): got = lax.ppermute(send, 'teach', flip(2, 1))  1.49 us
  transfers between devices with their start and end apart: 9, of which 6 were waited for; matrix products, arithmetic and copies ran while one was open for 0% of the time, Pallas kernels for 1%

profile of v8, /device:TPU:0, one launch (start us, length us, event | category | flops | bytes accessed | tf_op | source)
XLA Modules:
  0.0 29.5 jit_solution(5868104187066623097)
XLA Ops:
  0.6 0.0 copy-start
  0.6 0.9 %shard_map.67 = (f32[16,128]{1,0:T(8,128)S(1)}, f32[8,608]{1,0:T(8,128)S(1)}, bf16[4,3584]{1,0:T(4,128)(2,1)S(1)}) custom-call(s32[16]{0:T(128)} %mask_in.1, f32[8,608]{1,0:T(8,128)} %own_in.1, bf16[4,3584]{1,0:T(4,128)(2,1)} %h_in.1), custom_call_target="tpu_custom_call" | custom-call | flops 2000000000 | bytes 2097152 | tf_op jit(solution)/shard_map/pallas_call | solution.py:367
  1.6 5.1 %collective-permute-start.2 = (bf16[4,3584]{1,0:T(4,128)(2,1)S(1)}, bf16[4,3584]{1,0:T(4,128)(2,1)S(1)}, u32[]{:S(2)}, u32[]{:S(2)}) collective-permute-start(bf16[4,3584]{1,0:T(4,128)(2,1)S(1)} %get-tuple-element.22.h0), channel_id=1, source_target_pairs={{0,12},{4,8},{8,4},{12,0},{1,13},{5,9},{9,5},{13,1},{2,14},{6,10},... | collective-permute-start | bytes 86024 | tf_op jit(solution)/shard_map/ppermute | solution.py:388
  6.7 0.0 collective-permute-start.1
  6.7 0.6 %collective-permute-start = (bf16[4,3584]{1,0:T(4,128)(2,1)S(1)}, bf16[4,3584]{1,0:T(4,128)(2,1)S(1)}, u32[]{:S(2)}, u32[]{:S(2)}) collective-permute-start(bf16[4,3584]{1,0:T(4,128)(2,1)S(1)} %get-tuple-element.22.h0), channel_id=1, source_target_pairs={{0,4},{4,0},{8,12},{12,8},{1,5},{5,1},{9,13},{13,9},{2,6},{6,2},{1... | collective-permute-start | bytes 86024 | tf_op jit(solution)/shard_map/ppermute | solution.py:388
  7.3 0.0 collective-permute-start.3
  7.3 1.2 %collective-permute-done.3.got = f32[8,608]{1,0:T(8,128)S(1)} collective-permute-done((f32[8,608]{1,0:T(8,128)S(1)}, f32[8,608]{1,0:T(8,128)S(1)}, u32[]{:S(2)}, u32[]{:S(2)}) %collective-permute-start.3) | collective-permute-done | bytes 19488 | tf_op jit(solution)/shard_map/ppermute | solution.py:393
  8.5 0.2 shard_map.68
  8.8 0.0 collective-permute-done.2.h3
  8.8 2.7 %collective-permute-done.1.h2 = bf16[4,3584]{1,0:T(4,128)(2,1)S(1)} collective-permute-done((bf16[4,3584]{1,0:T(4,128)(2,1)S(1)}, bf16[4,3584]{1,0:T(4,128)(2,1)S(1)}, u32[]{:S(2)}, u32[]{:S(2)}) %collective-permute-start.1) | collective-permute-done | bytes 28704 | tf_op jit(solution)/shard_map/ppermute | solution.py:388
  11.5 0.0 collective-permute-done.h1
  11.5 0.0 copy-done
  11.5 1.3 %shard_map.69 = (f32[16,304]{1,0:T(8,128)S(1)}, f32[16,128]{1,0:T(8,128)S(1)}, bf16[16,3584]{1,0:T(8,128)(2,1)S(1)}, f32[16,3584]{1,0:T(8,128)S(1)}, f32[16,3712]{1,0:T(8,128)S(1)}) custom-call(bf16[4,3584]{1,0:T(4,128)(2,1)S(1)} %get-tuple-element.22.h0, bf16[4,3584]{1,0:T(4,128)(2,1)S(1)} %collective-permute-done.h1, ...), custom_call_target="tpu_custom_call" | custom-call | tf_op jit(solution)/shard_map/pallas_call | solution.py:367
  12.8 0.0 collective-permute-start.4
  12.8 1.5 %collective-permute-done.4.got = f32[16,3712]{1,0:T(8,128)S(1)} collective-permute-done((f32[16,3712]{1,0:T(8,128)S(1)}, f32[16,3712]{1,0:T(8,128)S(1)}, u32[]{:S(2)}, u32[]{:S(2)}) %collective-permute-start.4) | collective-permute-done | bytes 237600 | tf_op jit(solution)/shard_map/ppermute | solution.py:403
  14.3 0.2 shard_map.70
  14.6 1.5 %collective-permute-start.5 = (f32[4,4096]{1,0:T(4,128)S(1)}, f32[4,4096]{1,0:T(4,128)S(1)}, u32[]{:S(2)}, u32[]{:S(2)}) collective-permute-start(f32[4,4096]{1,0:T(4,128)S(1)} %get-tuple-element.33), channel_id=1, source_target_pairs={{0,12},{4,8},{8,4},{12,0},{1,13},{5,9},{9,5},{13,1},{2,14},{6,10},... | collective-permute-start | bytes 196616 | tf_op jit(solution)/shard_map/ppermute | solution.py:408
  16.1 0.6 %collective-permute-start.6 = (f32[4,4096]{1,0:T(4,128)S(1)}, f32[4,4096]{1,0:T(4,128)S(1)}, u32[]{:S(2)}, u32[]{:S(2)}) collective-permute-start(f32[4,4096]{1,0:T(4,128)S(1)} %get-tuple-element.34), channel_id=1, source_target_pairs={{0,8},{4,12},{8,0},{12,4},{1,9},{5,13},{9,1},{13,5},{2,10},{6,14},... | collective-permute-start | bytes 196616 | tf_op jit(solution)/shard_map/ppermute | solution.py:408
  16.7 2.3 %collective-permute-start.7 = (f32[4,4096]{1,0:T(4,128)S(1)}, f32[4,4096]{1,0:T(4,128)S(1)}, u32[]{:S(2)}, u32[]{:S(2)}) collective-permute-start(f32[4,4096]{1,0:T(4,128)S(1)} %get-tuple-element.35), channel_id=1, source_target_pairs={{0,4},{4,0},{8,12},{12,8},{1,5},{5,1},{9,13},{13,9},{2,6},{6,2},{1... | collective-permute-start | bytes 196616 | tf_op jit(solution)/shard_map/ppermute | solution.py:408
  19.0 2.4 %collective-permute-done.5.got3 = f32[4,4096]{1,0:T(4,128)S(1)} collective-permute-done((f32[4,4096]{1,0:T(4,128)S(1)}, f32[4,4096]{1,0:T(4,128)S(1)}, u32[]{:S(2)}, u32[]{:S(2)}) %collective-permute-start.5) | collective-permute-done | bytes 65568 | tf_op jit(solution)/shard_map/ppermute | solution.py:408
  21.4 2.0 %collective-permute-done.6.got2 = f32[4,4096]{1,0:T(4,128)S(1)} collective-permute-done((f32[4,4096]{1,0:T(4,128)S(1)}, f32[4,4096]{1,0:T(4,128)S(1)}, u32[]{:S(2)}, u32[]{:S(2)}) %collective-permute-start.6) | collective-permute-done | bytes 65568 | tf_op jit(solution)/shard_map/ppermute | solution.py:408
  23.4 0.0 collective-permute-done.7.got1
  23.4 0.2 shard_map.71
  23.6 1.6 %collective-permute-start.8 = (f32[2,4608]{1,0:T(2,128)S(1)}, f32[2,4608]{1,0:T(2,128)S(1)}, u32[]{:S(2)}, u32[]{:S(2)}) collective-permute-start(f32[2,4608]{1,0:T(2,128)S(1)} %get-tuple-element.38), channel_id=1, source_target_pairs={{0,2},{2,0},{1,3},{3,1},{4,6},{6,4},{5,7},{7,5},{8,10},{10,8},{9,1... | collective-permute-start | bytes 110600 | tf_op jit(solution)/shard_map/ppermute | solution.py:414
  25.1 2.5 %collective-permute-done.8.got = f32[2,4608]{1,0:T(2,128)S(1)} collective-permute-done((f32[2,4608]{1,0:T(2,128)S(1)}, f32[2,4608]{1,0:T(2,128)S(1)}, u32[]{:S(2)}, u32[]{:S(2)}) %collective-permute-start.8) | collective-permute-done | bytes 36896 | tf_op jit(solution)/shard_map/ppermute | solution.py:414
  27.6 1.9 %shard_map.72 = (f32[16]{0:T(128)}, bf16[1,3584]{1,0:T(2,128)(2,1)}, bf16[304,3584]{1,0:T(8,128)(2,1)}) custom-call(f32[2,3584]{1,0:T(2,128)S(1)} %get-tuple-element.36.part, f32[16,128]{1,0:T(8,128)S(1)} %get-tuple-element.37.stats, f32[2,4608]{1,0:T(2,128)S(1)} %collective-permute-done.8.got, f32[16,304]{1,0:T(8,128)S(1)} %get-tuple-element.39.student, ...), custom_call_target="tpu_custom_call" | custom-call | tf_op jit(solution)/shard_map/pallas_call | solution.py:367
Async XLA Ops:
  0.6 10.8 %copy-start = (bf16[304,3584]{1,0:T(8,128)(2,1)S(1)}, bf16[304,3584]{1,0:T(8,128)(2,1)}, u32[]{:S(2)}) copy-start(bf16[304,3584]{1,0:T(8,128)(2,1)} %w.1) | copy-start | bytes 6537220
  1.6 7.2 %collective-permute-start.2 = (bf16[4,3584]{1,0:T(4,128)(2,1)S(1)}, bf16[4,3584]{1,0:T(4,128)(2,1)S(1)}, u32[]{:S(2)}, u32[]{:S(2)}) collective-permute-start(bf16[4,3584]{1,0:T(4,128)(2,1)S(1)} %get-tuple-element.22.h0), channel_id=1, source_target_pairs={{0,12},{4,8},{8,4},{12,0},{1,13},{5,9},{9,5},{13,1},{2,14},{6,10},... | collective-permute-start | bytes 86024 | tf_op jit(solution)/shard_map/ppermute | solution.py:388
  6.7 4.8 %collective-permute-start.1 = (bf16[4,3584]{1,0:T(4,128)(2,1)S(1)}, bf16[4,3584]{1,0:T(4,128)(2,1)S(1)}, u32[]{:S(2)}, u32[]{:S(2)}) collective-permute-start(bf16[4,3584]{1,0:T(4,128)(2,1)S(1)} %get-tuple-element.22.h0), channel_id=1, source_target_pairs={{0,8},{4,12},{8,0},{12,4},{1,9},{5,13},{9,1},{13,5},{2,10},{6,14},... | collective-permute-start | bytes 86024 | tf_op jit(solution)/shard_map/ppermute | solution.py:388
  6.7 4.8 %collective-permute-start = (bf16[4,3584]{1,0:T(4,128)(2,1)S(1)}, bf16[4,3584]{1,0:T(4,128)(2,1)S(1)}, u32[]{:S(2)}, u32[]{:S(2)}) collective-permute-start(bf16[4,3584]{1,0:T(4,128)(2,1)S(1)} %get-tuple-element.22.h0), channel_id=1, source_target_pairs={{0,4},{4,0},{8,12},{12,8},{1,5},{5,1},{9,13},{13,9},{2,6},{6,2},{1... | collective-permute-start | bytes 86024 | tf_op jit(solution)/shard_map/ppermute | solution.py:388
  7.3 1.2 %collective-permute-start.3 = (f32[8,608]{1,0:T(8,128)S(1)}, f32[8,608]{1,0:T(8,128)S(1)}, u32[]{:S(2)}, u32[]{:S(2)}) collective-permute-start(f32[8,608]{1,0:T(8,128)S(1)} %get-tuple-element.24.own), channel_id=1, source_target_pairs={{0,1},{1,0},{2,3},{3,2},{4,5},{5,4},{6,7},{7,6},{8,9},{9,8},{10,11... | collective-permute-start | bytes 58376 | tf_op jit(solution)/shard_map/ppermute | solution.py:393
  12.8 1.5 %collective-permute-start.4 = (f32[16,3712]{1,0:T(8,128)S(1)}, f32[16,3712]{1,0:T(8,128)S(1)}, u32[]{:S(2)}, u32[]{:S(2)}) collective-permute-start(f32[16,3712]{1,0:T(8,128)S(1)} %get-tuple-element.30), channel_id=1, source_target_pairs={{0,1},{1,0},{2,3},{3,2},{4,5},{5,4},{6,7},{7,6},{8,9},{9,8},{10,11... | collective-permute-start | bytes 712712 | tf_op jit(solution)/shard_map/ppermute | solution.py:403
  14.6 6.8 %collective-permute-start.5 = (f32[4,4096]{1,0:T(4,128)S(1)}, f32[4,4096]{1,0:T(4,128)S(1)}, u32[]{:S(2)}, u32[]{:S(2)}) collective-permute-start(f32[4,4096]{1,0:T(4,128)S(1)} %get-tuple-element.33), channel_id=1, source_target_pairs={{0,12},{4,8},{8,4},{12,0},{1,13},{5,9},{9,5},{13,1},{2,14},{6,10},... | collective-permute-start | bytes 196616 | tf_op jit(solution)/shard_map/ppermute | solution.py:408
  16.1 7.3 %collective-permute-start.6 = (f32[4,4096]{1,0:T(4,128)S(1)}, f32[4,4096]{1,0:T(4,128)S(1)}, u32[]{:S(2)}, u32[]{:S(2)}) collective-permute-start(f32[4,4096]{1,0:T(4,128)S(1)} %get-tuple-element.34), channel_id=1, source_target_pairs={{0,8},{4,12},{8,0},{12,4},{1,9},{5,13},{9,1},{13,5},{2,10},{6,14},... | collective-permute-start | bytes 196616 | tf_op jit(solution)/shard_map/ppermute | solution.py:408
  16.7 6.6 %collective-permute-start.7 = (f32[4,4096]{1,0:T(4,128)S(1)}, f32[4,4096]{1,0:T(4,128)S(1)}, u32[]{:S(2)}, u32[]{:S(2)}) collective-permute-start(f32[4,4096]{1,0:T(4,128)S(1)} %get-tuple-element.35), channel_id=1, source_target_pairs={{0,4},{4,0},{8,12},{12,8},{1,5},{5,1},{9,13},{13,9},{2,6},{6,2},{1... | collective-permute-start | bytes 196616 | tf_op jit(solution)/shard_map/ppermute | solution.py:408
  23.6 4.0 %collective-permute-start.8 = (f32[2,4608]{1,0:T(2,128)S(1)}, f32[2,4608]{1,0:T(2,128)S(1)}, u32[]{:S(2)}, u32[]{:S(2)}) collective-permute-start(f32[2,4608]{1,0:T(2,128)S(1)} %get-tuple-element.38), channel_id=1, source_target_pairs={{0,2},{2,0},{1,3},{3,1},{4,6},{6,4},{5,7},{7,5},{8,10},{10,8},{9,1... | collective-permute-start | bytes 110600 | tf_op jit(solution)/shard_map/ppermute | solution.py:414

commit v9 on v7

--- a/solution.py
+++ b/solution.py
@@ -169,6 +169,23 @@
     lt = sum(s[:, 3:4] * f[:, 1:2] for s, f in zip(parts, factors))
     cross = sum(s[:, 4:5] * f[:, 1:2] for s, f in zip(parts, factors))
     return factors, [top[:, 0:1], top[:, 1:2], ls, lt, cross, top[:, 5:6]]
+
+
+def fold(st, rows):
+    shift = STATS // 2
+    while st.shape[0] > rows:
+        half = st.shape[0] // 2
+        st = st[0:half] + pltpu.roll(st[half:], shift, 1)
+        shift //= 2
+    return st
+
+
+def unfold(target, block, flipped):
+    rows = block.shape[0]
+    step = STATS * rows // ROWS
+    for i in range(ROWS // rows):
+        at = (i * rows) ^ flipped
+        target[at : at + rows, :] = block if i == 0 else pltpu.roll(block, STATS - step * i, 1)
 
 
 def places():
@@ -268,15 +285,14 @@
     total = part[...] * scale[0] + got[:, 0:d] * scale[1]
     keep[...] = total[0:8]
     send[:, 0:d] = total[8:16]
-    for i in range(2):
-        send[0:4, d + 128 * i : d + 128 * i + 128] = st[8 * i + 4 : 8 * i + 8]
-        send[4:8, d + 128 * i : d + 128 * i + 128] = st[8 * i : 8 * i + 4]
+    block = fold(st, 8)
+    send[0:4, d:] = block[4:8]
+    send[4:8, d:] = block[0:4]
 
 
 def third_kernel(part, stats, got, stats_out, keep, send3, send2, send1, gs):
     d = part.shape[1]
-    for i in range(2):
-        gs[8 * i : 8 * i + 8, :] = got[:, d + 128 * i : d + 128 * i + 128]
+    unfold(gs, got[:, d:], 0)
     factors, columns = unite([stats[...], gs[...]])
     st = pack(columns)
     stats_out[...] = st
@@ -284,13 +300,13 @@
     total = part[...] * scale[0] + got[:, 0:d] * scale[1]
     keep[0:1, :] = total[0:1]
     keep[1:2, :] = total[4:5]
+    block = fold(st, 2)
     for k, send in enumerate((send1, send2, send3), 1):
         send[0:1, 0:d] = total[k : k + 1]
         send[1:2, 0:d] = total[4 + k : 5 + k]
-        for p in range(ROWS):
-            at = d + 128 * (p // 2)
-            r = p ^ k
-            send[p % 2 : p % 2 + 1, at : at + 128] = st[r : r + 1]
+        for i in range(2):
+            r = i ^ (k & 1)
+            send[i : i + 1, d:] = block[r : r + 1]
 
 
 def make_last_kernel(chunk):
@@ -302,8 +318,7 @@
         d = part.shape[1]
         parts = [stats[...]]
         for k, got in enumerate((got1, got2, got3)):
-            for i in range(8):
-                gs[k, 2 * i : 2 * i + 2, :] = got[:, d + 128 * i : d + 128 * i + 128]
+            unfold(gs.at[k], got[:, d:], (k + 1) & 2)
             parts.append(gs[k])
         factors, (ms, mt, ls, lt, cross, valid) = unite(parts)
         lse_s = ms + jnp.log(ls)
@@ -398,12 +413,12 @@
     )(own, *pieces, head_weight, scaled, et, teacher)
     got = lax.ppermute(send, "teach", flip(2, 1))
     stats, keep, send = call(
-        second_kernel, [((ROWS, STATS), f32), ((8, d), f32), ((8, d + 2 * STATS), f32)]
+        second_kernel, [((ROWS, STATS), f32), ((8, d), f32), ((8, d + STATS), f32)]
     )(keep, stats, got)
     got = lax.ppermute(send, "rows", flip(2, 1))
     stats, keep, *sends = call(
         third_kernel,
-        [((ROWS, STATS), f32), ((2, d), f32)] + [((2, d + 8 * STATS), f32)] * 3,
+        [((ROWS, STATS), f32), ((2, d), f32)] + [((2, d + STATS), f32)] * 3,
         [pltpu.VMEM((ROWS, STATS), f32)],
     )(keep, stats, got)
     gots = [lax.ppermute(a, "vocab", flip(4, k)) for k, a in zip((3, 2, 1), sends)]

time: 29.1 us -> 29.1 us (level)
  Pallas kernels: 4.85 us -> 5.22 us
  waiting for transfers between devices: 11.6 us -> 11.3 us
    pallas_call x6, Pallas kernels: 4.85 us -> 5.22 us  [call(): pl.pallas_call(kernel, out_shape=shapes, in_specs=in_specs or [VMEM] * le...]
where the time goes in v9:
time: 29.1 us; the launch traced here: 29 us
  starting transfers between devices  11.8 us (41%)
  waiting for transfers between devices  11.3 us (39%)
  Pallas kernels  5.22 us (18%)
  between operations  0.67 us (2%)
    ppermute x3, starting transfers between devices, small_body(): pieces = [lax.ppermute(own, 'vocab', flip(4, k)) for k in (1, 2, 3)]  5.76 us
    pallas_call x6, Pallas kernels, call(): pl.pallas_call(kernel, out_shape=shapes, in_specs=in_specs or [VMEM] * le...  5.22 us
    ppermute x3, starting transfers between devices, small_body(): lax.ppermute(a, 'vocab', flip(4, k))  4.42 us
    ppermute x1, waiting for transfers between devices, small_body(): got = lax.ppermute(send, 'rows', flip(2, 1))  3.79 us
    ppermute x3, waiting for transfers between devices, small_body(): pieces = [lax.ppermute(own, 'vocab', flip(4, k)) for k in (1, 2, 3)]  2.69 us
    ppermute x3, waiting for transfers between devices, small_body(): lax.ppermute(a, 'vocab', flip(4, k))  2.17 us
    ppermute x1, starting transfers between devices, small_body(): got = lax.ppermute(send, 'rows', flip(2, 1))  1.55 us
    ppermute x1, waiting for transfers between devices, small_body(): got = lax.ppermute(send, 'teach', flip(2, 1))  1.49 us
  transfers between devices with their start and end apart: 9, of which 7 were waited for; matrix products, arithmetic and copies ran while one was open for 0% of the time, Pallas kernels for 1%

profile of v9, /device:TPU:0, one launch (start us, length us, event | category | flops | bytes accessed | tf_op | source)
XLA Modules:
  0.0 29.0 jit_solution(16339506567207436492)
XLA Ops:
  0.6 0.0 copy-start
  0.6 0.9 %shard_map.67 = (f32[16,128]{1,0:T(8,128)S(1)}, f32[8,608]{1,0:T(8,128)S(1)}, bf16[4,3584]{1,0:T(4,128)(2,1)S(1)}) custom-call(s32[16]{0:T(128)} %mask_in.1, f32[8,608]{1,0:T(8,128)} %own_in.1, bf16[4,3584]{1,0:T(4,128)(2,1)} %h_in.1), custom_call_target="tpu_custom_call" | custom-call | flops 2000000000 | bytes 2097152 | tf_op jit(solution)/shard_map/pallas_call | solution.py:378
  1.6 5.1 %collective-permute-start.2 = (bf16[4,3584]{1,0:T(4,128)(2,1)S(1)}, bf16[4,3584]{1,0:T(4,128)(2,1)S(1)}, u32[]{:S(2)}, u32[]{:S(2)}) collective-permute-start(bf16[4,3584]{1,0:T(4,128)(2,1)S(1)} %get-tuple-element.22.h0), channel_id=1, source_target_pairs={{0,12},{4,8},{8,4},{12,0},{1,13},{5,9},{9,5},{13,1},{2,14},{6,10},... | collective-permute-start | bytes 86024 | tf_op jit(solution)/shard_map/ppermute | solution.py:399
  6.7 0.0 collective-permute-start.1
  6.7 0.6 %collective-permute-start = (bf16[4,3584]{1,0:T(4,128)(2,1)S(1)}, bf16[4,3584]{1,0:T(4,128)(2,1)S(1)}, u32[]{:S(2)}, u32[]{:S(2)}) collective-permute-start(bf16[4,3584]{1,0:T(4,128)(2,1)S(1)} %get-tuple-element.22.h0), channel_id=1, source_target_pairs={{0,4},{4,0},{8,12},{12,8},{1,5},{5,1},{9,13},{13,9},{2,6},{6,2},{1... | collective-permute-start | bytes 86024 | tf_op jit(solution)/shard_map/ppermute | solution.py:399
  7.3 0.0 collective-permute-start.3
  7.3 1.2 %collective-permute-done.3.got = f32[8,608]{1,0:T(8,128)S(1)} collective-permute-done((f32[8,608]{1,0:T(8,128)S(1)}, f32[8,608]{1,0:T(8,128)S(1)}, u32[]{:S(2)}, u32[]{:S(2)}) %collective-permute-start.3) | collective-permute-done | bytes 19488 | tf_op jit(solution)/shard_map/ppermute | solution.py:404
  8.5 0.2 shard_map.68
  8.8 0.0 collective-permute-done.2.h3
  8.8 2.7 %collective-permute-done.1.h2 = bf16[4,3584]{1,0:T(4,128)(2,1)S(1)} collective-permute-done((bf16[4,3584]{1,0:T(4,128)(2,1)S(1)}, bf16[4,3584]{1,0:T(4,128)(2,1)S(1)}, u32[]{:S(2)}, u32[]{:S(2)}) %collective-permute-start.1) | collective-permute-done | bytes 28704 | tf_op jit(solution)/shard_map/ppermute | solution.py:399
  11.5 0.0 collective-permute-done.h1
  11.5 0.0 copy-done
  11.5 1.3 %shard_map.69 = (f32[16,304]{1,0:T(8,128)S(1)}, f32[16,128]{1,0:T(8,128)S(1)}, bf16[16,3584]{1,0:T(8,128)(2,1)S(1)}, f32[16,3584]{1,0:T(8,128)S(1)}, f32[16,3712]{1,0:T(8,128)S(1)}) custom-call(bf16[4,3584]{1,0:T(4,128)(2,1)S(1)} %get-tuple-element.22.h0, bf16[4,3584]{1,0:T(4,128)(2,1)S(1)} %collective-permute-done.h1, ...), custom_call_target="tpu_custom_call" | custom-call | tf_op jit(solution)/shard_map/pallas_call | solution.py:378
  12.8 0.0 collective-permute-start.4
  12.8 1.5 %collective-permute-done.4.got = f32[16,3712]{1,0:T(8,128)S(1)} collective-permute-done((f32[16,3712]{1,0:T(8,128)S(1)}, f32[16,3712]{1,0:T(8,128)S(1)}, u32[]{:S(2)}, u32[]{:S(2)}) %collective-permute-start.4) | collective-permute-done | bytes 237600 | tf_op jit(solution)/shard_map/ppermute | solution.py:414
  14.3 0.2 shard_map.70
  14.6 1.6 %collective-permute-start.5 = (f32[8,3712]{1,0:T(8,128)S(1)}, f32[8,3712]{1,0:T(8,128)S(1)}, u32[]{:S(2)}, u32[]{:S(2)}) collective-permute-start(f32[8,3712]{1,0:T(8,128)S(1)} %get-tuple-element.33), channel_id=1, source_target_pairs={{0,2},{2,0},{1,3},{3,1},{4,6},{6,4},{5,7},{7,5},{8,10},{10,8},{9,1... | collective-permute-start | bytes 356360 | tf_op jit(solution)/shard_map/ppermute | solution.py:418
  16.1 3.8 %collective-permute-done.5.got = f32[8,3712]{1,0:T(8,128)S(1)} collective-permute-done((f32[8,3712]{1,0:T(8,128)S(1)}, f32[8,3712]{1,0:T(8,128)S(1)}, u32[]{:S(2)}, u32[]{:S(2)}) %collective-permute-start.5) | collective-permute-done | bytes 118816 | tf_op jit(solution)/shard_map/ppermute | solution.py:418
  19.9 0.4 %shard_map.71 = (f32[16,128]{1,0:T(8,128)S(1)}, f32[2,3584]{1,0:T(2,128)S(1)}, f32[2,3712]{1,0:T(2,128)S(1)}, f32[2,3712]{1,0:T(2,128)S(1)}, f32[2,3712]{1,0:T(2,128)S(1)}) custom-call(f32[8,3584]{1,0:T(8,128)S(1)} %get-tuple-element.31.part, f32[16,128]{1,0:T(8,128)S(1)} %get-tuple-element.32.stats, f32[8,3712]{1,0:T(8,128)S(1)} %collective-permute-done.5.got), custom_call_target="tpu_custom_call" | custom-call | tf_op jit(solution)/shard_map/pallas_call | solution.py:378
  20.3 1.5 %collective-permute-start.6 = (f32[2,3712]{1,0:T(2,128)S(1)}, f32[2,3712]{1,0:T(2,128)S(1)}, u32[]{:S(2)}, u32[]{:S(2)}) collective-permute-start(f32[2,3712]{1,0:T(2,128)S(1)} %get-tuple-element.36), channel_id=1, source_target_pairs={{0,12},{4,8},{8,4},{12,0},{1,13},{5,9},{9,5},{13,1},{2,14},{6,10},... | collective-permute-start | bytes 89096 | tf_op jit(solution)/shard_map/ppermute | solution.py:424
  21.8 0.6 %collective-permute-start.7 = (f32[2,3712]{1,0:T(2,128)S(1)}, f32[2,3712]{1,0:T(2,128)S(1)}, u32[]{:S(2)}, u32[]{:S(2)}) collective-permute-start(f32[2,3712]{1,0:T(2,128)S(1)} %get-tuple-element.37), channel_id=1, source_target_pairs={{0,8},{4,12},{8,0},{12,4},{1,9},{5,13},{9,1},{13,5},{2,10},{6,14},... | collective-permute-start | bytes 89096 | tf_op jit(solution)/shard_map/ppermute | solution.py:424
  22.5 2.3 %collective-permute-start.8 = (f32[2,3712]{1,0:T(2,128)S(1)}, f32[2,3712]{1,0:T(2,128)S(1)}, u32[]{:S(2)}, u32[]{:S(2)}) collective-permute-start(f32[2,3712]{1,0:T(2,128)S(1)} %get-tuple-element.38), channel_id=1, source_target_pairs={{0,4},{4,0},{8,12},{12,8},{1,5},{5,1},{9,13},{13,9},{2,6},{6,2},{1... | collective-permute-start | bytes 89096 | tf_op jit(solution)/shard_map/ppermute | solution.py:424
  24.8 1.4 %collective-permute-done.6.got3 = f32[2,3712]{1,0:T(2,128)S(1)} collective-permute-done((f32[2,3712]{1,0:T(2,128)S(1)}, f32[2,3712]{1,0:T(2,128)S(1)}, u32[]{:S(2)}, u32[]{:S(2)}) %collective-permute-start.6) | collective-permute-done | bytes 29728 | tf_op jit(solution)/shard_map/ppermute | solution.py:424
  26.2 0.5 %collective-permute-done.7.got2 = f32[2,3712]{1,0:T(2,128)S(1)} collective-permute-done((f32[2,3712]{1,0:T(2,128)S(1)}, f32[2,3712]{1,0:T(2,128)S(1)}, u32[]{:S(2)}, u32[]{:S(2)}) %collective-permute-start.7) | collective-permute-done | bytes 29728 | tf_op jit(solution)/shard_map/ppermute | solution.py:424
  26.7 0.3 collective-permute-done.8.got1
  26.9 2.0 %shard_map.72 = (f32[16]{0:T(128)}, bf16[1,3584]{1,0:T(2,128)(2,1)}, bf16[304,3584]{1,0:T(8,128)(2,1)}) custom-call(f32[2,3584]{1,0:T(2,128)S(1)} %get-tuple-element.34.part, f32[16,128]{1,0:T(8,128)S(1)} %get-tuple-element.35.stats, f32[2,3712]{1,0:T(2,128)S(1)} %collective-permute-done.6.got3, f32[2,3712]{1,0:T(2,128)S(1)} %collective-permute-done.7.got2, ...), custom_call_target="tpu_custom_call" | custom-call | tf_op jit(solution)/shard_map/pallas_call | solution.py:378
Async XLA Ops:
  0.6 10.8 %copy-start = (bf16[304,3584]{1,0:T(8,128)(2,1)S(1)}, bf16[304,3584]{1,0:T(8,128)(2,1)}, u32[]{:S(2)}) copy-start(bf16[304,3584]{1,0:T(8,128)(2,1)} %w.1) | copy-start | bytes 6537220
  1.6 7.2 %collective-permute-start.2 = (bf16[4,3584]{1,0:T(4,128)(2,1)S(1)}, bf16[4,3584]{1,0:T(4,128)(2,1)S(1)}, u32[]{:S(2)}, u32[]{:S(2)}) collective-permute-start(bf16[4,3584]{1,0:T(4,128)(2,1)S(1)} %get-tuple-element.22.h0), channel_id=1, source_target_pairs={{0,12},{4,8},{8,4},{12,0},{1,13},{5,9},{9,5},{13,1},{2,14},{6,10},... | collective-permute-start | bytes 86024 | tf_op jit(solution)/shard_map/ppermute | solution.py:399
  6.7 4.8 %collective-permute-start.1 = (bf16[4,3584]{1,0:T(4,128)(2,1)S(1)}, bf16[4,3584]{1,0:T(4,128)(2,1)S(1)}, u32[]{:S(2)}, u32[]{:S(2)}) collective-permute-start(bf16[4,3584]{1,0:T(4,128)(2,1)S(1)} %get-tuple-element.22.h0), channel_id=1, source_target_pairs={{0,8},{4,12},{8,0},{12,4},{1,9},{5,13},{9,1},{13,5},{2,10},{6,14},... | collective-permute-start | bytes 86024 | tf_op jit(solution)/shard_map/ppermute | solution.py:399
  6.7 4.8 %collective-permute-start = (bf16[4,3584]{1,0:T(4,128)(2,1)S(1)}, bf16[4,3584]{1,0:T(4,128)(2,1)S(1)}, u32[]{:S(2)}, u32[]{:S(2)}) collective-permute-start(bf16[4,3584]{1,0:T(4,128)(2,1)S(1)} %get-tuple-element.22.h0), channel_id=1, source_target_pairs={{0,4},{4,0},{8,12},{12,8},{1,5},{5,1},{9,13},{13,9},{2,6},{6,2},{1... | collective-permute-start | bytes 86024 | tf_op jit(solution)/shard_map/ppermute | solution.py:399
  7.3 1.2 %collective-permute-start.3 = (f32[8,608]{1,0:T(8,128)S(1)}, f32[8,608]{1,0:T(8,128)S(1)}, u32[]{:S(2)}, u32[]{:S(2)}) collective-permute-start(f32[8,608]{1,0:T(8,128)S(1)} %get-tuple-element.24.own), channel_id=1, source_target_pairs={{0,1},{1,0},{2,3},{3,2},{4,5},{5,4},{6,7},{7,6},{8,9},{9,8},{10,11... | collective-permute-start | bytes 58376 | tf_op jit(solution)/shard_map/ppermute | solution.py:404
  12.8 1.5 %collective-permute-start.4 = (f32[16,3712]{1,0:T(8,128)S(1)}, f32[16,3712]{1,0:T(8,128)S(1)}, u32[]{:S(2)}, u32[]{:S(2)}) collective-permute-start(f32[16,3712]{1,0:T(8,128)S(1)} %get-tuple-element.30), channel_id=1, source_target_pairs={{0,1},{1,0},{2,3},{3,2},{4,5},{5,4},{6,7},{7,6},{8,9},{9,8},{10,11... | collective-permute-start | bytes 712712 | tf_op jit(solution)/shard_map/ppermute | solution.py:414
  14.6 5.3 %collective-permute-start.5 = (f32[8,3712]{1,0:T(8,128)S(1)}, f32[8,3712]{1,0:T(8,128)S(1)}, u32[]{:S(2)}, u32[]{:S(2)}) collective-permute-start(f32[8,3712]{1,0:T(8,128)S(1)} %get-tuple-element.33), channel_id=1, source_target_pairs={{0,2},{2,0},{1,3},{3,1},{4,6},{6,4},{5,7},{7,5},{8,10},{10,8},{9,1... | collective-permute-start | bytes 356360 | tf_op jit(solution)/shard_map/ppermute | solution.py:418
  20.3 5.8 %collective-permute-start.6 = (f32[2,3712]{1,0:T(2,128)S(1)}, f32[2,3712]{1,0:T(2,128)S(1)}, u32[]{:S(2)}, u32[]{:S(2)}) collective-permute-start(f32[2,3712]{1,0:T(2,128)S(1)} %get-tuple-element.36), channel_id=1, source_target_pairs={{0,12},{4,8},{8,4},{12,0},{1,13},{5,9},{9,5},{13,1},{2,14},{6,10},... | collective-permute-start | bytes 89096 | tf_op jit(solution)/shard_map/ppermute | solution.py:424
  21.8 4.8 %collective-permute-start.7 = (f32[2,3712]{1,0:T(2,128)S(1)}, f32[2,3712]{1,0:T(2,128)S(1)}, u32[]{:S(2)}, u32[]{:S(2)}) collective-permute-start(f32[2,3712]{1,0:T(2,128)S(1)} %get-tuple-element.37), channel_id=1, source_target_pairs={{0,8},{4,12},{8,0},{12,4},{1,9},{5,13},{9,1},{13,5},{2,10},{6,14},... | collective-permute-start | bytes 89096 | tf_op jit(solution)/shard_map/ppermute | solution.py:424
  22.5 4.5 %collective-permute-start.8 = (f32[2,3712]{1,0:T(2,128)S(1)}, f32[2,3712]{1,0:T(2,128)S(1)}, u32[]{:S(2)}, u32[]{:S(2)}) collective-permute-start(f32[2,3712]{1,0:T(2,128)S(1)} %get-tuple-element.38), channel_id=1, source_target_pairs={{0,4},{4,0},{8,12},{12,8},{1,5},{5,1},{9,13},{13,9},{2,6},{6,2},{1... | collective-permute-start | bytes 89096 | tf_op jit(solution)/shard_map/ppermute | solution.py:424

commit v10 on v7

--- a/solution.py
+++ b/solution.py
@@ -211,7 +211,7 @@
     stats[...] = pack([none, mt, none, jnp.sum(e, axis=1, keepdims=True), none, valid[:, 5:6]])
 
 
-def first_kernel(h0, h1, h2, h3, w, scaled, et_in, teacher, student, stats, hb, keep, send, hf, raw, e):
+def first_kernel(h0, h1, h3, h2, w, scaled, et_in, teacher, student, stats, hb, keep, send, hf, raw, e):
     z, x, c = places()
     for k, h in enumerate((h0, h1, h2, h3)):
         hf[4 * k : 4 * k + 4, :] = h[...].astype(jnp.float32)
@@ -273,7 +273,7 @@
         send[4:8, d + 128 * i : d + 128 * i + 128] = st[8 * i : 8 * i + 4]
 
 
-def third_kernel(part, stats, got, stats_out, keep, send3, send2, send1, gs):
+def third_kernel(part, stats, got, stats_out, keep, send2, send3, send1, gs):
     d = part.shape[1]
     for i in range(2):
         gs[8 * i : 8 * i + 8, :] = got[:, d + 128 * i : d + 128 * i + 128]
@@ -295,7 +295,7 @@
 
 def make_last_kernel(chunk):
     def last_kernel(
-        part, stats, got3, got2, got1, student, scaled, hb,
+        part, stats, got2, got3, got1, student, scaled, hb,
         divergence, hidden_grad, weight_grad, gs, gr, out, div, hid, sems,
     ):
         z, x, c = places()
@@ -381,7 +381,7 @@
         [ANY] * 3,
         cost=pl.CostEstimate(flops=2_000_000_000, transcendentals=0, bytes_accessed=2 << 20),
     )(*(pltpu.with_memory_space_constraint(a, pltpu.HBM) for a in (row_mask, mentor, hidden_rows)))
-    pieces = [lax.ppermute(own, "vocab", flip(4, k)) for k in (1, 2, 3)]
+    pieces = [lax.ppermute(own, "vocab", flip(4, k)) for k in (1, 3, 2)]
     scaled, et, teacher = call(
         teacher_kernel,
         [((ROWS, v), f32), ((ROWS, v), f32), ((ROWS, STATS), f32)],
@@ -406,7 +406,7 @@
         [((ROWS, STATS), f32), ((2, d), f32)] + [((2, d + 8 * STATS), f32)] * 3,
         [pltpu.VMEM((ROWS, STATS), f32)],
     )(keep, stats, got)
-    gots = [lax.ppermute(a, "vocab", flip(4, k)) for k, a in zip((3, 2, 1), sends)]
+    gots = [lax.ppermute(a, "vocab", flip(4, k)) for k, a in zip((2, 3, 1), sends)]
     chunk = 512
     return tuple(
         call(

time: 29.1 us -> 29.2 us (level)
  waiting for transfers between devices: 11.6 us -> 12.7 us
  starting transfers between devices: 11.8 us -> 10.8 us
    ppermute x3, waiting for transfers between devices: 2.35 us -> 3.51 us  [small_body(): lax.ppermute(a, 'vocab', flip(4, k))]
    ppermute x3, starting transfers between devices: 4.45 us -> 3.55 us  [small_body(): lax.ppermute(a, 'vocab', flip(4, k))]
  transfers between devices with their start and end apart: 9 -> 9, of which waited for: 7 -> 6; matrix products, arithmetic and copies ran while one was open for 0% -> 0% of each run, Pallas kernels for 1% -> 1%
where the time goes in v10:
time: 29.2 us; the launch traced here: 29.1 us
  waiting for transfers between devices  12.7 us (43%)
  starting transfers between devices  10.8 us (37%)
  Pallas kernels  4.85 us (17%)
  between operations  0.68 us (2%)
    ppermute x3, starting transfers between devices, small_body(): pieces = [lax.ppermute(own, 'vocab', flip(4, k)) for k in (1, 3, 2)]  5.68 us
    pallas_call x6, Pallas kernels, call(): pl.pallas_call(kernel, out_shape=shapes, in_specs=in_specs or [VMEM] * le...  4.85 us
    ppermute x1, waiting for transfers between devices, small_body(): got = lax.ppermute(send, 'rows', flip(2, 1))  3.87 us
    ppermute x3, starting transfers between devices, small_body(): lax.ppermute(a, 'vocab', flip(4, k))  3.55 us
    ppermute x3, waiting for transfers between devices, small_body(): lax.ppermute(a, 'vocab', flip(4, k))  3.51 us
    ppermute x3, waiting for transfers between devices, small_body(): pieces = [lax.ppermute(own, 'vocab', flip(4, k)) for k in (1, 3, 2)]  2.65 us
    ppermute x1, starting transfers between devices, small_body(): got = lax.ppermute(send, 'rows', flip(2, 1))  1.56 us
    ppermute x1, waiting for transfers between devices, small_body(): got = lax.ppermute(send, 'teach', flip(2, 1))  1.49 us
  transfers between devices with their start and end apart: 9, of which 6 were waited for; matrix products, arithmetic and copies ran while one was open for 0% of the time, Pallas kernels for 1%

profile of v10, /device:TPU:0, one launch (start us, length us, event | category | flops | bytes accessed | tf_op | source)
XLA Modules:
  0.0 29.1 jit_solution(14430366681275735605)
XLA Ops:
  0.6 0.0 copy-start
  0.6 0.9 %shard_map.67 = (f32[16,128]{1,0:T(8,128)S(1)}, f32[8,608]{1,0:T(8,128)S(1)}, bf16[4,3584]{1,0:T(4,128)(2,1)S(1)}) custom-call(s32[16]{0:T(128)} %mask_in.1, f32[8,608]{1,0:T(8,128)} %own_in.1, bf16[4,3584]{1,0:T(4,128)(2,1)} %h_in.1), custom_call_target="tpu_custom_call" | custom-call | flops 2000000000 | bytes 2097152 | tf_op jit(solution)/shard_map/pallas_call | solution.py:363
  1.6 4.1 %collective-permute-start.2 = (bf16[4,3584]{1,0:T(4,128)(2,1)S(1)}, bf16[4,3584]{1,0:T(4,128)(2,1)S(1)}, u32[]{:S(2)}, u32[]{:S(2)}) collective-permute-start(bf16[4,3584]{1,0:T(4,128)(2,1)S(1)} %get-tuple-element.22.h0), channel_id=1, source_target_pairs={{0,8},{4,12},{8,0},{12,4},{1,9},{5,13},{9,1},{13,5},{2,10},{6,14},... | collective-permute-start | bytes 86024 | tf_op jit(solution)/shard_map/ppermute | solution.py:384
  5.7 1.3 %collective-permute-start.1 = (bf16[4,3584]{1,0:T(4,128)(2,1)S(1)}, bf16[4,3584]{1,0:T(4,128)(2,1)S(1)}, u32[]{:S(2)}, u32[]{:S(2)}) collective-permute-start(bf16[4,3584]{1,0:T(4,128)(2,1)S(1)} %get-tuple-element.22.h0), channel_id=1, source_target_pairs={{0,12},{4,8},{8,4},{12,0},{1,13},{5,9},{9,5},{13,1},{2,14},{6,10},... | collective-permute-start | bytes 86024 | tf_op jit(solution)/shard_map/ppermute | solution.py:384
  7.0 0.2 collective-permute-start
  7.3 0.0 collective-permute-start.3
  7.3 1.2 %collective-permute-done.3.got = f32[8,608]{1,0:T(8,128)S(1)} collective-permute-done((f32[8,608]{1,0:T(8,128)S(1)}, f32[8,608]{1,0:T(8,128)S(1)}, u32[]{:S(2)}, u32[]{:S(2)}) %collective-permute-start.3) | collective-permute-done | bytes 19488 | tf_op jit(solution)/shard_map/ppermute | solution.py:389
  8.4 0.2 shard_map.68
  8.7 0.0 collective-permute-done.2.h2
  8.7 2.6 %collective-permute-done.1.h3 = bf16[4,3584]{1,0:T(4,128)(2,1)S(1)} collective-permute-done((bf16[4,3584]{1,0:T(4,128)(2,1)S(1)}, bf16[4,3584]{1,0:T(4,128)(2,1)S(1)}, u32[]{:S(2)}, u32[]{:S(2)}) %collective-permute-start.1) | collective-permute-done | bytes 28704 | tf_op jit(solution)/shard_map/ppermute | solution.py:384
  11.3 0.0 collective-permute-done.h1
  11.4 0.0 copy-done
  11.4 1.3 %shard_map.69 = (f32[16,304]{1,0:T(8,128)S(1)}, f32[16,128]{1,0:T(8,128)S(1)}, bf16[16,3584]{1,0:T(8,128)(2,1)S(1)}, f32[16,3584]{1,0:T(8,128)S(1)}, f32[16,3712]{1,0:T(8,128)S(1)}) custom-call(bf16[4,3584]{1,0:T(4,128)(2,1)S(1)} %get-tuple-element.22.h0, bf16[4,3584]{1,0:T(4,128)(2,1)S(1)} %collective-permute-done.h1, ...), custom_call_target="tpu_custom_call" | custom-call | tf_op jit(solution)/shard_map/pallas_call | solution.py:363
  12.7 0.0 collective-permute-start.4
  12.7 1.5 %collective-permute-done.4.got = f32[16,3712]{1,0:T(8,128)S(1)} collective-permute-done((f32[16,3712]{1,0:T(8,128)S(1)}, f32[16,3712]{1,0:T(8,128)S(1)}, u32[]{:S(2)}, u32[]{:S(2)}) %collective-permute-start.4) | collective-permute-done | bytes 237600 | tf_op jit(solution)/shard_map/ppermute | solution.py:399
  14.2 0.2 shard_map.70
  14.4 1.6 %collective-permute-start.5 = (f32[8,3840]{1,0:T(8,128)S(1)}, f32[8,3840]{1,0:T(8,128)S(1)}, u32[]{:S(2)}, u32[]{:S(2)}) collective-permute-start(f32[8,3840]{1,0:T(8,128)S(1)} %get-tuple-element.33), channel_id=1, source_target_pairs={{0,2},{2,0},{1,3},{3,1},{4,6},{6,4},{5,7},{7,5},{8,10},{10,8},{9,1... | collective-permute-start | bytes 368648 | tf_op jit(solution)/shard_map/ppermute | solution.py:403
  16.0 3.9 %collective-permute-done.5.got = f32[8,3840]{1,0:T(8,128)S(1)} collective-permute-done((f32[8,3840]{1,0:T(8,128)S(1)}, f32[8,3840]{1,0:T(8,128)S(1)}, u32[]{:S(2)}, u32[]{:S(2)}) %collective-permute-start.5) | collective-permute-done | bytes 122912 | tf_op jit(solution)/shard_map/ppermute | solution.py:403
  19.8 0.2 shard_map.71
  20.0 1.3 %collective-permute-start.6 = (f32[2,4608]{1,0:T(2,128)S(1)}, f32[2,4608]{1,0:T(2,128)S(1)}, u32[]{:S(2)}, u32[]{:S(2)}) collective-permute-start(f32[2,4608]{1,0:T(2,128)S(1)} %get-tuple-element.36), channel_id=1, source_target_pairs={{0,8},{4,12},{8,0},{12,4},{1,9},{5,13},{9,1},{13,5},{2,10},{6,14},... | collective-permute-start | bytes 110600 | tf_op jit(solution)/shard_map/ppermute | solution.py:409
  21.3 1.0 %collective-permute-start.7 = (f32[2,4608]{1,0:T(2,128)S(1)}, f32[2,4608]{1,0:T(2,128)S(1)}, u32[]{:S(2)}, u32[]{:S(2)}) collective-permute-start(f32[2,4608]{1,0:T(2,128)S(1)} %get-tuple-element.37), channel_id=1, source_target_pairs={{0,12},{4,8},{8,4},{12,0},{1,13},{5,9},{9,5},{13,1},{2,14},{6,10},... | collective-permute-start | bytes 110600 | tf_op jit(solution)/shard_map/ppermute | solution.py:409
  22.3 1.3 %collective-permute-start.8 = (f32[2,4608]{1,0:T(2,128)S(1)}, f32[2,4608]{1,0:T(2,128)S(1)}, u32[]{:S(2)}, u32[]{:S(2)}) collective-permute-start(f32[2,4608]{1,0:T(2,128)S(1)} %get-tuple-element.38), channel_id=1, source_target_pairs={{0,4},{4,0},{8,12},{12,8},{1,5},{5,1},{9,13},{13,9},{2,6},{6,2},{1... | collective-permute-start | bytes 110600 | tf_op jit(solution)/shard_map/ppermute | solution.py:409
  23.6 1.8 %collective-permute-done.6.got2 = f32[2,4608]{1,0:T(2,128)S(1)} collective-permute-done((f32[2,4608]{1,0:T(2,128)S(1)}, f32[2,4608]{1,0:T(2,128)S(1)}, u32[]{:S(2)}, u32[]{:S(2)}) %collective-permute-start.6) | collective-permute-done | bytes 36896 | tf_op jit(solution)/shard_map/ppermute | solution.py:409
  25.4 1.7 %collective-permute-done.7.got3 = f32[2,4608]{1,0:T(2,128)S(1)} collective-permute-done((f32[2,4608]{1,0:T(2,128)S(1)}, f32[2,4608]{1,0:T(2,128)S(1)}, u32[]{:S(2)}, u32[]{:S(2)}) %collective-permute-start.7) | collective-permute-done | bytes 36896 | tf_op jit(solution)/shard_map/ppermute | solution.py:409
  27.1 0.0 collective-permute-done.8.got1
  27.1 2.0 %shard_map.72 = (f32[16]{0:T(128)}, bf16[1,3584]{1,0:T(2,128)(2,1)}, bf16[304,3584]{1,0:T(8,128)(2,1)}) custom-call(f32[2,3584]{1,0:T(2,128)S(1)} %get-tuple-element.34.part, f32[16,128]{1,0:T(8,128)S(1)} %get-tuple-element.35.stats, f32[2,4608]{1,0:T(2,128)S(1)} %collective-permute-done.6.got2, f32[2,4608]{1,0:T(2,128)S(1)} %collective-permute-done.7.got3, ...), custom_call_target="tpu_custom_call" | custom-call | tf_op jit(solution)/shard_map/pallas_call | solution.py:363
Async XLA Ops:
  0.6 10.7 %copy-start = (bf16[304,3584]{1,0:T(8,128)(2,1)S(1)}, bf16[304,3584]{1,0:T(8,128)(2,1)}, u32[]{:S(2)}) copy-start(bf16[304,3584]{1,0:T(8,128)(2,1)} %w.1) | copy-start | bytes 6537220
  1.6 7.1 %collective-permute-start.2 = (bf16[4,3584]{1,0:T(4,128)(2,1)S(1)}, bf16[4,3584]{1,0:T(4,128)(2,1)S(1)}, u32[]{:S(2)}, u32[]{:S(2)}) collective-permute-start(bf16[4,3584]{1,0:T(4,128)(2,1)S(1)} %get-tuple-element.22.h0), channel_id=1, source_target_pairs={{0,8},{4,12},{8,0},{12,4},{1,9},{5,13},{9,1},{13,5},{2,10},{6,14},... | collective-permute-start | bytes 86024 | tf_op jit(solution)/shard_map/ppermute | solution.py:384
  5.7 5.7 %collective-permute-start.1 = (bf16[4,3584]{1,0:T(4,128)(2,1)S(1)}, bf16[4,3584]{1,0:T(4,128)(2,1)S(1)}, u32[]{:S(2)}, u32[]{:S(2)}) collective-permute-start(bf16[4,3584]{1,0:T(4,128)(2,1)S(1)} %get-tuple-element.22.h0), channel_id=1, source_target_pairs={{0,12},{4,8},{8,4},{12,0},{1,13},{5,9},{9,5},{13,1},{2,14},{6,10},... | collective-permute-start | bytes 86024 | tf_op jit(solution)/shard_map/ppermute | solution.py:384
  7.0 4.3 %collective-permute-start = (bf16[4,3584]{1,0:T(4,128)(2,1)S(1)}, bf16[4,3584]{1,0:T(4,128)(2,1)S(1)}, u32[]{:S(2)}, u32[]{:S(2)}) collective-permute-start(bf16[4,3584]{1,0:T(4,128)(2,1)S(1)} %get-tuple-element.22.h0), channel_id=1, source_target_pairs={{0,4},{4,0},{8,12},{12,8},{1,5},{5,1},{9,13},{13,9},{2,6},{6,2},{1... | collective-permute-start | bytes 86024 | tf_op jit(solution)/shard_map/ppermute | solution.py:384
  7.3 1.2 %collective-permute-start.3 = (f32[8,608]{1,0:T(8,128)S(1)}, f32[8,608]{1,0:T(8,128)S(1)}, u32[]{:S(2)}, u32[]{:S(2)}) collective-permute-start(f32[8,608]{1,0:T(8,128)S(1)} %get-tuple-element.24.own), channel_id=1, source_target_pairs={{0,1},{1,0},{2,3},{3,2},{4,5},{5,4},{6,7},{7,6},{8,9},{9,8},{10,11... | collective-permute-start | bytes 58376 | tf_op jit(solution)/shard_map/ppermute | solution.py:389
  12.7 1.5 %collective-permute-start.4 = (f32[16,3712]{1,0:T(8,128)S(1)}, f32[16,3712]{1,0:T(8,128)S(1)}, u32[]{:S(2)}, u32[]{:S(2)}) collective-permute-start(f32[16,3712]{1,0:T(8,128)S(1)} %get-tuple-element.30), channel_id=1, source_target_pairs={{0,1},{1,0},{2,3},{3,2},{4,5},{5,4},{6,7},{7,6},{8,9},{9,8},{10,11... | collective-permute-start | bytes 712712 | tf_op jit(solution)/shard_map/ppermute | solution.py:399
  14.4 5.4 %collective-permute-start.5 = (f32[8,3840]{1,0:T(8,128)S(1)}, f32[8,3840]{1,0:T(8,128)S(1)}, u32[]{:S(2)}, u32[]{:S(2)}) collective-permute-start(f32[8,3840]{1,0:T(8,128)S(1)} %get-tuple-element.33), channel_id=1, source_target_pairs={{0,2},{2,0},{1,3},{3,1},{4,6},{6,4},{5,7},{7,5},{8,10},{10,8},{9,1... | collective-permute-start | bytes 368648 | tf_op jit(solution)/shard_map/ppermute | solution.py:403
  20.0 5.3 %collective-permute-start.6 = (f32[2,4608]{1,0:T(2,128)S(1)}, f32[2,4608]{1,0:T(2,128)S(1)}, u32[]{:S(2)}, u32[]{:S(2)}) collective-permute-start(f32[2,4608]{1,0:T(2,128)S(1)} %get-tuple-element.36), channel_id=1, source_target_pairs={{0,8},{4,12},{8,0},{12,4},{1,9},{5,13},{9,1},{13,5},{2,10},{6,14},... | collective-permute-start | bytes 110600 | tf_op jit(solution)/shard_map/ppermute | solution.py:409
  21.3 5.8 %collective-permute-start.7 = (f32[2,4608]{1,0:T(2,128)S(1)}, f32[2,4608]{1,0:T(2,128)S(1)}, u32[]{:S(2)}, u32[]{:S(2)}) collective-permute-start(f32[2,4608]{1,0:T(2,128)S(1)} %get-tuple-element.37), channel_id=1, source_target_pairs={{0,12},{4,8},{8,4},{12,0},{1,13},{5,9},{9,5},{13,1},{2,14},{6,10},... | collective-permute-start | bytes 110600 | tf_op jit(solution)/shard_map/ppermute | solution.py:409
  22.3 4.8 %collective-permute-start.8 = (f32[2,4608]{1,0:T(2,128)S(1)}, f32[2,4608]{1,0:T(2,128)S(1)}, u32[]{:S(2)}, u32[]{:S(2)}) collective-permute-start(f32[2,4608]{1,0:T(2,128)S(1)} %get-tuple-element.38), channel_id=1, source_target_pairs={{0,4},{4,0},{8,12},{12,8},{1,5},{5,1},{9,13},{13,9},{2,6},{6,2},{1... | collective-permute-start | bytes 110600 | tf_op jit(solution)/shard_map/ppermute | solution.py:409
